TPU v7x, 32 devices: a whole 2x2x4 slice. The times are simulated.
32 devices in a mesh: dp: 16 (over z, y, core), tensor: 2 (over x).
Axes of the slice: x: 2, y: 2, z: 4, core: 2. Of those that a mesh axis runs over, the one named last changes fastest.
Arguments:
- tokens: bfloat16 [81920, 1024], P(('dp', 'tensor')), may hold values from -6 to 6
- kept: int32 [256], P('dp'), may hold values from 180 to 256
- cotangent: bfloat16 [81920, 1024], P(('dp', 'tensor')), may hold values from -6 to 6
- w_qkv: bfloat16 [3, 1024, 1024], P(None, 'dp', 'tensor'), may hold values from -0.1875 to 0.1875
- w_out: bfloat16 [1024, 1024], P('tensor', 'dp'), may hold values from -0.75 to 0.75
- w_up: bfloat16 [1024, 4096], P('dp', 'tensor'), may hold values from -0.1875 to 0.1875
- w_down: bfloat16 [4096, 1024], P('tensor', 'dp'), may hold values from -0.09375 to 0.09375
- qv_bias: bfloat16 [2, 1024], P(None, ('tensor', 'dp')), may hold values from -3 to 3
- up_bias: bfloat16 [4096], P(('tensor', 'dp')), may hold values from -3 to 3
- ln_gain: float32 [2, 1024], P(None, ('dp', 'tensor')), may hold values from 0.5 to 1.5
- shift: float32 [4, 1024], P(None, ('dp', 'tensor')), may hold values from -3 to 3
Outputs:
- layer_out: bfloat16 [81920, 1024], P(('dp', 'tensor'))
- grad_tokens: float32 [81920, 1024], P(('dp', 'tensor'))
- grad_qkv: float32 [3, 1024, 1024], P(None, 'dp', 'tensor')
- grad_out: float32 [1024, 1024], P('tensor', 'dp')
- grad_up: float32 [1024, 4096], P('dp', 'tensor')
- grad_down: float32 [4096, 1024], P('tensor', 'dp')
- grad_qv_bias: float32 [2, 1024], P(None, ('tensor', 'dp'))
- grad_up_bias: float32 [4096], P(('tensor', 'dp'))
- grad_gain: float32 [2, 1024], P(None, ('dp', 'tensor'))
- grad_shift: float32 [4, 1024], P(None, ('dp', 'tensor'))
Inputs may be any that keep to these rules, and one draw needn't show every extreme that they name: kept patches of each image; an image's first 64 tokens and its first kept patch tokens are valid, the rest of its 320 tokens are padding.
All inputs are finite; a program needn't handle non-finite values.
Results may differ from a plain program's by a relative error of at most 0.02.
Values may be sent and summed in bfloat16 or wider, within the bound.
No kernel may reach another device: no remote copies, remote signals or barrier semaphores. Data moves between devices by JAX's collectives and lax.ppermute only.
A program may use at most 320 MiB of HBM per device.

v0:
```python
import jax
import jax.numpy as jnp
from jax import lax
from jax.sharding import PartitionSpec as P

HEAD_DIM = 64
BUFFER = 64
SEQ = 320


EPSILON = 1e-06
NEGATIVE = -1000000000.0


def times_flip(left, right):
    return lax.dot_general(
        left, right, (((1,), (1,)), ((), ())), preferred_element_type=jnp.float32
    )


def inner_rows(left, right):
    return lax.dot_general(
        left, right, (((0,), (0,)), ((), ())), preferred_element_type=jnp.float32
    )


def norm_parts(values):
    centred = values - jnp.mean(values, axis=-1, keepdims=True)
    inverse = lax.rsqrt(jnp.mean(centred * centred, axis=-1, keepdims=True) + EPSILON)
    return (centred * inverse, inverse)


def norm_back(grad_normed, normed, inverse):
    first = jnp.mean(grad_normed, axis=-1, keepdims=True)
    second = jnp.mean(grad_normed * normed, axis=-1, keepdims=True)
    return inverse * (grad_normed - first - normed * second)


def gelu_tanh(values):
    return jax.nn.gelu(values, approximate=True)


def fetch_params(w_qkv, w_out, w_up, w_down, qv_bias, up_bias):
    part_qkv, part_out, part_up, part_down, part_qv, part_bias = (
        lax.all_gather(w_qkv, "dp", axis=1, tiled=True),
        lax.all_gather(w_out, "dp", axis=1, tiled=True),
        lax.all_gather(w_up, "dp", axis=0, tiled=True),
        lax.all_gather(w_down, "dp", axis=1, tiled=True),
        lax.all_gather(qv_bias, "dp", axis=1, tiled=True),
        lax.all_gather(up_bias, "dp", axis=0, tiled=True),
    )
    return (part_qkv, part_out, part_up, part_down, part_qv, part_bias)


def narrow_mlp(grad_up, grad_down, grad_bias_up):
    return (grad_up, grad_down, grad_bias_up)


def narrow_attn(grad_qkv, grad_out, grad_qv_bias):
    return (grad_qkv, grad_out, grad_qv_bias)


def gather_acts(values):
    return lax.all_gather(values, "tensor", axis=0, tiled=True)


def gather_grads(values):
    return lax.all_gather(values, "tensor", axis=0, tiled=True)


def sum_forward(left, right, rows):

    def term(start, count):
        return jnp.dot(left, right, preferred_element_type=jnp.float32)

    return lax.psum_scatter(
        term(jnp.int32(0), rows * lax.axis_size("tensor")).astype(jnp.bfloat16),
        "tensor",
        scatter_dimension=0,
        tiled=True,
    ).astype(jnp.float32)


def sum_backward(lefts, rights, rows):

    def term(start, count):
        total = None
        for left, right in zip(lefts, rights):
            part = times_flip(left, right)
            total = part if total is None else total + part
        return total

    return lax.psum_scatter(
        term(jnp.int32(0), rows * lax.axis_size("tensor")),
        "tensor",
        scatter_dimension=0,
        tiled=True,
    )


def scores_of(query, key, keep):
    scores = jnp.einsum(
        "bqhe,bkhe->bhqk", query, key, preferred_element_type=jnp.float32
    ) * HEAD_DIM ** (-0.5)
    return jnp.where(keep[:, None, None, :] > 0.5, scores, NEGATIVE)


def attend(block):
    query, key, value, keep = block
    scores = scores_of(query, key, keep)
    highest = jnp.max(scores, axis=-1, keepdims=True)
    expo = jnp.exp(scores - highest)
    denom = jnp.sum(expo, axis=-1, keepdims=True)
    probs = (expo / denom).astype(jnp.bfloat16)
    result = jnp.einsum("bhqk,bkhe->bqhe", probs, value, preferred_element_type=jnp.float32)
    return (result.astype(jnp.bfloat16), (highest + jnp.log(denom))[..., 0])


def attend_back(block):
    query, key, value, keep, logsum, grad_attn = block
    scores = scores_of(query, key, keep)
    probs = jnp.exp(scores - logsum[..., None])
    grad_probs = jnp.einsum("bqhe,bkhe->bhqk", grad_attn, value, preferred_element_type=jnp.float32)
    grad_scores = probs * (grad_probs - jnp.sum(probs * grad_probs, axis=-1, keepdims=True))
    grad_scores = grad_scores.astype(jnp.bfloat16)
    scale = HEAD_DIM ** (-0.5)
    grad_query = (
        jnp.einsum("bhqk,bkhe->bqhe", grad_scores, key, preferred_element_type=jnp.float32) * scale
    )
    grad_key = (
        jnp.einsum("bhqk,bqhe->bkhe", grad_scores, query, preferred_element_type=jnp.float32)
        * scale
    )
    grad_value = jnp.einsum(
        "bhqk,bqhe->bkhe", probs.astype(jnp.bfloat16), grad_attn, preferred_element_type=jnp.float32
    )
    return (
        grad_query.astype(jnp.bfloat16),
        grad_key.astype(jnp.bfloat16),
        grad_value.astype(jnp.bfloat16),
    )


def body(tokens, kept, cotangent, w_qkv, w_out, w_up, w_down, qv_bias, up_bias, ln_gain, shift):
    rows = tokens.shape[0]
    full_qkv, full_out, full_up, full_down, bias_qv, bias_up = fetch_params(
        w_qkv, w_out, w_up, w_down, qv_bias, up_bias
    )
    gain, shifts = (
        lax.all_gather(ln_gain, ("dp", "tensor"), axis=1, tiled=True),
        lax.all_gather(shift, ("dp", "tensor"), axis=1, tiled=True),
    )
    heads = full_qkv.shape[2] // HEAD_DIM
    width = heads * HEAD_DIM
    positions = jnp.arange(SEQ, dtype=jnp.int32)
    images = kept.shape[0]
    keep = (positions[None, :] < BUFFER + kept[:, None]).astype(jnp.float32)
    group = images * SEQ
    offset = lax.axis_index("tensor") * rows
    keep_own = lax.dynamic_slice_in_dim(keep.reshape(group), offset, rows, 0)[:, None]
    pairs = images // 2
    keep_pairs = keep.reshape(pairs, 2, SEQ)
    x_values = tokens.astype(jnp.float32)
    normed1, inverse1 = norm_parts(x_values)
    h1_all = gather_acts((normed1 * gain[0] + shifts[0]).astype(jnp.bfloat16))
    bias_float = bias_qv.astype(jnp.float32)
    bias_rows = jnp.stack([bias_float[0], jnp.zeros_like(bias_float[0]), bias_float[1]])
    projected = jnp.einsum("rd,kdc->krc", h1_all, full_qkv, preferred_element_type=jnp.float32)
    qkv = (projected + bias_rows[:, None, :]).astype(jnp.bfloat16)
    split_shape = (pairs, 2, SEQ, heads, HEAD_DIM)
    query = qkv[0].reshape(split_shape)
    key = qkv[1].reshape(split_shape)
    value = qkv[2].reshape(split_shape)
    attn_blocks, logsum = lax.map(attend, (query, key, value, keep_pairs))
    attn = attn_blocks.reshape(group, width)
    mixed = x_values + sum_forward(attn, full_out, rows) + shifts[2]
    normed2, inverse2 = norm_parts(mixed)
    h2_all = gather_acts((normed2 * gain[1] + shifts[1]).astype(jnp.bfloat16))
    pre = jnp.dot(h2_all, full_up, preferred_element_type=jnp.float32) + bias_up.astype(jnp.float32)
    activated, gelu_pull = jax.vjp(gelu_tanh, pre)
    activated = activated.astype(jnp.bfloat16)
    result = (mixed + sum_forward(activated, full_down, rows) + shifts[3]) * keep_own
    layer_out = result.astype(jnp.bfloat16)
    full_qkv, full_out, full_up, full_down, spare_qv, spare_up = fetch_params(
        w_qkv, w_out, w_up, w_down, qv_bias, up_bias
    )
    grad = cotangent.astype(jnp.float32) * keep_own
    grad_m_all = gather_grads(grad.astype(jnp.bfloat16))
    grad_down = inner_rows(activated, grad_m_all)
    grad_pre = gelu_pull(times_flip(grad_m_all, full_down))[0].astype(jnp.bfloat16)
    grad_bias_up = jnp.sum(grad_pre, axis=0, dtype=jnp.float32)
    grad_up = inner_rows(h2_all, grad_pre)
    grad_up, grad_down, grad_bias_up = narrow_mlp(grad_up, grad_down, grad_bias_up)
    grad_h2 = sum_backward((grad_pre,), (full_up,), rows)
    grad_mixed = grad + norm_back(grad_h2 * gain[1], normed2, inverse2)
    grad_o_all = gather_grads(grad_mixed.astype(jnp.bfloat16))
    grad_out = inner_rows(attn, grad_o_all)
    grad_attn = times_flip(grad_o_all, full_out).astype(jnp.bfloat16).reshape(split_shape)
    grad_query, grad_key, grad_value = lax.map(
        attend_back, (query, key, value, keep_pairs, logsum, grad_attn)
    )
    grad_query = grad_query.reshape(group, width)
    grad_key = grad_key.reshape(group, width)
    grad_value = grad_value.reshape(group, width)
    stacked = jnp.stack([grad_query, grad_key, grad_value])
    grad_qkv = jnp.einsum("rd,krc->kdc", h1_all, stacked, preferred_element_type=jnp.float32)
    grad_qv_bias = jnp.stack(
        [
            jnp.sum(grad_query, axis=0, dtype=jnp.float32),
            jnp.sum(grad_value, axis=0, dtype=jnp.float32),
        ]
    )
    grad_h1 = sum_backward(
        (grad_query, grad_key, grad_value), (full_qkv[0], full_qkv[1], full_qkv[2]), rows
    )
    grad_tokens = grad_mixed + norm_back(grad_h1 * gain[0], normed1, inverse1)
    grad_qkv, grad_out, grad_qv_bias = narrow_attn(grad_qkv, grad_out, grad_qv_bias)
    sent_qkv, sent_out, sent_up, sent_down, sent_qv_bias, sent_bias_up = (
        lax.psum_scatter(
            grad_qkv.astype(jnp.bfloat16), "dp", scatter_dimension=1, tiled=True
        ).astype(jnp.float32),
        lax.psum_scatter(
            grad_out.astype(jnp.bfloat16), "dp", scatter_dimension=1, tiled=True
        ).astype(jnp.float32),
        lax.psum_scatter(
            grad_up.astype(jnp.bfloat16), "dp", scatter_dimension=0, tiled=True
        ).astype(jnp.float32),
        lax.psum_scatter(
            grad_down.astype(jnp.bfloat16), "dp", scatter_dimension=1, tiled=True
        ).astype(jnp.float32),
        lax.psum_scatter(
            grad_qv_bias.astype(jnp.bfloat16), "dp", scatter_dimension=1, tiled=True
        ).astype(jnp.float32),
        lax.psum_scatter(
            grad_bias_up.astype(jnp.bfloat16), "dp", scatter_dimension=0, tiled=True
        ).astype(jnp.float32),
    )
    grad_gain = jnp.stack([jnp.sum(grad_h1 * normed1, axis=0), jnp.sum(grad_h2 * normed2, axis=0)])
    grad_shift = jnp.stack(
        [
            jnp.sum(grad_h1, axis=0),
            jnp.sum(grad_h2, axis=0),
            jnp.sum(grad_mixed, axis=0),
            jnp.sum(grad, axis=0),
        ]
    )
    sent_gain, sent_shift = (
        lax.psum_scatter(grad_gain, ("dp", "tensor"), scatter_dimension=1, tiled=True),
        lax.psum_scatter(grad_shift, ("dp", "tensor"), scatter_dimension=1, tiled=True),
    )
    return (
        layer_out,
        grad_tokens,
        sent_qkv,
        sent_out,
        sent_up,
        sent_down,
        sent_qv_bias,
        sent_bias_up,
        sent_gain,
        sent_shift,
    )


def solution(mesh):
    return jax.shard_map(
        body,
        mesh=mesh,
        in_specs=(
            P(("dp", "tensor"), None),
            P("dp"),
            P(("dp", "tensor"), None),
            P(None, "dp", "tensor"),
            P("tensor", "dp"),
            P("dp", "tensor"),
            P("tensor", "dp"),
            P(None, ("tensor", "dp")),
            P(("tensor", "dp")),
            P(None, ("dp", "tensor")),
            P(None, ("dp", "tensor")),
        ),
        out_specs=(
            P(("dp", "tensor"), None),
            P(("dp", "tensor"), None),
            P(None, "dp", "tensor"),
            P("tensor", "dp"),
            P("dp", "tensor"),
            P("tensor", "dp"),
            P(None, ("tensor", "dp")),
            P(("tensor", "dp")),
            P(None, ("dp", "tensor")),
            P(None, ("dp", "tensor")),
        ),
        check_vma=False,
    )
```

profile of v0, /device:TPU:0, one launch (start us, length us, event | category | flops | bytes accessed | tf_op | source)
XLA Modules:
  0.0 2642.8 jit_solution(9621192983766315646)
XLA Ops:
  8.0 70.4 %all-gather = f32[32,32,2]{1,2,0:T(2,128)S(1)} all-gather(f32[1,32,2]{1,2,0:T(2,128)} %bitcast.235), channel_id=1, replica_groups=mesh['dp'=16,'tensor'=2] {'dp','tensor'}, dimensions={0}, use_global_device_ids=true | all-gather | bytes 8448 | tf_op jit(solution)/shard_map/all_gather | solution.py:150
  78.4 63.9 %all-gather.1 = f32[32,32,4]{1,2,0:T(4,128)S(1)} all-gather(f32[1,32,4]{1,2,0:T(4,128)} %bitcast.234), channel_id=1, replica_groups=mesh['dp'=16,'tensor'=2] {'dp','tensor'}, dimensions={0}, use_global_device_ids=true | all-gather | bytes 16896 | tf_op jit(solution)/shard_map/all_gather | solution.py:151
  154.2 17.3 all-gather.2
  171.8 108.7 %all-gather.13.cloned.1.call-done = bf16[5120,1024]{1,0:T(8,128)(2,1)} async-done(((bf16[2560,1024]{1,0:T(8,128)(2,1)}), bf16[5120,1024]{1,0:T(8,128)(2,1)}) %all-gather.13.cloned.1.call-update) | async-done | bytes 10485776 | tf_op jit(solution)/shard_map/all_gather | solution.py:64
  280.4 19.9 fusion.62
  300.4 5.9 fusion.98
  306.3 13.9 reshape.173
  320.2 12.6 copy.101
  332.8 13.9 reshape.172
  346.7 12.7 copy.100
  359.3 13.9 reshape.171
  373.2 12.8 copy.99
  386.0 5.9 broadcast.130.clone2
  392.0 88.5 %while.26 = (s32[]{:T(128)}, bf16[8,2,320,8,64]{2,1,0,4,3:T(2,128)(2,1)}, f32[8,2,8,320]{3,2,1,0:T(8,128)}, bf16[8,2,320,8,64]{2,4,3,1,0:T(8,128)(2,1)}, f32[8,2...) while((s32[]{:T(128)}, ...), condition=%wide.region_5.6_spmd, body=%wide.region_2.5_spmd.sunk | while | flops 439414400 | bytes 24291436 | solution.py:174
  480.5 14.3 reshape.145
  494.8 11.3 convolution_convert_fusion
  506.8 121.5 %reduce-scatter.17.cloned.1.call-done = bf16[2560,1024]{1,0:T(8,128)(2,1)} async-done(((bf16[5120,1024]{1,0:T(8,128)(2,1)}), bf16[2560,1024]{1,0:T(8,128)(2,1)}) %reduce-scatter.17.cloned.1.call-update) | async-done | bytes 5242896 | tf_op jit(solution)/shard_map/reduce_scatter | solution.py:76
  628.3 6.0 fusion.88
  639.2 4.6 add_convert_fusion.1
  645.5 5.8 fusion.87
  651.4 21.7 all-gather.3
  673.0 7.8 all-gather.21.cloned.1.call-done
  680.9 130.0 %all-gather.19.cloned.1.call-done = bf16[5120,1024]{1,0:T(8,128)(2,1)} async-done(((bf16[2560,1024]{1,0:T(8,128)(2,1)}), bf16[5120,1024]{1,0:T(8,128)(2,1)}) %all-gather.19.cloned.1.call-update) | async-done | bytes 10485776 | tf_op jit(solution)/shard_map/all_gather | solution.py:64
  810.9 42.1 %multiply_convert_fusion.3 = (bf16[5120,2048]{1,0:T(8,128)(2,1)}, f32[5120,2048]{1,0:T(8,128)}) fusion(f32[2048]{0:T(1024)S(1)} %bitcast.232, bf16[5120,1024]{1,0:T(8,128)(2,1)} %all-gather.19.cloned.1.call-done, bf16[1024,2048]{1,0:T(8,128)(2,1)} %all-gather.21.cloned.1.call-done), kind=kOutput, calls=%fused_computation.71 | convolution fusion | flops 21579694080 | bytes 77602816 | tf_op jit(solution)/shard_map/dot_general | solution.py:179
  853.0 10.4 all-gather.23.cloned.1.call-done
  863.5 130.2 %all-gather.25.cloned.1.call-done = bf16[5120,1024]{1,0:T(8,128)(2,1)} async-done(((bf16[2560,1024]{1,0:T(8,128)(2,1)}), bf16[5120,1024]{1,0:T(8,128)(2,1)}) %all-gather.25.cloned.1.call-update) | async-done | bytes 10485776 | tf_op jit(solution)/shard_map/all_gather | solution.py:68
  993.6 56.0 %fusion.102 = (bf16[2048]{0:T(1024)(128)(2,1)}, bf16[5120,2048]{1,0:T(8,128)(2,1)}) fusion(f32[5120,2048]{1,0:T(8,128)} %get-tuple-element.277, f32[2048]{0:T(1024)S(1)} %bitcast.233, bf16[5120,1024]{1,0:T(8,128)(2,1)} %all-gather.25.cloned.1.call-done, bf16[2048,1024]{0,1:T(8,128)(2,1)} %all-gather.23.cloned.1.call-done), kind=kOutput, calls=%fused_computation.151 | convolution fusion | flops 21705521152 | bytes 77606912 | tf_op jit(solution)/shard_map/dot_general | solution.py:16
  1049.7 28.5 %fusion.103 = f32[5120,1024]{1,0:T(8,128)} fusion(bf16[5120,2048]{1,0:T(8,128)(2,1)} %get-tuple-element.279, bf16[1024,2048]{1,0:T(8,128)(2,1)} %all-gather.21.cloned.1.call-done), kind=kOutput, calls=%fused_computation.152 | convolution fusion | flops 21474836480 | bytes 46137344 | tf_op jit(solution)/shard_map/dot_general | solution.py:16
  1078.3 27.9 %convolution_convert_fusion.1 = bf16[5120,1024]{1,0:T(8,128)(2,1)} fusion(bf16[5120,2048]{1,0:T(8,128)(2,1)} %get-tuple-element.276, bf16[2048,1024]{0,1:T(8,128)(2,1)} %all-gather.23.cloned.1.call-done), kind=kOutput, calls=%fused_computation.112 | convolution fusion | flops 21480079360 | bytes 35651584 | tf_op jit(solution)/shard_map/dot_general | solution.py:74
  1106.2 206.4 %reduce-scatter.21.cloned.1.call-done = f32[2560,1024]{1,0:T(8,128)} async-done(((f32[5120,1024]{1,0:T(8,128)}), f32[2560,1024]{1,0:T(8,128)}) %reduce-scatter.21.cloned.1.call-update) | async-done | bytes 10485776 | tf_op jit(solution)/shard_map/reduce_scatter | solution.py:93
  1312.7 10.7 multiply_reduce_fusion.1
  1323.4 114.0 %reduce-scatter.19.cloned.1.call-done = bf16[2560,1024]{1,0:T(8,128)(2,1)} async-done(((bf16[5120,1024]{1,0:T(8,128)(2,1)}), bf16[2560,1024]{1,0:T(8,128)(2,1)}) %reduce-scatter.19.cloned.1.call-update) | async-done | bytes 5242896 | tf_op jit(solution)/shard_map/reduce_scatter | solution.py:76
  1437.4 16.5 fusion.97
  1461.2 29.1 %convolution_convert_fusion.3 = bf16[2048,1024]{0,1:T(8,128)(2,1)} fusion(bf16[5120,2048]{1,0:T(8,128)(2,1)} %get-tuple-element.276, bf16[5120,1024]{1,0:T(8,128)(2,1)} %all-gather.25.cloned.1.call-done), kind=kOutput, calls=%fused_computation.116 | convolution fusion | flops 21476933632 | bytes 35651584 | tf_op jit(solution)/shard_map/dot_general | solution.py:22
  1490.4 29.3 %convolution_convert_fusion.4 = bf16[1024,2048]{1,0:T(8,128)(2,1)} fusion(bf16[5120,1024]{1,0:T(8,128)(2,1)} %all-gather.19.cloned.1.call-done, bf16[5120,2048]{1,0:T(8,128)(2,1)} %get-tuple-element.279), kind=kOutput, calls=%fused_computation.117 | convolution fusion | flops 21476933632 | bytes 35651584 | tf_op jit(solution)/shard_map/dot_general | solution.py:22
  1519.8 71.1 %all-gather.27.cloned.1.call-done = bf16[5120,1024]{1,0:T(8,128)(2,1)} async-done(((bf16[2560,1024]{1,0:T(8,128)(2,1)}), bf16[5120,1024]{1,0:T(8,128)(2,1)}) %all-gather.27.cloned.1.call-update) | async-done | bytes 10485776 | tf_op jit(solution)/shard_map/all_gather | solution.py:68
  1590.8 11.3 convolution_convert_fusion.2
  1602.1 14.0 reshape.162
  1616.1 12.7 copy.106
  1628.8 5.8 broadcast.130.clone
  1634.7 177.6 %while.27 = (s32[]{:T(128)}, bf16[8,2,320,8,64]{2,4,3,1,0:T(8,128)(2,1)}, bf16[8,2,320,8,64]{2,1,0,4,3:T(2,128)(2,1)}, bf16[8,2,320,8,64]{2,4,3,1,0:T(8,128)(2,1...) while((s32[]{:T(128)}, ...), condition=%wide.region_15.16_spmd, body=%wide.region_13.15_spmd.sunk | while | flops 1074785920 | bytes 58479748 | solution.py:199
  1665.3 4.5 multiply_reduce_fusion.7
  1687.6 4.6 multiply_reduce_fusion.7
  1812.3 12.7 copy.110
  1828.9 12.9 copy.108
  1846.6 14.3 stack_reshape.9
  1860.8 14.3 stack_reshape.11
  1875.1 14.3 stack_reshape.10
  1889.5 22.5 convert_bitcast_fusion
  1912.0 5.7 copy.114
  1917.8 14.5 reshape.147
  1932.3 14.3 reshape.149
  1946.6 14.4 reshape.148
  1961.0 10.9 convolution_convert_fusion.5
  1972.1 13.0 fusion.93
  1985.0 12.6 fusion.94
  1997.7 23.9 add_add_fusion
  2024.1 34.6 %all-reduce.1 = bf16[2048]{0:T(1024)(128)(2,1)S(1)} all-reduce(bf16[2048]{0:T(1024)(128)(2,1)S(1)} %copy-done.27), channel_id=11, replica_groups=mesh['dp'=16,'tensor'=2] {'dp'}, use_global_device_ids=true, to_apply=%region_27.28.clone | all-reduce | flops 2048 | bytes 8192
  2066.0 53.7 %reduce-scatter.25.cloned.1.call-done = bf16[512,64]{0,1:T(8,128)(2,1)} async-done(((bf16[512,1024]{0,1:T(8,128)(2,1)}), bf16[512,64]{0,1:T(8,128)(2,1)}) %reduce-scatter.25.cloned.1.call-update) | async-done | bytes 65552 | tf_op jit(solution)/shard_map/reduce_scatter | solution.py:222
  2121.3 233.9 %reduce-scatter.23.cloned.1.call-done = f32[2560,1024]{1,0:T(8,128)} async-done(((f32[5120,1024]{1,0:T(8,128)}), f32[2560,1024]{1,0:T(8,128)}) %reduce-scatter.23.cloned.1.call-update) | async-done | bytes 10485776 | tf_op jit(solution)/shard_map/reduce_scatter | solution.py:93
  2355.2 8.0 fusion.81
  2365.5 14.1 fusion.80
  2379.6 120.8 %reduce-scatter.33.cloned.1.call-done = f32[32,2]{1,0:T(8,128)} async-done(((f32[1024,2]{1,0:T(8,128)}), f32[32,2]{1,0:T(8,128)}) %reduce-scatter.33.cloned.1.call-update) | async-done | bytes 272
  2501.7 132.9 %reduce-scatter.35.cloned.1.call-done = f32[32,4]{1,0:T(8,128)} async-done(((f32[1024,4]{1,0:T(8,128)}), f32[32,4]{1,0:T(8,128)}) %reduce-scatter.35.cloned.1.call-update) | async-done | bytes 528
  (291 shorter events, 307.8 us)
Async XLA Ops:
  7.2 164.6 %all-gather.15.cloned.1.call-start = ((), (), s32[]{:S(2)}) async-start(), calls=%async_computation.11 | async-start | bytes 3342336 | tf_op jit(solution)/shard_map/all_gather | solution.py:45
  7.9 272.5 %all-gather.13.cloned.1.call-start = ((), (), s32[]{:S(2)}) async-start(), calls=%async_computation.10 | async-start | bytes 15728640 | tf_op jit(solution)/shard_map/all_gather | solution.py:64
  142.5 4.2 copy-start
  143.1 5.8 copy-start.17
  146.6 2.2 copy-start.4
  148.2 5.5 copy-start.33
  148.2 6.0 copy-start.30
  148.2 0.6 copy-start.8
  152.8 341.9 %all-gather.17.cloned.1.call-start = ((), (), s32[]{:S(2)}) async-start(), calls=%async_computation.12 | async-start | bytes 1114112 | tf_op jit(solution)/shard_map/all_gather | solution.py:46
  153.6 474.7 %reduce-scatter.17.cloned.1.call-start = ((), (), s32[]{:S(2)}) async-start(), calls=%async_computation.13 | async-start | bytes 15728640 | tf_op jit(solution)/shard_map/reduce_scatter | solution.py:76
  153.7 0.5 copy-start.28
  480.4 25.7 copy-start.14
  506.1 122.1 %copy-start.12 = (f32[1,1024]{1,0:T(1,128)S(1)}, f32[1,1024]{1,0:T(1,128)}, u32[]{:S(2)}) copy-start(f32[1,1024]{1,0:T(1,128)} %get-tuple-element.270) | copy-start | bytes 12292
  506.1 128.1 %slice-start = ((s8[5242880]{0:T(1024)(128)(4,1)}), s8[1048576]{0:T(1024)(128)(4,1)S(1)}, s32[]{:S(2)}) async-start(s8[5242880]{0:T(1024)(128)(4,1)} %bitcast.201), calls=%async_computation.29 | async-start | bytes 2097152
  506.2 174.7 %all-gather.21.cloned.1.call-start = ((), (), s32[]{:S(2)}) async-start(), calls=%async_computation.15 | async-start | bytes 4456448 | tf_op jit(solution)/shard_map/all_gather | solution.py:47
  506.7 304.1 %all-gather.19.cloned.1.call-start = ((), (), s32[]{:S(2)}) async-start(), calls=%async_computation.14 | async-start | bytes 15728640 | tf_op jit(solution)/shard_map/all_gather | solution.py:64
  628.2 6.0 copy-start.1
  628.2 6.8 slice-start.1
  628.3 11.0 copy-start.19
  628.3 11.0 copy-start.23
  635.0 3.6 copy-start.6
  638.6 0.6 copy-start.10
  639.2 5.5 copy-start.29
  643.9 7.5 copy-start.31
  643.9 219.6 %all-gather.23.cloned.1.call-start = ((), (), s32[]{:S(2)}) async-start(), calls=%async_computation.16 | async-start | bytes 4456448 | tf_op jit(solution)/shard_map/all_gather | solution.py:48
  644.6 349.0 %all-gather.25.cloned.1.call-start = ((), (), s32[]{:S(2)}) async-start(), calls=%async_computation.18 | async-start | bytes 15728640 | tf_op jit(solution)/shard_map/all_gather | solution.py:68
  644.9 0.6 copy-start.15
  651.3 661.4 %reduce-scatter.21.cloned.1.call-start = ((), (), s32[]{:S(2)}) async-start(), calls=%async_computation.19 | async-start | bytes 31457280 | tf_op jit(solution)/shard_map/reduce_scatter | solution.py:93
  1078.2 359.2 %reduce-scatter.19.cloned.1.call-start = ((), (), s32[]{:S(2)}) async-start(), calls=%async_computation.17 | async-start | bytes 15728640 | tf_op jit(solution)/shard_map/reduce_scatter | solution.py:76
  1106.1 206.6 %copy-start.7 = (f32[2560]{0:T(1024)S(1)}, f32[2560]{0:T(1024)}, u32[]{:S(2)}) copy-start(f32[2560]{0:T(1024)} %copy-done.6) | copy-start | bytes 30724
  1106.1 206.6 %copy-start.11 = (f32[2560]{0:T(1024)S(1)}, f32[2560]{0:T(1024)}, u32[]{:S(2)}) copy-start(f32[2560]{0:T(1024)} %copy-done.10) | copy-start | bytes 30724
  1106.1 206.6 %copy-start.13 = (f32[1,1024]{1,0:T(1,128)S(1)}, f32[1,1024]{1,0:T(1,128)}, u32[]{:S(2)}) copy-start(f32[1,1024]{1,0:T(1,128)} %get-tuple-element.270) | copy-start | bytes 12292
  1106.1 206.6 %copy-start.20 = (f32[1,1024]{1,0:T(1,128)S(1)}, f32[1,1024]{1,0:T(1,128)}, u32[]{:S(2)}) copy-start(f32[1,1024]{1,0:T(1,128)} %get-tuple-element.273) | copy-start | bytes 12292
  1106.2 331.2 %copy-start.16 = (f32[2560]{0:T(1024)S(1)}, f32[2560]{0:T(1024)}, u32[]{:S(2)}) copy-start(f32[2560]{0:T(1024)} %copy-done.15) | copy-start | bytes 30724
  1106.2 331.2 %copy-start.26 = (f32[1,1024]{1,0:T(1,128)S(1)}, f32[1,1024]{1,0:T(1,128)}, u32[]{:S(2)}) copy-start(f32[1,1024]{1,0:T(1,128)} %get-tuple-element.268) | copy-start | bytes 12292
  1106.2 484.6 %all-gather.27.cloned.1.call-start = ((), (), s32[]{:S(2)}) async-start(), calls=%async_computation.20 | async-start | bytes 15728640 | tf_op jit(solution)/shard_map/all_gather | solution.py:68
  1453.9 4.1 copy-start.2
  1461.2 598.1 %reduce-scatter.29.cloned.1.call-start = ((), (), s32[]{:S(2)}) async-start(), calls=%async_computation.24 | async-start | bytes 4456448 | tf_op jit(solution)/shard_map/reduce_scatter | solution.py:228
  1490.3 570.7 %reduce-scatter.27.cloned.1.call-start = ((), (), s32[]{:S(2)}) async-start(), calls=%async_computation.23 | async-start | bytes 4456448 | tf_op jit(solution)/shard_map/reduce_scatter | solution.py:225
  1490.4 100.4 %copy-start.32 = (bf16[512,1024]{0,1:T(8,128)(2,1)S(1)}, bf16[512,1024]{0,1:T(8,128)(2,1)}, u32[]{:S(2)}) copy-start(bf16[512,1024]{0,1:T(8,128)(2,1)} %all-gather.17.cloned.1.call-done) | copy-start | bytes 3145732
  1519.7 543.1 %reduce-scatter.31.cloned.1.call-start = ((), (), s32[]{:S(2)}) async-start(), calls=%async_computation.25 | async-start | bytes 139264
  1889.5 174.7 %all-reduce.4.cloned.1.call-start = ((), (), s32[]{:S(2)}) async-start(), calls=%async_computation.28 | async-start | bytes 8388608
  1917.8 202.0 %reduce-scatter.25.cloned.1.call-start = ((), (), s32[]{:S(2)}) async-start(), calls=%async_computation.22 | async-start | bytes 1114112 | tf_op jit(solution)/shard_map/reduce_scatter | solution.py:222
  1961.0 11.0 copy-start.3
  1972.0 383.2 %reduce-scatter.23.cloned.1.call-start = ((), (), s32[]{:S(2)}) async-start(), calls=%async_computation.21 | async-start | bytes 31457280 | tf_op jit(solution)/shard_map/reduce_scatter | solution.py:93
  2021.6 0.7 copy-start.34
  2021.6 2.5 copy-start.27
  2021.6 333.7 %copy-start.5 = (f32[2560]{0:T(1024)S(1)}, f32[2560]{0:T(1024)}, u32[]{:S(2)}) copy-start(f32[2560]{0:T(1024)} %copy-done.4) | copy-start | bytes 30724
  2021.6 333.7 %copy-start.9 = (f32[2560]{0:T(1024)S(1)}, f32[2560]{0:T(1024)}, u32[]{:S(2)}) copy-start(f32[2560]{0:T(1024)} %copy-done.8) | copy-start | bytes 30724
  2021.6 333.7 %copy-start.18 = (f32[1,1024]{1,0:T(1,128)S(1)}, f32[1,1024]{1,0:T(1,128)}, u32[]{:S(2)}) copy-start(f32[1,1024]{1,0:T(1,128)} %copy-done.17) | copy-start | bytes 12292
  2021.6 478.8 %reduce-scatter.33.cloned.1.call-start = ((), (), s32[]{:S(2)}) async-start(), calls=%async_computation.26 | async-start | bytes 540672
  2065.2 298.1 %copy-start.21 = (f32[1024]{0:T(1024)S(1)}, f32[1024]{0:T(1024)}, u32[]{:S(2)}) copy-start(f32[1024]{0:T(1024)} %get-tuple-element.215) | copy-start | bytes 12292
  2121.3 243.1 %copy-start.22 = (f32[1024]{0:T(1024)S(1)}, f32[1024]{0:T(1024)}, u32[]{:S(2)}) copy-start(f32[1024]{0:T(1024)} %get-tuple-element.222) | copy-start | bytes 12292
  2121.3 243.1 %copy-start.24 = (f32[1024]{0:T(1024)S(1)}, f32[1024]{0:T(1024)}, u32[]{:S(2)}) copy-start(f32[1024]{0:T(1024)} %get-tuple-element.257) | copy-start | bytes 12292
  2121.3 243.1 %copy-start.25 = (f32[1024]{0:T(1024)S(1)}, f32[1024]{0:T(1024)}, u32[]{:S(2)}) copy-start(f32[1024]{0:T(1024)} %get-tuple-element.267) | copy-start | bytes 12292
  2364.4 270.3 %reduce-scatter.35.cloned.1.call-start = ((), (), s32[]{:S(2)}) async-start(), calls=%async_computation.27 | async-start | bytes 540672
Sparse Core Ops, SparseCore 0:
  10.2 48.2 all-gather.14
  153.0 127.4 all-gather.12
  282.6 37.8 all-gather.16
  506.3 121.9 reduce-scatter.16
  630.3 50.5 all-gather.20
  682.9 127.9 all-gather.18
  813.0 50.3 all-gather.22
  865.6 127.9 all-gather.24
  1078.3 234.2 reduce-scatter.20
  1315.4 121.9 reduce-scatter.18
  1461.3 129.4 all-gather.26
  1594.5 72.7 reduce-scatter.28
  1671.2 71.8 reduce-scatter.26
  1889.6 55.8 reduce-scatter.30
  1949.0 110.3 all-reduce.3
  2062.8 56.9 reduce-scatter.24
  2121.9 233.2 reduce-scatter.22
  2364.5 135.8 reduce-scatter.32
  2502.6 131.9 reduce-scatter.34
where the time goes:
time: 2650 us; the launch traced here: 2640 us
  waiting for transfers between devices  1440 us (54%)
  matrix products  525 us (20%)
  local copies, waits for them, and re-layouts  306 us (12%)
  blocking collectives  208 us (8%)
  other arithmetic  142 us (5%)
    reduce_scatter x2, waiting for transfers between devices, sum_backward(): lax.psum_scatter(term(jnp.int32(0), rows * lax.axis_size('tensor')), 'ten...  440 us
    unnamed x23, waiting for transfers between devices  257 us
    all_gather x2, waiting for transfers between devices, gather_acts(): return lax.all_gather(values, 'tensor', axis=0, tiled=True)  239 us
    reduce_scatter x2, waiting for transfers between devices, sum_forward(): lax.psum_scatter(term(jnp.int32(0), rows * lax.axis_size('tensor')).astyp...  235 us
    all_gather x2, waiting for transfers between devices, gather_grads(): return lax.all_gather(values, 'tensor', axis=0, tiled=True)  201 us
    dot_general x6, matrix products, times_flip(): lax.dot_general(left, right, (((1,), (1,)), ((), ())), preferred_element_...  145 us
    all_gather x1, blocking collectives, body(): lax.all_gather(ln_gain, ('dp', 'tensor'), axis=1, tiled=True)  70.4 us
    dot_general x3, matrix products, inner_rows(): lax.dot_general(left, right, (((0,), (0,)), ((), ())), preferred_element_...  69.3 us
  transfers between devices with their start and end apart: 19, of which 13 were waited for; matrix products, arithmetic and copies ran while one was open for 32% of the time, Pallas kernels for 0%

commit v1 on v0

v1 whole, which is shorter than its diff:
```python
import functools

import jax
import jax.numpy as jnp
from jax import lax
from jax.experimental import pallas as pl
from jax.experimental.pallas import tpu as pltpu
from jax.sharding import PartitionSpec as P

HEAD_DIM = 64
BUFFER = 64
SEQ = 320
KEYS = 384
LANES = 128
EPSILON = 1e-06
SCALE = HEAD_DIM ** (-0.5)
LOG2E = 1.4426950408889634
NEGATIVE = -1000000000.0 / SCALE
VMEM = 56 << 20

f32 = jnp.float32
bf16 = jnp.bfloat16


def dot(left, right):
    return lax.dot_general(left, right, (((1,), (0,)), ((), ())), preferred_element_type=f32)


def dot_flip(left, right):
    return lax.dot_general(left, right, (((1,), (1,)), ((), ())), preferred_element_type=f32)


def split_heads(values):
    low = lax.broadcasted_iota(jnp.int32, (1, LANES), 1) < HEAD_DIM
    zero = jnp.zeros_like(values)
    return jnp.where(low, values, zero), jnp.where(low, zero, values)


def pad_keys(values):
    return jnp.concatenate([values, jnp.zeros((KEYS - SEQ, values.shape[1]), values.dtype)], 0)


def attend_kernel(kept_ref, q_ref, k_ref, v_ref, o_ref, e_ref, r_ref, *, pairs):
    valid = BUFFER + kept_ref[pl.program_id(1)]
    alive = lax.broadcasted_iota(jnp.int32, (1, KEYS), 1) < valid
    ones = split_heads(jnp.ones((KEYS, LANES), bf16))
    for pair in range(pairs):
        cols = slice(LANES * pair, LANES * (pair + 1))
        keys = pad_keys(k_ref[0, :, cols])
        values = split_heads(pad_keys(v_ref[0, :, cols]))
        expos = []
        for head, query in enumerate(split_heads(q_ref[0, :, cols])):
            scores = jnp.where(alive, dot_flip(query, keys), NEGATIVE)
            highest = jnp.max(scores, axis=-1, keepdims=True)
            expo = jnp.exp2((scores - highest) * (SCALE * LOG2E)).astype(bf16)
            e_ref[0, 0, pair, head] = expo
            expos.append(expo)
        right = jnp.concatenate(
            [jnp.concatenate([value, one], 1) for value, one in zip(values, ones)], 0
        )
        both = dot(jnp.concatenate(expos, 1), right)
        inverse = 1.0 / both[:, LANES:]
        o_ref[0, :, cols] = (both[:, :LANES] * inverse).astype(bf16)
        r_ref[0, :, cols] = inverse


def attend(qkv, kept):
    shards, rows, width = qkv.shape
    cols = width // 3
    pairs = cols // LANES
    images = rows // SEQ
    part = lambda which: pl.BlockSpec((1, SEQ, cols), lambda t, i, k: (t, i, which))
    probs = pl.BlockSpec((1, 1, pairs, 2, SEQ, KEYS), lambda t, i, k: (t, i, 0, 0, 0, 0))
    return pl.pallas_call(
        functools.partial(attend_kernel, pairs=pairs),
        grid_spec=pltpu.PrefetchScalarGridSpec(
            num_scalar_prefetch=1,
            grid=(shards, images),
            in_specs=[part(0), part(1), part(2)],
            out_specs=[part(0), probs, part(0)],
        ),
        out_shape=[
            jax.ShapeDtypeStruct((shards, rows, cols), bf16),
            jax.ShapeDtypeStruct((shards, images, pairs, 2, SEQ, KEYS), bf16),
            jax.ShapeDtypeStruct((shards, rows, cols), f32),
        ],
        name="attend",
        compiler_params=pltpu.CompilerParams(
            dimension_semantics=("arbitrary", "arbitrary"), vmem_limit_bytes=VMEM
        ),
    )(kept, qkv, qkv, qkv)


def attend_back_kernel(q_ref, k_ref, v_ref, g_ref, o_ref, e_ref, r_ref, out_ref, bias_ref, *, pairs):
    width = pairs * LANES

    @pl.when(pl.program_id(1) == 0)
    def _():
        bias_ref[...] = jnp.zeros_like(bias_ref)

    for pair in range(pairs):
        cols = slice(LANES * pair, LANES * (pair + 1))
        query = q_ref[0, :, cols]
        values = pad_keys(v_ref[0, :, cols])
        grad = (g_ref[0, :, cols].astype(f32) * r_ref[0, :, cols]).astype(bf16)
        product = split_heads(grad.astype(f32) * o_ref[0, :, cols].astype(f32))
        grads = []
        for head, grad_head in enumerate(split_heads(grad)):
            inner = jnp.sum(product[head], axis=-1, keepdims=True)
            expo = e_ref[0, 0, pair, head].astype(f32)
            grads.append((expo * (dot_flip(grad_head, values) - inner)).astype(bf16))
        keys = jnp.concatenate(split_heads(pad_keys(k_ref[0, :, cols])), 0)
        grad_query = (dot(jnp.concatenate(grads, 1), keys) * SCALE).astype(bf16)
        query_flip, grad_flip = query.T, grad.T
        halves = [slice(HEAD_DIM * head, HEAD_DIM * (head + 1)) for head in range(2)]
        grad_key = jnp.concatenate([dot(query_flip[half], grads[h]) for h, half in enumerate(halves)], 0)
        grad_value = jnp.concatenate(
            [dot(grad_flip[half], e_ref[0, 0, pair, h]) for h, half in enumerate(halves)], 0
        )
        grad_key = (grad_key.T[:SEQ] * SCALE).astype(bf16)
        grad_value = grad_value.T[:SEQ].astype(bf16)
        for which, value in enumerate((grad_query, grad_key, grad_value)):
            start = which * width + LANES * pair
            out_ref[0, :, start : start + LANES] = value
        bias_ref[0, 0:1, cols] += jnp.sum(grad_query.astype(f32), axis=0, keepdims=True)
        bias_ref[0, 1:2, cols] += jnp.sum(grad_value.astype(f32), axis=0, keepdims=True)


def attend_back(qkv, grad, attn, expo, inverse):
    shards, rows, width = qkv.shape
    cols = width // 3
    pairs = cols // LANES
    images = rows // SEQ
    part = lambda which: pl.BlockSpec((1, SEQ, cols), lambda t, i: (t, i, which))
    probs = pl.BlockSpec((1, 1, pairs, 2, SEQ, KEYS), lambda t, i: (t, i, 0, 0, 0, 0))
    return pl.pallas_call(
        functools.partial(attend_back_kernel, pairs=pairs),
        grid=(shards, images),
        in_specs=[part(0), part(1), part(2), part(0), part(0), probs, part(0)],
        out_specs=[
            pl.BlockSpec((1, SEQ, width), lambda t, i: (t, i, 0)),
            pl.BlockSpec((1, 2, cols), lambda t, i: (t, 0, 0)),
        ],
        out_shape=[
            jax.ShapeDtypeStruct((shards, rows, width), bf16),
            jax.ShapeDtypeStruct((shards, 2, cols), f32),
        ],
        name="attend_back",
        compiler_params=pltpu.CompilerParams(
            dimension_semantics=("arbitrary", "arbitrary"), vmem_limit_bytes=VMEM
        ),
    )(qkv, qkv, qkv, grad, attn, expo, inverse)


def norm_parts(values):
    centred = values - jnp.mean(values, axis=-1, keepdims=True)
    inverse = lax.rsqrt(jnp.mean(centred * centred, axis=-1, keepdims=True) + EPSILON)
    return centred * inverse, inverse


def norm_back(grad_normed, normed, inverse):
    first = jnp.mean(grad_normed, axis=-1, keepdims=True)
    second = jnp.mean(grad_normed * normed, axis=-1, keepdims=True)
    return inverse * (grad_normed - first - normed * second)


def gelu_tanh(values):
    return jax.nn.gelu(values, approximate=True)


def columns(left, right):
    return jnp.einsum("rd,tdc->trc", left, right, preferred_element_type=f32)


def contract(left, right):
    return jnp.einsum("trc,tdc->rd", left, right, preferred_element_type=f32)


def weight_grad(left, right):
    return jnp.einsum("rd,trc->tdc", left, right, preferred_element_type=f32).astype(bf16)


def gather(part):
    full = lax.all_gather(part, ("tensor", "dp"), axis=0, tiled=True)
    return full.reshape(lax.axis_size("tensor"), -1, part.shape[1])


def scatter(full):
    flat = full.reshape(-1, full.shape[2])
    return lax.psum_scatter(flat, ("tensor", "dp"), scatter_dimension=0, tiled=True)


def body(tokens, kept, cotangent, w_qkv, w_out, w_up, w_down, qv_bias, up_bias, ln_gain, shift):
    rows, width = tokens.shape
    dp, shards = lax.axis_size("dp"), lax.axis_size("tensor")
    images = rows // SEQ
    part = w_qkv.shape[1]
    cols = w_qkv.shape[2]

    small = jnp.concatenate(
        [ln_gain, shift, qv_bias.astype(f32), up_bias.astype(f32).reshape(-1, ln_gain.shape[1])], 0
    )
    small = lax.all_gather(small, ("dp", "tensor"), axis=0, tiled=False)
    small = small.reshape((dp, shards) + small.shape[1:])
    straight = small[:, :, :6].transpose(2, 0, 1, 3).reshape(6, width)
    gain, shifts = straight[:2], straight[2:]
    bias_qv = small[:, :, 6:8].transpose(1, 2, 0, 3).reshape(shards, 2, cols)
    bias_up = small[:, :, 8:].transpose(1, 0, 2, 3).reshape(shards, -1)

    full_qkv = gather(w_qkv.transpose(1, 0, 2).reshape(part, 3 * cols))
    full_out = gather(w_out.T)
    full_up = gather(w_up)
    full_down = gather(w_down.T)

    first_image = lax.axis_index("tensor") * images
    kept_own = lax.dynamic_slice_in_dim(kept, first_image, images, 0)
    positions = jnp.arange(SEQ, dtype=jnp.int32)
    keep = (positions[None, :] < BUFFER + kept_own[:, None]).astype(f32).reshape(rows, 1)

    x_values = tokens.astype(f32)
    normed1, inverse1 = norm_parts(x_values)
    h1 = (normed1 * gain[0] + shifts[0]).astype(bf16)
    bias_rows = jnp.concatenate([bias_qv[:, 0], jnp.zeros_like(bias_qv[:, 0]), bias_qv[:, 1]], 1)
    qkv = (columns(h1, full_qkv) + bias_rows[:, None, :]).astype(bf16)
    attn, expo, inverse_sum = attend(qkv, kept_own)
    mixed = x_values + contract(attn, full_out) + shifts[2]
    normed2, inverse2 = norm_parts(mixed)
    h2 = (normed2 * gain[1] + shifts[1]).astype(bf16)
    pre = columns(h2, full_up) + bias_up[:, None, :]
    activated, gelu_pull = jax.vjp(gelu_tanh, pre)
    slope = gelu_pull(jnp.ones_like(pre))[0].astype(bf16)
    activated = activated.astype(bf16)

    grad = cotangent.astype(f32) * keep
    grad_m = grad.astype(bf16)
    grad_down = weight_grad(grad_m, activated)
    sent_down = scatter(grad_down)
    grad_pre = (columns(grad_m, full_down) * slope.astype(f32)).astype(bf16)
    grad_bias_up = jnp.sum(grad_pre, axis=1, dtype=f32)
    grad_up = weight_grad(h2, grad_pre)
    sent_up = scatter(grad_up)
    grad_h2 = contract(grad_pre, full_up)
    grad_mixed = grad + norm_back(grad_h2 * gain[1], normed2, inverse2)
    grad_o = grad_mixed.astype(bf16)
    grad_out = weight_grad(grad_o, attn)
    sent_out = scatter(grad_out)
    grad_attn = columns(grad_o, full_out).astype(bf16)
    grad_heads, grad_bias_qv = attend_back(qkv, grad_attn, attn, expo, inverse_sum)
    grad_qkv = weight_grad(h1, grad_heads)
    sent_qkv = scatter(grad_qkv)
    grad_h1 = contract(grad_heads, full_qkv)
    grad_tokens = grad_mixed + norm_back(grad_h1 * gain[0], normed1, inverse1)

    result = (mixed + contract(activated, full_down) + shifts[3]) * keep
    layer_out = result.astype(bf16)

    grad_rows = jnp.stack(
        [
            jnp.sum(grad_h1 * normed1, axis=0),
            jnp.sum(grad_h2 * normed2, axis=0),
            jnp.sum(grad_h1, axis=0),
            jnp.sum(grad_h2, axis=0),
            jnp.sum(grad_mixed, axis=0),
            jnp.sum(grad, axis=0),
        ]
    )
    own = ln_gain.shape[1]
    packed = jnp.concatenate(
        [
            grad_rows.reshape(6, dp, shards, own).transpose(1, 2, 0, 3),
            grad_bias_qv.reshape(shards, 2, dp, own).transpose(2, 0, 1, 3),
            grad_bias_up.reshape(shards, dp, -1, own).transpose(1, 0, 2, 3),
        ],
        2,
    )
    packed = packed.reshape((dp * shards,) + packed.shape[2:])
    sent_small = lax.psum_scatter(packed, ("dp", "tensor"), scatter_dimension=0, tiled=False)

    return (
        layer_out,
        grad_tokens,
        sent_qkv.astype(f32).reshape(part, 3, cols).transpose(1, 0, 2),
        sent_out.astype(f32).T,
        sent_up.astype(f32),
        sent_down.astype(f32).T,
        sent_small[6:8],
        sent_small[8:].reshape(-1),
        sent_small[:2],
        sent_small[2:6],
    )


def solution(mesh):
    both = P(("dp", "tensor"), None)
    matrices = (
        P(None, "dp", "tensor"),
        P("tensor", "dp"),
        P("dp", "tensor"),
        P("tensor", "dp"),
        P(None, ("tensor", "dp")),
        P(("tensor", "dp")),
        P(None, ("dp", "tensor")),
        P(None, ("dp", "tensor")),
    )
    return jax.shard_map(
        body,
        mesh=mesh,
        in_specs=(both, P("dp"), both) + matrices,
        out_specs=(both, both) + matrices,
        check_vma=False,
    )
```

time: 2650 us -> 1230 us (0.46)
  waiting for transfers between devices: 1440 us -> 597 us
  local copies, waits for them, and re-layouts: 306 us -> 76.4 us
  matrix products: 525 us -> 327 us
  blocking collectives: 208 us -> 72.4 us
  other arithmetic: 142 us -> 63.8 us
  Pallas kernels: 0 us -> 74.4 us
    all_gather x8 -> x4, waiting for transfers between devices: 458 us -> 71.5 us  [gather(): full = lax.all_gather(part, ('tensor', 'dp'), axis=0, tiled=True)]
    unnamed x23 -> x9, waiting for transfers between devices: 257 us -> 2 us
    reduce_scatter x7 -> x5, waiting for transfers between devices: 730 us -> 524 us  [the longest x4 524 us: scatter(): lax.psum_scatter(flat, ('tensor', 'dp'), scatter_dimension=0, tiled=True)]
    dot_general x70 -> x12, matrix products: 525 us -> 327 us  [the longest x4 146 us: columns(): return jnp.einsum('rd,tdc->trc', left, right, preferred_element_type=f32)]
    all_gather x4 -> x1, blocking collectives: 173 us -> 72.4 us  [body(): small = lax.all_gather(small, ('dp', 'tensor'), axis=0, tiled=False)]
    another operation x11 -> x7, local copies, waits for them, and re-layouts: 96.6 us -> 0.67 us  [body(): jnp.stack([jnp.sum(grad_h1 * normed1, axis=0), jnp.sum(grad_h2 * normed2,...]
    while x6 -> x0, local copies, waits for them, and re-layouts: 76.3 us -> none  [the longest x3 38.3 us: body(): lax.map(attend_back, (query, key, value, keep_pairs, logsum, grad_attn))]
    pallas_call x0 -> x2, Pallas kernels: none -> 74.4 us  [the longest x1 41.8 us: attend_back(): pl.pallas_call(functools.partial(attend_back_kernel, pairs=pairs), grid=(...]
  transfers between devices with their start and end apart: 19 -> 9, of which waited for: 13 -> 6; matrix products, arithmetic and copies ran while one was open for 32% -> 22% of each run, Pallas kernels for 0% -> 3%
where the time goes in v1:
time: 1230 us
  waiting for transfers between devices  597 us (49%)
  matrix products  327 us (27%)
  local copies, waits for them, and re-layouts  76.4 us (6%)
  Pallas kernels  74.4 us (6%)
  blocking collectives  72.4 us (6%)
  other arithmetic  63.8 us (5%)
  between operations  14.5 us (1%)
    reduce_scatter x4, waiting for transfers between devices, scatter(): lax.psum_scatter(flat, ('tensor', 'dp'), scatter_dimension=0, tiled=True)  524 us
    dot_general x4, matrix products, columns(): return jnp.einsum('rd,tdc->trc', left, right, preferred_element_type=f32)  146 us
    dot_general x4, matrix products, contract(): return jnp.einsum('trc,tdc->rd', left, right, preferred_element_type=f32)  90.6 us
    dot_general x4, matrix products, weight_grad(): jnp.einsum('rd,trc->tdc', left, right, preferred_element_type=f32)  90.1 us
    all_gather x1, blocking collectives, body(): small = lax.all_gather(small, ('dp', 'tensor'), axis=0, tiled=False)  72.4 us
    all_gather x4, waiting for transfers between devices, gather(): full = lax.all_gather(part, ('tensor', 'dp'), axis=0, tiled=True)  71.5 us
    pallas_call x1, Pallas kernels, attend_back(): pl.pallas_call(functools.partial(attend_back_kernel, pairs=pairs), grid=(...  41.8 us
    unnamed x53, local copies, waits for them, and re-layouts  40.2 us
  transfers between devices with their start and end apart: 9, of which 6 were waited for; matrix products, arithmetic and copies ran while one was open for 22% of the time, Pallas kernels for 3%

profile of v1, /device:TPU:0, one launch (start us, length us, event | category | flops | bytes accessed | tf_op | source)
XLA Modules:
  0.0 1225.9 jit_solution(7461622682263961851)
XLA Ops:
  7.2 1.6 copy.96
  8.9 0.7 all-gather.9.cloned.1.call-update
  9.7 0.7 all-gather.11.cloned.1.call-update
  10.4 0.5 all-gather.13.cloned.1.call-update
  11.0 0.7 convert_element_type.91
  11.6 0.7 reshape.189
  12.4 1.2 broadcast_add_fusion
  13.7 0.7 reshape.190
  14.4 0.7 maximum_bitcast_fusion
  15.1 72.4 %all-gather.1 = f32[32,12,32]{2,1,0:T(8,128)S(1)} all-gather(f32[1,12,32]{2,1,0:T(8,128)S(1)} %maximum_bitcast_fusion), channel_id=2, replica_groups=mesh['dp'=16,'tensor'=2] {'dp','tensor'}, dimensions={0}, use_global_device_ids=true | all-gather | bytes 50688 | tf_op jit(solution)/shard_map/all_gather | solution.py:203
  87.6 0.1 add.129
  87.7 0.8 slice_reduce_fusion
  89.0 8.0 copy.61
  97.0 7.9 copy.68
  105.0 3.3 convert_reduce_fusion.1
  108.2 3.9 fusion.24
  112.2 23.9 %fusion.10.q_ref.k_ref.v_ref = bf16[2,2560,1536]{2,1,0:T(8,128)(2,1)} fusion(f32[2,1536]{1,0:T(2,128)S(1)} %pad_maximum_fusion.1, bf16[2,1024,1536]{2,1,0:T(8,128)(2,1)} %bitcast.159, bf16[2560,1024]{0,1:T(8,128)(2,1)} %copy.61, f32[1024]{0:T(1024)S(1)} %add.116, f32[1024]{0:T(1024)S(1)} %mul.156, f32[2560]{0:T(1024)S(1)} %add_rsqrt_fusion.1, ...), kind=kOutput, calls=%fused_computation.20 | convolution fusion | flops 16137584640 | bytes 27303936 | tf_op jit(solution)/shard_map/rd,tdc->trc/dot_general | solution.py:172
  136.2 32.6 %attend.1 = (bf16[2,2560,512]{2,1,0:T(8,128)(2,1)}, bf16[2,8,4,2,320,384]{5,4,3,2,1,0:T(8,128)(2,1)}, f32[2,2560,512]{2,1,0:T(8,128)}) custom-call(s32[8]{0:T(128)} %get-tuple-element.65.kept_ref, bf16[2,2560,1536]{2,1,0:T(8,128)(2,1)} %fusion.10.q_ref.k_ref.v_ref, bf16[2,2560,1536]{2,1,0:T(8,128)(2,1)} %fusion.10.q_ref.k_ref.v_ref, ...), custom_call_target="tpu_custom_call" | custom-call | tf_op jit(solution)/shard_map/attend/pallas_call | solution.py:74
  168.7 10.1 fusion.53
  178.8 3.9 copy-done
  182.7 1.1 multiply_reduce_fusion.2
  183.8 37.5 %all-gather.11.cloned.1.call-done = bf16[2048,2048]{1,0:T(8,128)(2,1)} async-done(((bf16[64,2048]{1,0:T(8,128)(2,1)}), bf16[2048,2048]{1,0:T(8,128)(2,1)}) %all-gather.11.cloned.1.call-update) | async-done | bytes 8388624 | tf_op jit(solution)/shard_map/all_gather | solution.py:184
  221.3 44.5 %fusion.9 = (bf16[2,2560,2048]{2,1,0:T(8,128)(2,1)}, f32[2560,2,2048]{2,0,1:T(8,128)}) fusion(f32[2,2048]{1,0:T(2,128)S(1)} %add.129, bf16[2,1024,2048]{2,1,0:T(8,128)(2,1)} %bitcast.157, f32[2560,1024]{0,1:T(8,128)} %copy-done, f32[1024]{0:T(1024)S(1)} %add.126, f32[1024]{0:T(1024)S(1)} %mul.162, f32[2560]{0:T(1024)S(1)} %add_rsqrt_fusion, ...), kind=kOutput, calls=%fused_computation.14 | convolution fusion | flops 21592801280 | bytes 81833984 | tf_op jit(solution)/shard_map/rd,tdc->trc/dot_general | solution.py:172
  265.8 34.0 %all-gather.13.cloned.1.call-done = bf16[2048,2048]{1,0:T(8,128)(2,1)} async-done(((bf16[64,2048]{1,0:T(8,128)(2,1)}), bf16[2048,2048]{1,0:T(8,128)(2,1)}) %all-gather.13.cloned.1.call-update) | async-done | bytes 8388624 | tf_op jit(solution)/shard_map/all_gather | solution.py:184
  299.8 67.3 %convert_reduce_fusion = (f32[2,2048]{1,0:T(2,128)S(1)}, bf16[2,2560,2048]{2,1,0:T(8,128)(2,1)}) fusion(f32[2560,2,2048]{2,0,1:T(8,128)} %get-tuple-element.76, f32[2,2048]{1,0:T(2,128)S(1)} %add.129, bf16[2,1024,2048]{2,1,0:T(8,128)(2,1)} %bitcast.155, bf16[2560,1024]{0,1:T(8,128)(2,1)} %copy.68, f32[2560]{0:T(1024)S(1)} %copy-done.12), kind=kOutput, calls=%fused_computation.15 | convolution fusion | flops 21734354944 | bytes 76589056 | tf_op jit(solution)/shard_map/rd,tdc->trc/dot_general | solution.py:172
  367.1 0.1 reshape.185
  367.2 29.0 %fusion.55 = (f32[1024]{0:T(1024)S(1)}, f32[2560,1024]{1,0:T(8,128)}) fusion(bf16[2,2560,2048]{2,1,0:T(8,128)(2,1)} %get-tuple-element.78, bf16[2,1024,2048]{2,1,0:T(8,128)(2,1)} %bitcast.158), kind=kOutput, calls=%fused_computation.101 | convolution fusion | flops 21477457920 | bytes 39849984 | tf_op jit(solution)/shard_map/trc,tdc->rd/dot_general | solution.py:176
  396.2 0.1 stack.24
  396.3 11.5 copy.70
  407.8 9.6 multiply_reduce_fusion
  417.4 0.1 stack.22
  417.5 13.7 %fusion.52 = (f32[1024]{0:T(1024)S(1)}, f32[2560,1024]{0,1:T(8,128)}, f32[1024]{0:T(1024)S(1)}) fusion(f32[2560]{0:T(1024)S(1)} %get-tuple-element.83, f32[2560,1024]{0,1:T(8,128)} %copy-done, f32[2560]{0:T(1024)S(1)} %broadcast_multiply_fusion.4, f32[2560]{0:T(1024)S(1)} %get-tuple-element.84, f32[2560,1024]{0,1:T(8,128)} %copy.70, f32[1024]{0:T(1024)S(1)} %mul.162, ...), kind=kLoop, calls=%fused_computation.98 | loop fusion | flops 31455232 | bytes 36763648 | tf_op jit(solution)/shard_map/reduce_sum | solution.py:263
  431.2 0.1 stack.25
  431.3 0.1 stack.26
  431.4 10.5 fusion.37.g_ref
  441.9 41.8 %attend_back.1 = (bf16[2,2560,1536]{2,1,0:T(8,128)(2,1)}, f32[2,2,512]{2,1,0:T(2,128)}) custom-call(bf16[2,2560,1536]{2,1,0:T(8,128)(2,1)} %fusion.10.q_ref.k_ref.v_ref, bf16[2,2560,1536]{2,1,0:T(8,128)(2,1)} %fusion.10.q_ref.k_ref.v_ref, bf16[2,2560,1536]{2,1,0:T(8,128)(2,1)} %fusion.10.q_ref.k_ref.v_ref, bf16[2,2560,512]{2,1,0:T(8,128)(2,1)} %fusion.37.g_ref, ...), custom_call_target="tpu_custom_call" | custom-call | tf_op jit(solution)/shard_map/attend_back/pallas_call | solution.py:136
  483.7 0.8 reshape.184
  484.5 22.6 %fusion.54 = (f32[1024]{0:T(1024)S(1)}, f32[2560,1024]{1,0:T(8,128)}) fusion(bf16[2,2560,1536]{2,1,0:T(8,128)(2,1)} %get-tuple-element.18, bf16[2,1024,1536]{2,1,0:T(8,128)(2,1)} %bitcast.160), kind=kOutput, calls=%fused_computation.100 | convolution fusion | flops 16108747776 | bytes 32509952 | tf_op jit(solution)/shard_map/trc,tdc->rd/dot_general | solution.py:176
  507.1 0.1 stack.23
  507.2 11.5 copy.72
  518.7 9.4 fusion.23
  528.2 0.2 stack.27
  528.4 0.8 pad_maximum_fusion
  529.2 9.9 convert_bitcast_fusion
  539.1 2.6 copy.75
  541.8 22.6 %convolution_convert_fusion.3 = bf16[2,1536,1024]{1,2,0:T(8,128)(2,1)} fusion(bf16[2,2560,1536]{2,1,0:T(8,128)(2,1)} %get-tuple-element.18, bf16[2560,1024]{0,1:T(8,128)(2,1)} %copy.61, f32[1024]{0:T(1024)S(1)} %copy-done.23, f32[1024]{0:T(1024)S(1)} %copy-done.16, f32[2560]{0:T(1024)S(1)} %copy-done.7, f32[2560]{0:T(1024)S(1)} %copy-done.2), kind=kOutput, calls=%fused_computation.56 | convolution fusion | flops 16125001728 | bytes 27291648 | tf_op jit(solution)/shard_map/rd,trc->tdc/dot_general | solution.py:180
  564.5 27.8 %convolution_convert_fusion.1 = bf16[2,2048,1024]{1,2,0:T(8,128)(2,1)} fusion(bf16[2,2560,2048]{2,1,0:T(8,128)(2,1)} %get-tuple-element.75, bf16[2560,1024]{0,1:T(8,128)(2,1)} %copy.68, f32[2560]{0:T(1024)S(1)} %copy-done.12), kind=kOutput, calls=%fused_computation.54 | convolution fusion | flops 21486895104 | bytes 34613248 | tf_op jit(solution)/shard_map/rd,trc->tdc/dot_general | solution.py:180
  592.4 29.8 %convolution_convert_fusion.2 = bf16[2,2048,1024]{1,2,0:T(8,128)(2,1)} fusion(bf16[2,2560,2048]{2,1,0:T(8,128)(2,1)} %get-tuple-element.78, f32[2560,1024]{0,1:T(8,128)} %copy-done, f32[1024]{0:T(1024)S(1)} %copy-done.21, f32[1024]{0:T(1024)S(1)} %copy-done.19, f32[2560]{0:T(1024)S(1)} %copy-done.10, f32[2560]{0:T(1024)S(1)} %copy-done.5), kind=kOutput, calls=%fused_computation.55 | convolution fusion | flops 21492137984 | bytes 39874560 | tf_op jit(solution)/shard_map/rd,trc->tdc/dot_general | solution.py:180
  622.4 29.0 %fusion.28 = bf16[2560,1024]{0,1:T(8,128)(2,1)} fusion(f32[2560,1024]{0,1:T(8,128)} %copy-done, bf16[2,2560,2048]{2,1,0:T(8,128)(2,1)} %get-tuple-element.75, bf16[2,1024,2048]{2,1,0:T(8,128)(2,1)} %bitcast.156, f32[2560]{0:T(1024)S(1)} %copy-done.12, f32[1024]{0:T(1024)S(1)} %add.136), kind=kOutput, calls=%fused_computation.39 | convolution fusion | flops 21485322240 | bytes 45103104 | tf_op jit(solution)/shard_map/trc,tdc->rd/dot_general | solution.py:176
  651.4 8.0 copy.80
  659.4 14.2 %fusion.22 = f32[2560,1024]{0,1:T(8,128)} fusion(f32[2560,1024]{0,1:T(8,128)} %get-tuple-element.63, bf16[2560,1024]{0,1:T(8,128)(2,1)} %copy.61, f32[2560,1024]{0,1:T(8,128)} %copy.72, f32[2560]{0:T(1024)S(1)} %broadcast_multiply_fusion, f32[2560]{0:T(1024)S(1)} %broadcast_multiply_fusion.1, f32[1024]{0:T(1024)S(1)} %copy-done.17, f32[2560]{0:T(1024)S(1)} %copy-done.8, ...), kind=kLoop, calls=%fused_computation.32 | loop fusion | flops 23592960 | bytes 36745216 | tf_op jit(solution)/shard_map/add | solution.py:252
  673.7 11.4 copy.81
  685.1 1.3 slice_bitcast_fusion.5
  686.4 0.6 reshape.187
  686.9 1.3 slice_bitcast_fusion.6
  688.3 111.4 %reduce-scatter.8.cloned.1.call-done = bf16[64,512]{1,0:T(8,128)(2,1)} async-done(((bf16[2048,512]{1,0:T(8,128)(2,1)}), bf16[64,512]{1,0:T(8,128)(2,1)}) %reduce-scatter.8.cloned.1.call-update) | async-done | bytes 65552 | tf_op jit(solution)/shard_map/reduce_scatter | solution.py:190
  799.6 1.5 convert_bitcast_fusion.2
  801.1 115.5 %reduce-scatter.6.cloned.1.call-done = bf16[64,1536]{1,0:T(8,128)(2,1)} async-done(((bf16[2048,1536]{1,0:T(8,128)(2,1)}), bf16[64,1536]{1,0:T(8,128)(2,1)}) %reduce-scatter.6.cloned.1.call-update) | async-done | bytes 196624 | tf_op jit(solution)/shard_map/reduce_scatter | solution.py:190
  916.7 1.3 reshape.191
  917.9 0.9 copy.82
  918.8 149.8 %reduce-scatter.12.cloned.1.call-done = bf16[64,2048]{1,0:T(8,128)(2,1)} async-done(((bf16[2048,2048]{1,0:T(8,128)(2,1)}), bf16[64,2048]{1,0:T(8,128)(2,1)}) %reduce-scatter.12.cloned.1.call-update) | async-done | bytes 262160 | tf_op jit(solution)/shard_map/reduce_scatter | solution.py:190
  1068.6 1.8 convert_bitcast_fusion.1
  1070.4 147.0 %reduce-scatter.10.cloned.1.call-done = bf16[64,2048]{1,0:T(8,128)(2,1)} async-done(((bf16[2048,2048]{1,0:T(8,128)(2,1)}), bf16[64,2048]{1,0:T(8,128)(2,1)}) %reduce-scatter.10.cloned.1.call-update) | async-done | bytes 262160 | tf_op jit(solution)/shard_map/reduce_scatter | solution.py:190
  1217.3 1.8 convert_element_type.114
  (91 shorter events, 1.5 us)
Async XLA Ops:
  7.2 105.0 %all-gather.7.cloned.1.call-start = ((), (), s32[]{:S(2)}) async-start(), calls=%async_computation.5 | async-start | bytes 6488064 | tf_op jit(solution)/shard_map/all_gather | solution.py:184
  8.9 159.9 %all-gather.9.cloned.1.call-start = ((), (), s32[]{:S(2)}) async-start(), calls=%async_computation.6 | async-start | bytes 2162688 | tf_op jit(solution)/shard_map/all_gather | solution.py:184
  9.6 211.7 %all-gather.11.cloned.1.call-start = ((), (), s32[]{:S(2)}) async-start(), calls=%async_computation.7 | async-start | bytes 8650752 | tf_op jit(solution)/shard_map/all_gather | solution.py:184
  10.4 289.5 %all-gather.13.cloned.1.call-start = ((), (), s32[]{:S(2)}) async-start(), calls=%async_computation.8 | async-start | bytes 8650752 | tf_op jit(solution)/shard_map/all_gather | solution.py:184
  10.9 674.2 %reduce-scatter.14.cloned.1.call-start = ((), (), s32[]{:S(2)}) async-start(), calls=%async_computation.13 | async-start | bytes 270336 | tf_op jit(solution)/shard_map/reduce_scatter | solution.py:277
  88.6 328.9 %copy-start.18 = (f32[1024]{0:T(1024)}, f32[1024]{0:T(1024)S(1)}, u32[]{:S(2)}) copy-start(f32[1024]{0:T(1024)S(1)} %mul.162) | copy-start | bytes 12292
  88.7 23.5 %copy-start.15 = (f32[1024]{0:T(1024)}, f32[1024]{0:T(1024)S(1)}, u32[]{:S(2)}) copy-start(f32[1024]{0:T(1024)S(1)} %mul.156) | copy-start | bytes 12292
  88.8 132.6 %copy-start.20 = (f32[1024]{0:T(1024)}, f32[1024]{0:T(1024)S(1)}, u32[]{:S(2)}) copy-start(f32[1024]{0:T(1024)S(1)} %add.126) | copy-start | bytes 12292
  88.9 23.3 %copy-start.22 = (f32[1024]{0:T(1024)}, f32[1024]{0:T(1024)S(1)}, u32[]{:S(2)}) copy-start(f32[1024]{0:T(1024)S(1)} %add.116) | copy-start | bytes 12292
  108.2 27.9 %copy-start.1 = (f32[2560]{0:T(1024)}, f32[2560]{0:T(1024)S(1)}, u32[]{:S(2)}) copy-start(f32[2560]{0:T(1024)S(1)} %broadcast_multiply_fusion.5) | copy-start | bytes 30724
  112.2 24.0 %copy-start.6 = (f32[2560]{0:T(1024)}, f32[2560]{0:T(1024)S(1)}, u32[]{:S(2)}) copy-start(f32[2560]{0:T(1024)S(1)} %add_rsqrt_fusion.1) | copy-start | bytes 30724
  178.8 3.9 copy-start
  178.8 238.7 %copy-start.4 = (f32[2560]{0:T(1024)}, f32[2560]{0:T(1024)S(1)}, u32[]{:S(2)}) copy-start(f32[2560]{0:T(1024)S(1)} %broadcast_multiply_fusion.4) | copy-start | bytes 30724
  183.8 233.7 %copy-start.9 = (f32[2560]{0:T(1024)}, f32[2560]{0:T(1024)S(1)}, u32[]{:S(2)}) copy-start(f32[2560]{0:T(1024)S(1)} %add_rsqrt_fusion) | copy-start | bytes 30724
  221.3 78.5 %copy-start.12 = (f32[2560]{0:T(1024)S(1)}, f32[2560]{0:T(1024)}, u32[]{:S(2)}) copy-start(f32[2560]{0:T(1024)} %reshape.190) | copy-start | bytes 30724
  507.2 11.5 copy-start.2
  507.2 11.5 copy-start.7
  507.2 11.5 copy-start.16
  529.1 12.7 %copy-start.23 = (f32[1024]{0:T(1024)S(1)}, f32[1024]{0:T(1024)}, u32[]{:S(2)}) copy-start(f32[1024]{0:T(1024)} %copy-done.22) | copy-start | bytes 12292
  529.1 270.5 %reduce-scatter.8.cloned.1.call-start = ((), (), s32[]{:S(2)}) async-start(), calls=%async_computation.10 | async-start | bytes 2162688 | tf_op jit(solution)/shard_map/reduce_scatter | solution.py:190
  541.8 374.9 %reduce-scatter.6.cloned.1.call-start = ((), (), s32[]{:S(2)}) async-start(), calls=%async_computation.9 | async-start | bytes 6488064 | tf_op jit(solution)/shard_map/reduce_scatter | solution.py:190
  564.4 504.2 %reduce-scatter.12.cloned.1.call-start = ((), (), s32[]{:S(2)}) async-start(), calls=%async_computation.12 | async-start | bytes 8650752 | tf_op jit(solution)/shard_map/reduce_scatter | solution.py:190
  564.5 27.9 %copy-start.5 = (f32[2560]{0:T(1024)S(1)}, f32[2560]{0:T(1024)}, u32[]{:S(2)}) copy-start(f32[2560]{0:T(1024)} %copy-done.4) | copy-start | bytes 30724
  564.5 27.9 %copy-start.10 = (f32[2560]{0:T(1024)S(1)}, f32[2560]{0:T(1024)}, u32[]{:S(2)}) copy-start(f32[2560]{0:T(1024)} %copy-done.9) | copy-start | bytes 30724
  564.5 27.9 %copy-start.19 = (f32[1024]{0:T(1024)S(1)}, f32[1024]{0:T(1024)}, u32[]{:S(2)}) copy-start(f32[1024]{0:T(1024)} %copy-done.18) | copy-start | bytes 12292
  564.5 27.9 %copy-start.21 = (f32[1024]{0:T(1024)S(1)}, f32[1024]{0:T(1024)}, u32[]{:S(2)}) copy-start(f32[1024]{0:T(1024)} %copy-done.20) | copy-start | bytes 12292
  592.3 29.9 %copy-start.11 = (f32[16,2,32]{2,1,0:T(2,128)S(1)}, f32[16,2,32]{2,1,0:T(2,128)}, u32[]{:S(2)}) copy-start(f32[16,2,32]{2,1,0:T(2,128)} %get-tuple-element.56) | copy-start | bytes 12292
  592.4 625.0 %reduce-scatter.10.cloned.1.call-start = ((), (), s32[]{:S(2)}) async-start(), calls=%async_computation.11 | async-start | bytes 8650752 | tf_op jit(solution)/shard_map/reduce_scatter | solution.py:190
  651.4 8.0 copy-start.14
  651.4 8.0 copy-start.13
  651.4 8.0 copy-start.3
  651.4 8.0 copy-start.8
  651.4 8.0 copy-start.17
Sparse Core Ops, SparseCore 0:
  11.4 73.1 all-gather.6
  87.5 54.9 all-gather.8
  145.4 75.9 all-gather.10
  224.1 75.6 all-gather.12
  529.3 133.9 reduce-scatter.13
  665.4 134.2 reduce-scatter.7
  805.3 111.3 reduce-scatter.5
  919.0 149.5 reduce-scatter.11
  1070.9 146.4 reduce-scatter.9

commit v2 on v1

--- a/solution.py
+++ b/solution.py
@@ -85,6 +85,7 @@
             jax.ShapeDtypeStruct((shards, rows, cols), f32),
         ],
         name="attend",
+        cost_estimate=cost(rows * cols * shards * SEQ * 16, qkv, qkv),
         compiler_params=pltpu.CompilerParams(
             dimension_semantics=("arbitrary", "arbitrary"), vmem_limit_bytes=VMEM
         ),
@@ -146,6 +147,7 @@
             jax.ShapeDtypeStruct((shards, 2, cols), f32),
         ],
         name="attend_back",
+        cost_estimate=cost(rows * cols * shards * SEQ * 24, qkv, qkv, expo),
         compiler_params=pltpu.CompilerParams(
             dimension_semantics=("arbitrary", "arbitrary"), vmem_limit_bytes=VMEM
         ),
@@ -164,20 +166,460 @@
     return inverse * (grad_normed - first - normed * second)
 
 
-def gelu_tanh(values):
-    return jax.nn.gelu(values, approximate=True)
-
-
-def columns(left, right):
-    return jnp.einsum("rd,tdc->trc", left, right, preferred_element_type=f32)
-
-
-def contract(left, right):
-    return jnp.einsum("trc,tdc->rd", left, right, preferred_element_type=f32)
-
-
-def weight_grad(left, right):
-    return jnp.einsum("rd,trc->tdc", left, right, preferred_element_type=f32).astype(bf16)
+def block_rows(rows):
+    return next(size for size in (512, 320, rows) if rows % size == 0)
+
+
+def cost(flops, *arrays):
+    return pl.CostEstimate(
+        flops=flops, transcendentals=0, bytes_accessed=sum(a.size * a.dtype.itemsize for a in arrays)
+    )
+
+
+def call(kernel, name, grid, in_specs, outs, prefetch=0, aliases=None, estimate=None):
+    return pl.pallas_call(
+        kernel,
+        grid_spec=pltpu.PrefetchScalarGridSpec(
+            num_scalar_prefetch=prefetch,
+            grid=grid,
+            in_specs=in_specs,
+            out_specs=[pl.BlockSpec(block, index) for block, index, _, _ in outs],
+        ),
+        out_shape=[jax.ShapeDtypeStruct(shape, kind) for _, _, shape, kind in outs],
+        name=name,
+        input_output_aliases=aliases or {},
+        cost_estimate=estimate,
+        compiler_params=pltpu.CompilerParams(
+            dimension_semantics=("arbitrary",) * len(grid), vmem_limit_bytes=VMEM
+        ),
+    )
+
+
+def fixed(block, *index):
+    return pl.BlockSpec(block, lambda *_: index, pipeline_mode=pl.Buffered(1))
+
+
+GAIN1, GAIN2, SHIFT1, SHIFT2, SHIFT3, SHIFT4 = range(6)
+
+
+def row(ref, index):
+    return ref[index : index + 1, :]
+
+
+def norm_in_kernel(x_ref, vec_ref, h_ref):
+    normed, _ = norm_parts(x_ref[...].astype(f32))
+    h_ref[...] = (normed * row(vec_ref, GAIN1) + row(vec_ref, SHIFT1)).astype(bf16)
+
+
+def norm_in(tokens, vectors):
+    rows, width = tokens.shape
+    step = pl.BlockSpec((SEQ, width), lambda i: (i, 0))
+    return call(
+        norm_in_kernel,
+        "norm_in",
+        (rows // SEQ,),
+        [step, fixed(vectors.shape, 0, 0)],
+        [((SEQ, width), lambda i: (i, 0), (rows, width), bf16)],
+        estimate=cost(16 * rows * width, tokens, tokens),
+    )(tokens, vectors)[0]
+
+
+def project_kernel(h_ref, w_ref, bias_ref, out_ref):
+    for shard in range(out_ref.shape[0]):
+        out_ref[shard] = (dot(h_ref[...], w_ref[shard]) + bias_ref[shard]).astype(bf16)
+
+
+def project(h1, weights, bias):
+    rows, width = h1.shape
+    shards, _, cols = bias.shape
+    size = block_rows(rows)
+    return call(
+        project_kernel,
+        "project",
+        (rows // size,),
+        [
+            pl.BlockSpec((size, width), lambda i: (i, 0)),
+            fixed((shards, width, cols), 0, 0, 0),
+            fixed(bias.shape, 0, 0, 0),
+        ],
+        [((shards, size, cols), lambda i: (0, i, 0), (shards, rows, cols), bf16)],
+        estimate=cost(2 * rows * width * cols * shards, h1, weights),
+    )(h1, weights, bias)[0]
+
+
+def mix_kernel(attn_ref, w_ref, x_ref, vec_ref, mixed_ref, h_ref):
+    total = dot_flip(attn_ref[0], w_ref[0])
+    for shard in range(1, attn_ref.shape[0]):
+        total += dot_flip(attn_ref[shard], w_ref[shard])
+    mixed = x_ref[...].astype(f32) + total + row(vec_ref, SHIFT3)
+    normed, _ = norm_parts(mixed)
+    mixed_ref[...] = mixed
+    h_ref[...] = (normed * row(vec_ref, GAIN2) + row(vec_ref, SHIFT2)).astype(bf16)
+
+
+def mix(attn, weights, tokens, vectors):
+    shards, rows, cols = attn.shape
+    width = tokens.shape[1]
+    size = block_rows(rows)
+    step = lambda i: (i, 0)
+    return call(
+        mix_kernel,
+        "mix",
+        (rows // size,),
+        [
+            pl.BlockSpec((shards, size, cols), lambda i: (0, i, 0)),
+            fixed((shards, width, cols), 0, 0, 3),
+            pl.BlockSpec((size, width), step),
+            fixed(vectors.shape, 0, 0),
+        ],
+        [
+            ((size, width), step, (rows, width), f32),
+            ((size, width), step, (rows, width), bf16),
+        ],
+        estimate=cost(2 * rows * width * cols * shards, attn, tokens),
+    )(attn, weights, tokens, vectors)
+
+
+GELU_IN = 0.7978845608
+GELU_CUBE = 0.044715
+
+
+def gelu_parts(pre):
+    square = pre * pre
+    tanh = jnp.tanh(pre * (GELU_IN + (GELU_IN * GELU_CUBE) * square))
+    half = 0.5 * tanh + 0.5
+    slope = half + (0.5 * pre * (1.0 - tanh * tanh)) * (GELU_IN + (3.0 * GELU_IN * GELU_CUBE) * square)
+    return pre * half, slope
+
+
+CHUNK = 512
+
+
+def expand_kernel(h_ref, w_ref, bias_ref, act_ref, slope_ref):
+    cols = act_ref.shape[2]
+    chunk = min(CHUNK, cols)
+    for start in range(0, cols, chunk):
+        part = slice(start, start + chunk)
+        act, slope = gelu_parts(dot(h_ref[...], w_ref[0, :, part]) + bias_ref[0, :, part])
+        act_ref[0, :, part] = act.astype(bf16)
+        slope_ref[0, :, part] = slope.astype(bf16)
+
+
+def expand(h2, weights, bias):
+    rows, width = h2.shape
+    shards, _, cols = weights.shape
+    size = block_rows(rows)
+    out = ((1, size, cols), lambda t, i: (t, i, 0), (shards, rows, cols), bf16)
+    return call(
+        expand_kernel,
+        "expand",
+        (shards, rows // size),
+        [
+            pl.BlockSpec((size, width), lambda t, i: (i, 0)),
+            pl.BlockSpec((1, width, cols), lambda t, i: (t, 0, 0)),
+            pl.BlockSpec((1, 1, cols), lambda t, i: (t, 0, 0)),
+        ],
+        [out, out],
+        estimate=cost(3 * rows * width * cols * shards, h2, weights),
+    )(h2, weights, bias)
+
+
+def expand_back_kernel(g_ref, w_ref, slope_ref, out_ref, bias_ref):
+    @pl.when(pl.program_id(1) == 0)
+    def _():
+        bias_ref[...] = jnp.zeros_like(bias_ref)
+
+    cols = out_ref.shape[2]
+    chunk = min(CHUNK, cols)
+    for start in range(0, cols, chunk):
+        part = slice(start, start + chunk)
+        grad = (dot(g_ref[...], w_ref[0, :, part]) * slope_ref[0, :, part].astype(f32)).astype(bf16)
+        out_ref[0, :, part] = grad
+        bias_ref[0, :, part] += jnp.sum(grad.astype(f32), axis=0, keepdims=True)
+
+
+def expand_back(grad, weights, slope):
+    rows, width = grad.shape
+    shards, _, cols = weights.shape
+    size = block_rows(rows)
+    step = lambda t, i: (t, i, 0)
+    return call(
+        expand_back_kernel,
+        "expand_back",
+        (shards, rows // size),
+        [
+            pl.BlockSpec((size, width), lambda t, i: (i, 0)),
+            pl.BlockSpec((1, width, cols), lambda t, i: (t, 0, 0)),
+            pl.BlockSpec((1, size, cols), step),
+        ],
+        [
+            ((1, size, cols), step, (shards, rows, cols), bf16),
+            ((1, 1, cols), lambda t, i: (t, 0, 0), (shards, 1, cols), f32),
+        ],
+        estimate=cost(2 * rows * width * cols * shards, slope, slope),
+    )(grad, weights, slope)
+
+
+def dot_rows(left, right):
+    return lax.dot_general(left, right, (((0,), (0,)), ((), ())), preferred_element_type=f32)
+
+
+def weight_grad_kernel(left_ref, right_ref, out_ref, *, chunk, used):
+    which = pl.program_id(1)
+    start = pl.multiple_of(which * chunk, chunk)
+    out_ref[0, :, pl.ds(start, chunk)] = dot_rows(left_ref[...], right_ref[0]).astype(bf16)
+    if out_ref.shape[2] > used:
+
+        @pl.when(which == 0)
+        def _():
+            spare = out_ref.shape[2] - used
+            out_ref[0, :, used:] = jnp.zeros((out_ref.shape[1], spare), bf16)
+
+
+def weight_grad(left, right, spare=0):
+    rows, width = left.shape
+    shards, _, cols = right.shape
+    chunk = min(512, cols)
+    return call(
+        functools.partial(weight_grad_kernel, chunk=chunk, used=cols),
+        "weight_grad",
+        (shards, cols // chunk),
+        [
+            fixed((rows, width), 0, 0),
+            pl.BlockSpec((1, rows, chunk), lambda t, n: (t, 0, n)),
+        ],
+        [
+            (
+                (1, width, cols + spare),
+                lambda t, n: (t, 0, 0),
+                (shards, width, cols + spare),
+                bf16,
+            )
+        ],
+        estimate=cost(2 * rows * width * cols * shards, left, right),
+    )(left, right)[0]
+
+
+def weight_grad_slots_kernel(slot_ref, left_ref, right_ref, out_ref, *, owners, per_chain):
+    which, shard = pl.program_id(0), pl.program_id(1)
+    grad = dot_rows(left_ref[...], right_ref[0]).astype(bf16)
+    part = out_ref.shape[1]
+    base = which // per_chain * out_ref.shape[0] + shard * owners
+    for owner in range(owners):
+        out_ref[slot_ref[base + owner]] = grad[owner * part : (owner + 1) * part]
+
+
+def weight_grad_slots(left, right, slots, chains):
+    rows, width = left.shape
+    shards, _, cols = right.shape
+    count = slots.shape[0] // chains
+    owners = count // shards
+    part = width // owners
+    share = cols // chains
+    chunk = share if share <= 1024 else 512
+    return call(
+        functools.partial(weight_grad_slots_kernel, owners=owners, per_chain=share // chunk),
+        "weight_grad_slots",
+        (cols // chunk, shards),
+        [
+            fixed((rows, width), 0, 0),
+            pl.BlockSpec((1, rows, chunk), lambda n, t, s: (t, 0, n)),
+        ],
+        [((count, part, chunk), lambda n, t, s: (0, 0, n), (count, part, cols), bf16)],
+        prefetch=1,
+        estimate=cost(2 * rows * width * cols * shards, left, right),
+    )(slots, left, right)[0]
+
+
+def middle_back_kernel(
+    g_ref, up_ref, mixed_ref, gm_ref, vec_ref, out_w_ref, gmixed_ref, go_ref, gattn_ref, sums_ref
+):
+    @pl.when(pl.program_id(0) == 0)
+    def _():
+        sums_ref[...] = jnp.zeros_like(sums_ref)
+
+    grad_h = dot_flip(g_ref[0], up_ref[0])
+    for shard in range(1, g_ref.shape[0]):
+        grad_h += dot_flip(g_ref[shard], up_ref[shard])
+    normed, inverse = norm_parts(mixed_ref[...])
+    grad = gm_ref[...].astype(f32)
+    grad_mixed = grad + norm_back(grad_h * row(vec_ref, GAIN2), normed, inverse)
+    gmixed_ref[...] = grad_mixed
+    rounded = grad_mixed.astype(bf16)
+    go_ref[...] = rounded
+    for index, value in enumerate((grad_h * normed, grad_h, grad_mixed, grad)):
+        sums_ref[index : index + 1, :] += jnp.sum(value, axis=0, keepdims=True)
+    for shard in range(gattn_ref.shape[0]):
+        gattn_ref[shard] = dot(rounded, out_w_ref[shard]).astype(bf16)
+
+
+def middle_back(grad_pre, up, mixed, grad_m, vectors, weights):
+    shards, rows, cols = grad_pre.shape
+    width = mixed.shape[1]
+    heads = weights.shape[2] // 4
+    step = lambda i: (i, 0)
+    wide = pl.BlockSpec((SEQ, width), step)
+    return call(
+        middle_back_kernel,
+        "middle_back",
+        (rows // SEQ,),
+        [
+            pl.BlockSpec((shards, SEQ, cols), lambda i: (0, i, 0)),
+            fixed(up.shape, 0, 0, 0),
+            wide,
+            wide,
+            fixed(vectors.shape, 0, 0),
+            fixed((shards, width, heads), 0, 0, 3),
+        ],
+        [
+            ((SEQ, width), step, (rows, width), f32),
+            ((SEQ, width), step, (rows, width), bf16),
+            ((shards, SEQ, heads), lambda i: (0, i, 0), (shards, rows, heads), bf16),
+            ((8, width), lambda i: (0, 0), (8, width), f32),
+        ],
+        estimate=cost(2 * rows * width * (cols + heads) * shards, grad_pre, up, mixed),
+    )(grad_pre, up, mixed, grad_m, vectors, weights)
+
+
+def input_back_kernel(g_ref, w_ref, x_ref, gmixed_ref, vec_ref, before_ref, *refs):
+    out_ref, sums_ref = refs[-2:]
+
+    @pl.when(pl.program_id(0) == 0)
+    def _():
+        sums_ref[...] = before_ref[...]
+
+    grad_h = dot_flip(g_ref[0], w_ref[0])
+    for shard in range(1, g_ref.shape[0]):
+        grad_h += dot_flip(g_ref[shard], w_ref[shard])
+    normed, inverse = norm_parts(x_ref[...].astype(f32))
+    out_ref[...] = gmixed_ref[...] + norm_back(grad_h * row(vec_ref, GAIN1), normed, inverse)
+    for index, value in enumerate((grad_h * normed, grad_h)):
+        sums_ref[index : index + 1, :] += jnp.sum(value, axis=0, keepdims=True)
+
+
+def input_back(first, count, grad_heads, weights, tokens, grad_mixed, vectors, sums, *out):
+    shards, rows, cols = grad_heads.shape
+    width = tokens.shape[1]
+    step = lambda i: (first + i, 0)
+    wide = pl.BlockSpec((SEQ, width), step)
+    return call(
+        input_back_kernel,
+        "input_back",
+        (count,),
+        [
+            pl.BlockSpec((shards, SEQ, cols), lambda i: (0, first + i, 0)),
+            fixed((shards, width, cols), 0, 0, 0),
+            wide,
+            wide,
+            fixed(vectors.shape, 0, 0),
+            fixed(sums.shape, 0, 0),
+        ]
+        + [pl.BlockSpec(memory_space=pl.ANY)] * len(out),
+        [
+            ((SEQ, width), step, (rows, width), f32),
+            ((8, width), lambda i: (0, 0), (8, width), f32),
+        ],
+        aliases={6: 0} if out else None,
+        estimate=cost(2 * count * SEQ * width * cols * shards, weights),
+    )(grad_heads, weights, tokens, grad_mixed, vectors, sums, *out)
+
+
+def shrink_kernel(kept_ref, act_ref, w_ref, mixed_ref, vec_ref, *refs, first):
+    out_ref = refs[-1]
+    total = dot_flip(act_ref[0], w_ref[0])
+    for shard in range(1, act_ref.shape[0]):
+        total += dot_flip(act_ref[shard], w_ref[shard])
+    valid = BUFFER + kept_ref[first + pl.program_id(0)]
+    alive = lax.broadcasted_iota(jnp.int32, (SEQ, 1), 0) < valid
+    result = mixed_ref[...] + total + row(vec_ref, SHIFT4)
+    out_ref[...] = jnp.where(alive, result, 0.0).astype(bf16)
+
+
+def shrink(first, count, kept, act, weights, mixed, vectors, *out):
+    shards, rows, cols = act.shape
+    width = mixed.shape[1]
+    step = lambda i, k: (first + i, 0)
+    return call(
+        functools.partial(shrink_kernel, first=first),
+        "shrink",
+        (count,),
+        [
+            pl.BlockSpec((shards, SEQ, cols), lambda i, k: (0, first + i, 0)),
+            fixed(weights.shape, 0, 0, 0),
+            pl.BlockSpec((SEQ, width), step),
+            fixed(vectors.shape, 0, 0),
+        ]
+        + [pl.BlockSpec(memory_space=pl.ANY)] * len(out),
+        [((SEQ, width), step, (rows, width), bf16)],
+        prefetch=1,
+        aliases={5: 0} if out else None,
+        estimate=cost(2 * count * SEQ * width * cols * shards, weights),
+    )(kept, act, weights, mixed, vectors, *out)[0]
+
+
+def swap(values, axis, bit):
+    places = range(lax.axis_size(axis))
+    return lax.ppermute(values, axis, [(place, place ^ bit) for place in places])
+
+
+def bits_of(axis):
+    return [1 << power for power in range(lax.axis_size(axis).bit_length() - 1)]
+
+
+def flip_gather(part):
+    values = part[None]
+    for axis in ("tensor", "dp"):
+        for bit in bits_of(axis):
+            values = jnp.concatenate([values, swap(values, axis, bit)], 0)
+    here = lax.axis_index("dp") * lax.axis_size("tensor") + lax.axis_index("tensor")
+    places = jnp.arange(values.shape[0], dtype=jnp.int32) ^ here.astype(jnp.int32)
+    values = jnp.take(values, places, axis=0)
+    return values.reshape((lax.axis_size("dp"), lax.axis_size("tensor")) + part.shape)
+
+
+def owner_tables(order):
+    dp, shards = lax.axis_size("dp"), lax.axis_size("tensor")
+    here = {axis: lax.axis_index(axis).astype(jnp.int32) for axis in ("dp", "tensor")}
+    index = jnp.arange(dp * shards, dtype=jnp.int32)
+    apart = {"tensor": (index // dp) ^ here["tensor"], "dp": (index % dp) ^ here["dp"]}
+    slot = jnp.zeros_like(index)
+    place = dict(here)
+    for depth, (axis, bit) in enumerate(order):
+        weight = 1 << (len(order) - 1 - depth)
+        slot += jnp.where((apart[axis] & bit) != 0, weight, 0)
+        place[axis] = place[axis] ^ jnp.where((index & weight) != 0, bit, 0)
+    return slot, place["tensor"] * dp + place["dp"]
+
+
+class Chain:
+    def __init__(self, values, order):
+        self.values, self.order = values, list(order)
+
+    def send(self):
+        axis, bit = self.order.pop(0)
+        half = self.values.shape[0] // 2
+        self.near = self.values[:half]
+        self.far = swap(self.values[half:], axis, bit)
+
+    def settle(self):
+        self.values = self.near + self.far
+
+    def finish(self):
+        self.settle()
+        while self.order:
+            self.send()
+            self.settle()
+        return self.values[0]
+
+
+def meet(values, *chains):
+    values, far = lax.optimization_barrier((values, [chain.far for chain in chains]))
+    for chain, arrived in zip(chains, far):
+        chain.far = arrived
+        chain.settle()
+        if chain.order:
+            chain.send()
+    return values
 
 
 def gather(part):
@@ -196,85 +638,102 @@
     images = rows // SEQ
     part = w_qkv.shape[1]
     cols = w_qkv.shape[2]
-
-    small = jnp.concatenate(
-        [ln_gain, shift, qv_bias.astype(f32), up_bias.astype(f32).reshape(-1, ln_gain.shape[1])], 0
-    )
-    small = lax.all_gather(small, ("dp", "tensor"), axis=0, tiled=False)
-    small = small.reshape((dp, shards) + small.shape[1:])
-    straight = small[:, :, :6].transpose(2, 0, 1, 3).reshape(6, width)
-    gain, shifts = straight[:2], straight[2:]
-    bias_qv = small[:, :, 6:8].transpose(1, 2, 0, 3).reshape(shards, 2, cols)
-    bias_up = small[:, :, 8:].transpose(1, 0, 2, 3).reshape(shards, -1)
-
-    full_qkv = gather(w_qkv.transpose(1, 0, 2).reshape(part, 3 * cols))
-    full_out = gather(w_out.T)
+    own = ln_gain.shape[1]
+    barrier = lax.optimization_barrier
+
+    full_heads = gather(jnp.concatenate([w_qkv.transpose(1, 0, 2).reshape(part, 3 * cols), w_out.T], 1))
     full_up = gather(w_up)
     full_down = gather(w_down.T)
+
+    small = jnp.concatenate(
+        [ln_gain, shift, qv_bias.astype(f32), up_bias.astype(f32).reshape(-1, own)], 0
+    )
+    small = flip_gather(small)
+    vectors = small[:, :, :6].transpose(2, 0, 1, 3).reshape(6, width)
+    vectors = jnp.concatenate([vectors, jnp.zeros((2, width), f32)], 0)
+    bias_qv = small[:, :, 6:8].transpose(1, 2, 0, 3).reshape(shards, 2, cols)
+    bias_up = small[:, :, 8:].transpose(1, 0, 2, 3).reshape(shards, 1, -1)
+    bias_heads = jnp.concatenate([bias_qv[:, :1], jnp.zeros_like(bias_qv[:, :1]), bias_qv[:, 1:]], 2)
 
     first_image = lax.axis_index("tensor") * images
     kept_own = lax.dynamic_slice_in_dim(kept, first_image, images, 0)
     positions = jnp.arange(SEQ, dtype=jnp.int32)
-    keep = (positions[None, :] < BUFFER + kept_own[:, None]).astype(f32).reshape(rows, 1)
-
-    x_values = tokens.astype(f32)
-    normed1, inverse1 = norm_parts(x_values)
-    h1 = (normed1 * gain[0] + shifts[0]).astype(bf16)
-    bias_rows = jnp.concatenate([bias_qv[:, 0], jnp.zeros_like(bias_qv[:, 0]), bias_qv[:, 1]], 1)
-    qkv = (columns(h1, full_qkv) + bias_rows[:, None, :]).astype(bf16)
+    alive = (positions[None, :] < BUFFER + kept_own[:, None]).reshape(rows, 1)
+    grad_m = jnp.where(alive, cotangent, jnp.zeros_like(cotangent))
+
+    core, along_x = [("dp", 1)], [("tensor", bit) for bit in bits_of("tensor")[::-1]]
+    low, high = [("dp", 2)], [("dp", bit) for bit in bits_of("dp")[::-1] if bit > 2]
+    order_x, order_low = core + along_x + low + high, core + low + along_x + high
+    slots_x, owners_x = owner_tables(order_x)
+    slots_both = jnp.concatenate([slots_x, owner_tables(order_low)[0]])
+
+    h1 = norm_in(tokens, vectors)
+    qkv = project(h1, full_heads, bias_heads)
     attn, expo, inverse_sum = attend(qkv, kept_own)
-    mixed = x_values + contract(attn, full_out) + shifts[2]
-    normed2, inverse2 = norm_parts(mixed)
-    h2 = (normed2 * gain[1] + shifts[1]).astype(bf16)
-    pre = columns(h2, full_up) + bias_up[:, None, :]
-    activated, gelu_pull = jax.vjp(gelu_tanh, pre)
-    slope = gelu_pull(jnp.ones_like(pre))[0].astype(bf16)
-    activated = activated.astype(bf16)
-
-    grad = cotangent.astype(f32) * keep
-    grad_m = grad.astype(bf16)
-    grad_down = weight_grad(grad_m, activated)
-    sent_down = scatter(grad_down)
-    grad_pre = (columns(grad_m, full_down) * slope.astype(f32)).astype(bf16)
-    grad_bias_up = jnp.sum(grad_pre, axis=1, dtype=f32)
-    grad_up = weight_grad(h2, grad_pre)
-    sent_up = scatter(grad_up)
-    grad_h2 = contract(grad_pre, full_up)
-    grad_mixed = grad + norm_back(grad_h2 * gain[1], normed2, inverse2)
-    grad_o = grad_mixed.astype(bf16)
-    grad_out = weight_grad(grad_o, attn)
-    sent_out = scatter(grad_out)
-    grad_attn = columns(grad_o, full_out).astype(bf16)
+    mixed, h2 = mix(attn, full_heads, tokens, vectors)
+    act, slope = expand(h2, full_up, bias_up)
+
+    spare = act.shape[2] // 8
+    grad_down = weight_grad(grad_m, act, spare)
+    grad_m, grad_down = barrier((grad_m, grad_down))
+    sent_down = scatter(grad_down)[:, : act.shape[2]]
+    grad_pre, grad_bias_up = expand_back(grad_m, full_down, slope)
+    grad_up = weight_grad(h2, grad_pre, spare)
+    grad_pre, grad_up = barrier((grad_pre, grad_up))
+    sent_up = scatter(grad_up)[:, : act.shape[2]]
+    grad_mixed, grad_o, grad_attn, sums2 = middle_back(
+        grad_pre, full_up, mixed, grad_m, vectors, full_heads
+    )
+
+    grad_out = weight_grad_slots(grad_o, attn, slots_x, 1)
+    grad_attn, grad_out = barrier((grad_attn, grad_out))
+    chain_out = Chain(grad_out, order_x)
+    chain_out.send()
     grad_heads, grad_bias_qv = attend_back(qkv, grad_attn, attn, expo, inverse_sum)
-    grad_qkv = weight_grad(h1, grad_heads)
-    sent_qkv = scatter(grad_qkv)
-    grad_h1 = contract(grad_heads, full_qkv)
-    grad_tokens = grad_mixed + norm_back(grad_h1 * gain[0], normed1, inverse1)
-
-    result = (mixed + contract(activated, full_down) + shifts[3]) * keep
-    layer_out = result.astype(bf16)
-
-    grad_rows = jnp.stack(
-        [
-            jnp.sum(grad_h1 * normed1, axis=0),
-            jnp.sum(grad_h2 * normed2, axis=0),
-            jnp.sum(grad_h1, axis=0),
-            jnp.sum(grad_h2, axis=0),
-            jnp.sum(grad_mixed, axis=0),
-            jnp.sum(grad, axis=0),
-        ]
-    )
-    own = ln_gain.shape[1]
+    grad_heads = meet(grad_heads, chain_out)
+    chains = 2 if (3 * cols // 2) % LANES == 0 else 1
+    grad_qkv = weight_grad_slots(h1, grad_heads, slots_both if chains == 2 else slots_x, chains)
+    grad_qkv = meet(grad_qkv, chain_out)
+    grad_heads, grad_qkv = barrier((grad_heads, grad_qkv))
+    share = 3 * cols // chains
+    chains_qkv = [
+        Chain(grad_qkv[..., share * at : share * (at + 1)], order)
+        for at, order in enumerate((order_x, order_low)[:chains])
+    ]
+    for chain in chains_qkv:
+        chain.send()
+
+    first = images // 2
+    blank = jnp.zeros((8, width), f32)
+    grad_tokens, sums1 = input_back(
+        0, first, grad_heads, full_heads, tokens, grad_mixed, vectors, blank
+    )
+    sums1 = meet(sums1, chain_out, *chains_qkv)
+    grad_tokens, sums1 = input_back(
+        first, images - first, grad_heads, full_heads, tokens, grad_mixed, vectors, sums1, grad_tokens
+    )
+    sums1, act = meet((sums1, act), chain_out, *chains_qkv)
+
+    sums = jnp.stack([sums1[0], sums2[0], sums1[1], sums2[1], sums2[2], sums2[3]])
     packed = jnp.concatenate(
         [
-            grad_rows.reshape(6, dp, shards, own).transpose(1, 2, 0, 3),
-            grad_bias_qv.reshape(shards, 2, dp, own).transpose(2, 0, 1, 3),
-            grad_bias_up.reshape(shards, dp, -1, own).transpose(1, 0, 2, 3),
+            sums.reshape(6, dp, shards, own).transpose(2, 1, 0, 3),
+            grad_bias_qv.reshape(shards, 2, dp, own).transpose(0, 2, 1, 3),
+            grad_bias_up.reshape(shards, dp, -1, own),
         ],
         2,
     )
-    packed = packed.reshape((dp * shards,) + packed.shape[2:])
-    sent_small = lax.psum_scatter(packed, ("dp", "tensor"), scatter_dimension=0, tiled=False)
+    packed = jnp.take(packed.reshape((dp * shards,) + packed.shape[2:]), owners_x, axis=0)
+    packed, act = barrier((packed, act))
+    chain_small = Chain(packed, order_x)
+    chain_small.send()
+    layer_out = shrink(0, first, kept_own, act, full_down, mixed, vectors)
+    layer_out = meet(layer_out, chain_small, *chains_qkv)
+    layer_out = shrink(first, images - first, kept_own, act, full_down, mixed, vectors, layer_out)
+    layer_out = meet(layer_out, chain_small, *chains_qkv)
+    sent_qkv = jnp.concatenate([chain.finish() for chain in chains_qkv], 1)
+    sent_out = chain_out.finish()
+    sent_small = chain_small.finish()
 
     return (
         layer_out,

time: 1230 us -> 582 us (0.47)
  waiting for transfers between devices: 597 us -> 80.7 us
  Pallas kernels: 74.4 us -> 403 us
  matrix products: 327 us -> 0 us
  blocking collectives: 72.4 us -> 0 us
  local copies, waits for them, and re-layouts: 76.4 us -> 20.1 us
  other arithmetic: 63.8 us -> 26.8 us
  starting transfers between devices: 0.36 us -> 26.9 us
    reduce_scatter x4 -> x2, waiting for transfers between devices: 524 us -> 0.01 us  [scatter(): lax.psum_scatter(flat, ('tensor', 'dp'), scatter_dimension=0, tiled=True)]
    pallas_call x0 -> x14, Pallas kernels: none -> 328 us  [the longest x2 60.4 us: weight_grad(): call(functools.partial(weight_grad_kernel, chunk=chunk, used=cols), 'weig...]
    dot_general x12 -> x0, matrix products: 327 us -> none  [the longest x4 146 us: columns(): return jnp.einsum('rd,tdc->trc', left, right, preferred_element_type=f32)]
    all_gather x1 -> x0, blocking collectives: 72.4 us -> none  [body(): small = lax.all_gather(small, ('dp', 'tensor'), axis=0, tiled=False)]
    reduce_sum x6 -> x0, other arithmetic: 41 us -> none  [the longest x1 13.7 us: body(): jnp.sum(grad_mixed, axis=0)]
    unnamed x53 -> x24, local copies, waits for them, and re-layouts: 40.2 us -> 2.97 us
    ppermute x0 -> x25, waiting for transfers between devices: none -> 31.5 us  [swap(): lax.ppermute(values, axis, [(place, place ^ bit) for place in places])]
    ppermute x0 -> x25, starting transfers between devices: none -> 26.7 us  [swap(): lax.ppermute(values, axis, [(place, place ^ bit) for place in places])]
  transfers between devices with their start and end apart: 9 -> 30, of which waited for: 6 -> 13; matrix products, arithmetic and copies ran while one was open for 22% -> 7% of each run, Pallas kernels for 3% -> 70%
where the time goes in v2:
time: 582 us; the launch traced here: 573 us
  Pallas kernels  403 us (69%)
  waiting for transfers between devices  80.7 us (14%)
  starting transfers between devices  26.9 us (5%)
  other arithmetic  26.8 us (5%)
  local copies, waits for them, and re-layouts  20.1 us (3%)
  between operations  14.8 us (3%)
    pallas_call x2, Pallas kernels, weight_grad(): call(functools.partial(weight_grad_kernel, chunk=chunk, used=cols), 'weig...  60.4 us
    pallas_call x1, Pallas kernels, expand(): call(expand_kernel, 'expand', (shards, rows // size), [pl.BlockSpec((size...  48.2 us
    all_gather x3, waiting for transfers between devices, gather(): full = lax.all_gather(part, ('tensor', 'dp'), axis=0, tiled=True)  47.7 us
    pallas_call x1, Pallas kernels, attend_back(): pl.pallas_call(functools.partial(attend_back_kernel, pairs=pairs), grid=(...  42.3 us
    pallas_call x1, Pallas kernels, middle_back(): call(middle_back_kernel, 'middle_back', (rows // SEQ,), [pl.BlockSpec((sh...  39.9 us
    pallas_call x2, Pallas kernels, shrink(): call(functools.partial(shrink_kernel, first=first), 'shrink', (count,), [...  35.8 us
    pallas_call x2, Pallas kernels, weight_grad_slots(): call(functools.partial(weight_grad_slots_kernel, owners=owners, per_chain...  34.9 us
    pallas_call x1, Pallas kernels, expand_back(): call(expand_back_kernel, 'expand_back', (shards, rows // size), [pl.Block...  33.3 us
  transfers between devices with their start and end apart: 30, of which 13 were waited for; matrix products, arithmetic and copies ran while one was open for 7% of the time, Pallas kernels for 70%

profile of v2, /device:TPU:0, one launch (start us, length us, event | category | flops | bytes accessed | tf_op | source)
XLA Modules:
  0.0 572.6 jit_solution(17653245645476119190)
XLA Ops:
  7.2 0.9 copy.48
  8.2 1.6 pad_maximum_fusion
  11.9 0.7 reshape.120
  13.4 3.0 collective-permute-start
  16.4 1.2 broadcast_add_fusion
  18.5 6.4 %broadcast_select_fusion.left_ref.g_ref.gm_ref = bf16[2560,1024]{1,0:T(8,128)(2,1)} fusion(bf16[2560,1024]{1,0:T(8,128)(2,1)} %param.15, pred[2560]{0:T(1024)(128)(4,1)S(1)} %lt.41), kind=kLoop, calls=%fused_computation.2 | loop fusion | flops 2621440 | bytes 10488320 | tf_op jit(solution)/shard_map/jit(_where)/select_n | solution.py:662
  25.0 1.2 collective-permute-done.1
  26.2 1.5 collective-permute-start.2
  27.7 2.4 collective-permute-done.2
  30.1 1.6 collective-permute-start.3
  31.8 3.5 collective-permute-done.3
  35.3 2.1 collective-permute-start.4
  37.4 5.3 collective-permute-done.4
  45.0 8.6 %norm_in.1.h_ref.left_ref = bf16[2560,1024]{1,0:T(8,128)(2,1)} custom-call(bf16[2560,1024]{1,0:T(8,128)(2,1)} %x_ref.7, f32[8,1024]{1,0:T(8,128)} %concatenate.53.vec_ref), custom_call_target="tpu_custom_call" | custom-call | flops 41943040 | bytes 10485760 | tf_op jit(solution)/shard_map/norm_in/pallas_call | solution.py:217
  54.2 37.2 %all-gather.4.cloned.1.call-done = bf16[2048,2048]{1,0:T(8,128)(2,1)} async-done(((bf16[64,2048]{1,0:T(8,128)(2,1)}), bf16[2048,2048]{1,0:T(8,128)(2,1)}) %all-gather.4.cloned.1.call-update) | async-done | bytes 8388624 | tf_op jit(solution)/shard_map/all_gather | solution.py:626
  91.4 22.0 %project.1.q_ref.k_ref.v_ref = bf16[2,2560,1536]{2,1,0:T(8,128)(2,1)} custom-call(bf16[2560,1024]{1,0:T(8,128)(2,1)} %norm_in.1.h_ref.left_ref, bf16[2,1024,2048]{2,1,0:T(8,128)(2,1)} %bitcast.53, f32[2,1,1536]{2,1,0:T(1,128)} %pad_maximum_fusion.6.bias_ref), custom_call_target="tpu_custom_call" | custom-call | flops 16106127360 | bytes 13631488 | tf_op jit(solution)/shard_map/project/pallas_call | solution.py:236
  113.4 32.6 %attend.1 = (bf16[2,2560,512]{2,1,0:T(8,128)(2,1)}, bf16[2,8,4,2,320,384]{5,4,3,2,1,0:T(8,128)(2,1)}, f32[2,2560,512]{2,1,0:T(8,128)}) custom-call(s32[8]{0:T(128)} %get-tuple-element.134.kept_ref, bf16[2,2560,1536]{2,1,0:T(8,128)(2,1)} %project.1.q_ref.k_ref.v_ref, bf16[2,2560,1536]{2,1,0:T(8,128)(2,1)} %project.1.q_ref.k_ref.v_ref, ...), custom_call_target="tpu_custom_call" | custom-call | flops 13421772800 | bytes 31457280 | tf_op jit(solution)/shard_map/attend/pallas_call | solution.py:74
  146.0 13.5 %mix.1 = (f32[2560,1024]{1,0:T(8,128)}, bf16[2560,1024]{1,0:T(8,128)(2,1)}) custom-call(bf16[2,2560,512]{2,1,0:T(8,128)(2,1)} %get-tuple-element.61.attn_ref.right_ref.o_ref, bf16[2,1024,2048]{2,1,0:T(8,128)(2,1)} %bitcast.54, bf16[2560,1024]{1,0:T(8,128)(2,1)} %x_ref.7, f32[8,1024]{1,0:T(8,128)} %concatenate.53.vec_ref), custom_call_target="tpu_custom_call" | custom-call | flops 5368709120 | bytes 10485760 | tf_op jit(solution)/shard_map/mix/pallas_call | solution.py:265
  159.5 10.5 %all-gather.6.cloned.1.call-done = bf16[2048,2048]{1,0:T(8,128)(2,1)} async-done(((bf16[64,2048]{1,0:T(8,128)(2,1)}), bf16[2048,2048]{1,0:T(8,128)(2,1)}) %all-gather.6.cloned.1.call-update) | async-done | bytes 8388624 | tf_op jit(solution)/shard_map/all_gather | solution.py:626
  170.0 48.2 %expand.1 = (bf16[2,2560,2048]{2,1,0:T(8,128)(2,1)}, bf16[2,2560,2048]{2,1,0:T(8,128)(2,1)}) custom-call(bf16[2560,1024]{1,0:T(8,128)(2,1)} %get-tuple-element.62.h_ref.left_ref, bf16[2,1024,2048]{2,1,0:T(8,128)(2,1)} %bitcast.75, f32[2,1,2048]{2,1,0:T(1,128)} %reshape.112.bias_ref), custom_call_target="tpu_custom_call" | custom-call | flops 32212254720 | bytes 13631488 | tf_op jit(solution)/shard_map/expand/pallas_call | solution.py:313
  218.2 30.6 %weight_grad.2 = bf16[2,1024,2304]{2,1,0:T(8,128)(2,1)} custom-call(bf16[2560,1024]{1,0:T(8,128)(2,1)} %broadcast_select_fusion.left_ref.g_ref.gm_ref, bf16[2,2560,2048]{2,1,0:T(8,128)(2,1)} %get-tuple-element.95.right_ref.act_ref), custom_call_target="tpu_custom_call" | custom-call | flops 21474836480 | bytes 26214400 | tf_op jit(solution)/shard_map/weight_grad/pallas_call | solution.py:383
  249.6 33.3 %expand_back.1 = (bf16[2,2560,2048]{2,1,0:T(8,128)(2,1)}, f32[2,1,2048]{2,1,0:T(1,128)}) custom-call(bf16[2560,1024]{1,0:T(8,128)(2,1)} %broadcast_select_fusion.left_ref.g_ref.gm_ref, bf16[2,1024,2048]{2,1,0:T(8,128)(2,1)} %bitcast.58, bf16[2,2560,2048]{2,1,0:T(8,128)(2,1)} %get-tuple-element.65.slope_ref), custom_call_target="tpu_custom_call" | custom-call | flops 21474836480 | bytes 41943040 | tf_op jit(solution)/shard_map/expand_back/pallas_call | solution.py:346
  282.9 29.8 %weight_grad.3 = bf16[2,1024,2304]{2,1,0:T(8,128)(2,1)} custom-call(bf16[2560,1024]{1,0:T(8,128)(2,1)} %get-tuple-element.62.h_ref.left_ref, bf16[2,2560,2048]{2,1,0:T(8,128)(2,1)} %get-tuple-element.67.right_ref.g_ref), custom_call_target="tpu_custom_call" | custom-call | flops 21474836480 | bytes 26214400 | tf_op jit(solution)/shard_map/weight_grad/pallas_call | solution.py:383
  312.7 39.9 %middle_back.1 = (f32[2560,1024]{1,0:T(8,128)}, bf16[2560,1024]{1,0:T(8,128)(2,1)}, bf16[2,2560,512]{2,1,0:T(8,128)(2,1)}, f32[8,1024]{1,0:T(8,128)}) custom-call(bf16[2,2560,2048]{2,1,0:T(8,128)(2,1)} %get-tuple-element.67.right_ref.g_ref, bf16[2,1024,2048]{2,1,0:T(8,128)(2,1)} %bitcast.76, f32[2560,1024]{1,0:T(8,128)} %get-tuple-element.68.mixed_ref, ...), custom_call_target="tpu_custom_call" | custom-call | flops 26843545600 | bytes 39845888 | tf_op jit(solution)/shard_map/middle_back/pallas_call | solution.py:462
  352.6 11.1 %weight_grad_slots.2 = bf16[32,64,512]{2,1,0:T(8,128)(2,1)} custom-call(s32[32]{0:T(128)} %copy-done.8, bf16[2560,1024]{1,0:T(8,128)(2,1)} %get-tuple-element.70.left_ref, bf16[2,2560,512]{2,1,0:T(8,128)(2,1)} %get-tuple-element.61.attn_ref.right_ref.o_ref), custom_call_target="tpu_custom_call" | custom-call | flops 5368709120 | bytes 10485760 | tf_op jit(solution)/shard_map/weight_grad_slots/pallas_call | solution.py:420
  363.7 1.3 slice.189
  365.4 42.3 %attend_back.1 = (bf16[2,2560,1536]{2,1,0:T(8,128)(2,1)}, f32[2,2,512]{2,1,0:T(2,128)}) custom-call(bf16[2,2560,1536]{2,1,0:T(8,128)(2,1)} %project.1.q_ref.k_ref.v_ref, bf16[2,2560,1536]{2,1,0:T(8,128)(2,1)} %project.1.q_ref.k_ref.v_ref, bf16[2,2560,1536]{2,1,0:T(8,128)(2,1)} %project.1.q_ref.k_ref.v_ref, bf16[2,2560,512]{2,1,0:T(8,128)(2,1)} %get-tuple-element.71.g_ref, ...), custom_call_target="tpu_custom_call" | custom-call | flops 20132659200 | bytes 62914560 | tf_op jit(solution)/shard_map/attend_back/pallas_call | solution.py:137
  407.9 1.5 collective-permute-start.6
  409.5 23.8 %weight_grad_slots.3 = bf16[32,64,1536]{2,1,0:T(8,128)(2,1)} custom-call(s32[64]{0:T(128)} %pad_add_fusion.slot_ref, bf16[2560,1024]{1,0:T(8,128)(2,1)} %norm_in.1.h_ref.left_ref, bf16[2,2560,1536]{2,1,0:T(8,128)(2,1)} %get-tuple-element.79.right_ref.g_ref), custom_call_target="tpu_custom_call" | custom-call | flops 16106127360 | bytes 20971520 | tf_op jit(solution)/shard_map/weight_grad_slots/pallas_call | solution.py:420
  433.3 4.1 fusion.19
  438.0 0.7 concatenate.59
  440.8 15.8 %input_back.2 = (f32[2560,1024]{1,0:T(8,128)}, f32[8,1024]{1,0:T(8,128)}) custom-call(bf16[2,2560,1536]{2,1,0:T(8,128)(2,1)} %get-tuple-element.79.right_ref.g_ref, bf16[2,1024,2048]{2,1,0:T(8,128)(2,1)} %bitcast.56, bf16[2560,1024]{1,0:T(8,128)(2,1)} %x_ref.7, f32[2560,1024]{1,0:T(8,128)} %get-tuple-element.80.gmixed_ref, f32[8,1024]{1,0:T(8,128)} %concatenate.53.vec_ref, ...), custom_call_target="tpu_custom_call" | custom-call | flops 8053063680 | bytes 8388608 | tf_op jit(solution)/shard_map/input_back/pallas_call | solution.py:505
  456.6 1.1 copy-done.1
  457.7 3.2 slice_add_fusion
  461.1 1.6 collective-permute-start.11
  463.2 2.0 collective-permute-start.10
  465.2 16.1 %input_back.3 = (f32[2560,1024]{1,0:T(8,128)}, f32[8,1024]{1,0:T(8,128)}) custom-call(bf16[2,2560,1536]{2,1,0:T(8,128)(2,1)} %get-tuple-element.79.right_ref.g_ref, bf16[2,1024,2048]{2,1,0:T(8,128)(2,1)} %bitcast.57, bf16[2560,1024]{1,0:T(8,128)(2,1)} %x_ref.7, f32[2560,1024]{1,0:T(8,128)} %get-tuple-element.80.gmixed_ref, ...), custom_call_target="tpu_custom_call", output_to_operand_aliasing={{0}: (6, {})} | custom-call | flops 8053063680 | bytes 8388608 | tf_op jit(solution)/shard_map/input_back/pallas_call | solution.py:505
  481.3 6.0 %collective-permute-done.11 = bf16[8,64,768]{2,1,0:T(8,128)(2,1)S(1)} collective-permute-done((bf16[8,64,768]{2,1,0:T(8,128)(2,1)S(1)}, bf16[8,64,768]{2,1,0:T(8,128)(2,1)S(1)}, u32[]{:S(2)}, u32[]{:S(2)}) %collective-permute-start.11) | collective-permute-done | bytes 786464 | tf_op jit(solution)/shard_map/ppermute | solution.py:562
  487.4 2.4 collective-permute-done.12
  489.7 0.9 copy-done.3
  490.6 0.8 fusion.20
  491.7 1.6 pad_maximum_fusion.1
  493.3 2.2 gather_fusion.1
  495.5 1.0 broadcast_select_fusion.1
  496.6 0.9 slice_add_fusion.11
  497.5 1.9 collective-permute-start.21
  499.6 1.2 slice_add_fusion.4
  500.8 1.4 slice_add_fusion.3
  502.3 1.0 collective-permute-start.15
  503.3 0.8 collective-permute-start.14
  504.1 17.9 %shrink.2.refs_0_ = bf16[2560,1024]{1,0:T(8,128)(2,1)} custom-call(s32[8]{0:T(128)} %get-tuple-element.134.kept_ref, bf16[2,2560,2048]{2,1,0:T(8,128)(2,1)} %get-tuple-element.95.right_ref.act_ref, bf16[2,1024,2048]{2,1,0:T(8,128)(2,1)} %bitcast.59, f32[2560,1024]{1,0:T(8,128)} %get-tuple-element.68.mixed_ref, f32[8,1024]{1,0:T(8,128)} %concatenate.53.vec_ref), custom_call_target="tpu_custom_call" | custom-call | flops 10737418240 | bytes 8388608 | tf_op jit(solution)/shard_map/shrink/pallas_call | solution.py:542
  522.1 1.1 collective-permute-start.16
  523.3 1.0 collective-permute-start.18
  524.3 2.0 collective-permute-start.17
  526.3 17.9 %shrink.3 = bf16[2560,1024]{1,0:T(8,128)(2,1)} custom-call(s32[8]{0:T(128)} %get-tuple-element.134.kept_ref, bf16[2,2560,2048]{2,1,0:T(8,128)(2,1)} %get-tuple-element.95.right_ref.act_ref, bf16[2,1024,2048]{2,1,0:T(8,128)(2,1)} %bitcast.60, f32[2560,1024]{1,0:T(8,128)} %get-tuple-element.68.mixed_ref, ...), custom_call_target="tpu_custom_call", output_to_operand_aliasing={{}: (5, {})} | custom-call | flops 10737418240 | bytes 8388608 | tf_op jit(solution)/shard_map/shrink/pallas_call | solution.py:542
  544.2 0.9 collective-permute-done.17
  546.2 2.9 collective-permute-done.22
  549.9 4.2 collective-permute-done.23
  554.2 2.1 collective-permute-start.20
  556.4 1.4 collective-permute-done.24
  559.5 1.3 collective-permute-done.19
  561.2 0.9 copy.43
  562.1 1.8 convert_bitcast_fusion
  563.9 1.8 slice_convert_fusion
  (137 shorter events, 16.0 us)
Async XLA Ops:
  7.2 84.2 %all-gather.4.cloned.1.call-start = ((), (), s32[]{:S(2)}) async-start(), calls=%async_computation.2 | async-start | bytes 8650752 | tf_op jit(solution)/shard_map/all_gather | solution.py:626
  9.8 160.3 %all-gather.6.cloned.1.call-start = ((), (), s32[]{:S(2)}) async-start(), calls=%async_computation.3 | async-start | bytes 8650752 | tf_op jit(solution)/shard_map/all_gather | solution.py:626
  10.5 239.1 %all-gather.8.cloned.1.call-start = ((), (), s32[]{:S(2)}) async-start(), calls=%async_computation.4 | async-start | bytes 8650752 | tf_op jit(solution)/shard_map/all_gather | solution.py:626
  11.2 550.9 %reduce-scatter.5.cloned.1.call-start = ((), (), s32[]{:S(2)}) async-start(), calls=%async_computation.6 | async-start | bytes 9732096 | tf_op jit(solution)/shard_map/reduce_scatter | solution.py:632
  13.4 11.5 %collective-permute-start = (f32[1,12,32]{2,1,0:T(8,128)S(1)}, f32[1,12,32]{2,1,0:T(8,128)S(1)}, u32[]{:S(2)}, u32[]{:S(2)}) collective-permute-start(f32[1,12,32]{2,1,0:T(8,128)S(1)} %maximum_bitcast_fusion), channel_id=1, source_target_pairs={{0,1},{1,0},{2,3},{3,2},{4,5},{5,4},{6,7},{7,6},{8,9},{9,8},{10,11... | collective-permute-start | bytes 4616 | tf_op jit(solution)/shard_map/ppermute | solution.py:562
  24.9 1.2 collective-permute-start.1
  26.2 3.9 collective-permute-start.2
  30.1 5.2 collective-permute-start.3
  35.3 7.3 %collective-permute-start.4 = (f32[16,12,32]{2,1,0:T(8,128)S(1)}, f32[16,12,32]{2,1,0:T(8,128)S(1)}, u32[]{:S(2)}, u32[]{:S(2)}) collective-permute-start(f32[16,12,32]{2,1,0:T(8,128)S(1)} %get-tuple-element.139), channel_id=1, source_target_pairs={{0,16},{2,18},{4,20},{6,22},{8,24},{10,26},{12,28},{14,30},{16,0},... | collective-permute-start | bytes 73736 | tf_op jit(solution)/shard_map/ppermute | solution.py:562
  248.9 315.0 %reduce-scatter.3.cloned.1.call-start = ((), (), s32[]{:S(2)}) async-start(), calls=%async_computation.5 | async-start | bytes 9732096 | tf_op jit(solution)/shard_map/reduce_scatter | solution.py:632
  248.9 34.0 %copy-start.8 = (s32[32]{0:T(128)}, s32[32]{0:T(128)S(1)}, u32[]{:S(2)}) copy-start(s32[32]{0:T(128)S(1)} %add_add_fusion.slot_ref) | copy-start | bytes 388
  365.1 42.7 %collective-permute-start.5 = (bf16[16,64,512]{2,1,0:T(8,128)(2,1)S(1)}, bf16[16,64,512]{2,1,0:T(8,128)(2,1)S(1)}, u32[]{:S(2)}, u32[]{:S(2)}) collective-permute-start(bf16[16,64,512]{2,1,0:T(8,128)(2,1)S(1)} %slice.189), channel_id=1, source_target_pairs={{0,2},{2,0},{4,6},{6,4},{8,10},{10,8},{12,14},{14,12},{16,18},{18,... | collective-permute-start | bytes 3145736 | tf_op jit(solution)/shard_map/ppermute | solution.py:562
  365.4 42.3 %copy-start = (bf16[32,64,512]{2,1,0:T(8,128)(2,1)S(1)}, bf16[32,64,512]{2,1,0:T(8,128)(2,1)}, u32[]{:S(2)}) copy-start(bf16[32,64,512]{2,1,0:T(8,128)(2,1)} %weight_grad_slots.2) | copy-start | bytes 6291460
  407.9 25.3 %collective-permute-start.6 = (bf16[8,64,512]{2,1,0:T(8,128)(2,1)S(1)}, bf16[8,64,512]{2,1,0:T(8,128)(2,1)S(1)}, u32[]{:S(2)}, u32[]{:S(2)}) collective-permute-start(bf16[8,64,512]{2,1,0:T(8,128)(2,1)S(1)} %slice.251), channel_id=1, source_target_pairs={{0,1},{1,0},{2,3},{3,2},{4,5},{5,4},{6,7},{7,6},{8,9},{9,8},{10,11... | collective-permute-start | bytes 1572872 | tf_op jit(solution)/shard_map/ppermute | solution.py:562
  433.3 4.7 copy-start.6
  433.3 4.7 copy-start.5
  433.3 5.5 copy-start.7
  437.4 19.2 %collective-permute-start.9 = (bf16[16,64,768]{2,1,0:T(8,128)(2,1)}, bf16[16,64,768]{2,1,0:T(8,128)(2,1)S(1)}, u32[]{:S(2)}, u32[]{:S(2)}) collective-permute-start(bf16[16,64,768]{2,1,0:T(8,128)(2,1)} %get-tuple-element.137), channel_id=1, source_target_pairs={{0,2},{2,0},{4,6},{6,4},{8,10},{10,8},{12,14},{14,12},{16,18},{18,... | collective-permute-start | bytes 4718600 | tf_op jit(solution)/shard_map/ppermute | solution.py:562
  437.4 19.2 %collective-permute-start.8 = (bf16[16,64,768]{2,1,0:T(8,128)(2,1)}, bf16[16,64,768]{2,1,0:T(8,128)(2,1)}, u32[]{:S(2)}, u32[]{:S(2)}) collective-permute-start(bf16[16,64,768]{2,1,0:T(8,128)(2,1)} %get-tuple-element.138), channel_id=1, source_target_pairs={{0,2},{2,0},{4,6},{6,4},{8,10},{10,8},{12,14},{14,12},{16,18},{18,... | collective-permute-start | bytes 4718600 | tf_op jit(solution)/shard_map/ppermute | solution.py:562
  439.6 17.0 %collective-permute-start.7 = (bf16[4,64,512]{2,1,0:T(8,128)(2,1)S(1)}, bf16[4,64,512]{2,1,0:T(8,128)(2,1)S(1)}, u32[]{:S(2)}, u32[]{:S(2)}) collective-permute-start(bf16[4,64,512]{2,1,0:T(8,128)(2,1)S(1)} %slice.253), channel_id=1, source_target_pairs={{0,4},{2,6},{4,0},{6,2},{8,12},{10,14},{12,8},{14,10},{16,20},{18,... | collective-permute-start | bytes 786440 | tf_op jit(solution)/shard_map/ppermute | solution.py:562
  456.6 1.1 copy-start.1
  461.1 26.3 %collective-permute-start.11 = (bf16[8,64,768]{2,1,0:T(8,128)(2,1)S(1)}, bf16[8,64,768]{2,1,0:T(8,128)(2,1)S(1)}, u32[]{:S(2)}, u32[]{:S(2)}) collective-permute-start(bf16[8,64,768]{2,1,0:T(8,128)(2,1)S(1)} %slice.256), channel_id=1, source_target_pairs={{0,1},{1,0},{2,3},{3,2},{4,5},{5,4},{6,7},{7,6},{8,9},{9,8},{10,11... | collective-permute-start | bytes 2359304 | tf_op jit(solution)/shard_map/ppermute | solution.py:562
  462.7 27.1 %collective-permute-start.12 = (bf16[8,64,768]{2,1,0:T(8,128)(2,1)S(1)}, bf16[8,64,768]{2,1,0:T(8,128)(2,1)S(1)}, u32[]{:S(2)}, u32[]{:S(2)}) collective-permute-start(bf16[8,64,768]{2,1,0:T(8,128)(2,1)S(1)} %slice.257), channel_id=1, source_target_pairs={{0,4},{2,6},{4,0},{6,2},{8,12},{10,14},{12,8},{14,10},{16,20},{18,... | collective-permute-start | bytes 2359304 | tf_op jit(solution)/shard_map/ppermute | solution.py:562
  463.2 18.2 %collective-permute-start.10 = (bf16[2,64,512]{2,1,0:T(8,128)(2,1)S(1)}, bf16[2,64,512]{2,1,0:T(8,128)(2,1)S(1)}, u32[]{:S(2)}, u32[]{:S(2)}) collective-permute-start(bf16[2,64,512]{2,1,0:T(8,128)(2,1)S(1)} %slice.255), channel_id=1, source_target_pairs={{0,16},{2,18},{4,20},{6,22},{8,24},{10,26},{12,28},{14,30},{16,0},... | collective-permute-start | bytes 393224 | tf_op jit(solution)/shard_map/ppermute | solution.py:562
  481.3 10.1 %copy-start.4 = (bf16[2,64,512]{2,1,0:T(8,128)(2,1)}, bf16[2,64,512]{2,1,0:T(8,128)(2,1)S(1)}, u32[]{:S(2)}) copy-start(bf16[2,64,512]{2,1,0:T(8,128)(2,1)S(1)} %collective-permute-done.10) | copy-start | bytes 393220
  487.4 2.4 copy-start.2
  489.7 0.9 copy-start.3
  497.5 48.0 %collective-permute-start.21 = (bf16[1,64,512]{2,1,0:T(8,128)(2,1)S(1)}, bf16[1,64,512]{2,1,0:T(8,128)(2,1)S(1)}, u32[]{:S(2)}, u32[]{:S(2)}) collective-permute-start(bf16[1,64,512]{2,1,0:T(8,128)(2,1)S(1)} %slice.275), channel_id=1, source_target_pairs={{0,8},{2,10},{4,12},{6,14},{8,0},{10,2},{12,4},{14,6},{16,24},{18,... | collective-permute-start | bytes 196616 | tf_op jit(solution)/shard_map/ppermute | solution.py:562
  499.5 22.5 %collective-permute-start.13 = (f32[16,12,32]{2,1,0:T(8,128)S(1)}, f32[16,12,32]{2,1,0:T(8,128)S(1)}, u32[]{:S(2)}, u32[]{:S(2)}) collective-permute-start(f32[16,12,32]{2,1,0:T(8,128)S(1)} %slice.206), channel_id=1, source_target_pairs={{0,2},{2,0},{4,6},{6,4},{8,10},{10,8},{12,14},{14,12},{16,18},{18,... | collective-permute-start | bytes 73736 | tf_op jit(solution)/shard_map/ppermute | solution.py:562
  502.3 19.7 %collective-permute-start.15 = (bf16[4,64,768]{2,1,0:T(8,128)(2,1)S(1)}, bf16[4,64,768]{2,1,0:T(8,128)(2,1)S(1)}, u32[]{:S(2)}, u32[]{:S(2)}) collective-permute-start(bf16[4,64,768]{2,1,0:T(8,128)(2,1)S(1)} %slice.261), channel_id=1, source_target_pairs={{0,1},{1,0},{2,3},{3,2},{4,5},{5,4},{6,7},{7,6},{8,9},{9,8},{10,11... | collective-permute-start | bytes 1179656 | tf_op jit(solution)/shard_map/ppermute | solution.py:562
  503.3 18.7 %collective-permute-start.14 = (bf16[4,64,768]{2,1,0:T(8,128)(2,1)S(1)}, bf16[4,64,768]{2,1,0:T(8,128)(2,1)S(1)}, u32[]{:S(2)}, u32[]{:S(2)}) collective-permute-start(bf16[4,64,768]{2,1,0:T(8,128)(2,1)S(1)} %slice.259), channel_id=1, source_target_pairs={{0,4},{2,6},{4,0},{6,2},{8,12},{10,14},{12,8},{14,10},{16,20},{18,... | collective-permute-start | bytes 1179656 | tf_op jit(solution)/shard_map/ppermute | solution.py:562
  522.1 22.2 %collective-permute-start.16 = (f32[8,12,32]{2,1,0:T(8,128)S(1)}, f32[8,12,32]{2,1,0:T(8,128)S(1)}, u32[]{:S(2)}, u32[]{:S(2)}) collective-permute-start(f32[8,12,32]{2,1,0:T(8,128)S(1)} %slice.262), channel_id=1, source_target_pairs={{0,1},{1,0},{2,3},{3,2},{4,5},{5,4},{6,7},{7,6},{8,9},{9,8},{10,11... | collective-permute-start | bytes 36872 | tf_op jit(solution)/shard_map/ppermute | solution.py:562
  523.3 20.9 %collective-permute-start.18 = (bf16[2,64,768]{2,1,0:T(8,128)(2,1)S(1)}, bf16[2,64,768]{2,1,0:T(8,128)(2,1)S(1)}, u32[]{:S(2)}, u32[]{:S(2)}) collective-permute-start(bf16[2,64,768]{2,1,0:T(8,128)(2,1)S(1)} %slice.266), channel_id=1, source_target_pairs={{0,16},{2,18},{4,20},{6,22},{8,24},{10,26},{12,28},{14,30},{16,0},... | collective-permute-start | bytes 589832 | tf_op jit(solution)/shard_map/ppermute | solution.py:562
  524.3 20.8 %collective-permute-start.17 = (bf16[2,64,768]{2,1,0:T(8,128)(2,1)S(1)}, bf16[2,64,768]{2,1,0:T(8,128)(2,1)S(1)}, u32[]{:S(2)}, u32[]{:S(2)}) collective-permute-start(bf16[2,64,768]{2,1,0:T(8,128)(2,1)S(1)} %slice.264), channel_id=1, source_target_pairs={{0,16},{2,18},{4,20},{6,22},{8,24},{10,26},{12,28},{14,30},{16,0},... | collective-permute-start | bytes 589832 | tf_op jit(solution)/shard_map/ppermute | solution.py:562
  545.2 4.0 collective-permute-start.22
  549.1 5.0 collective-permute-start.23
  554.1 3.7 collective-permute-start.24
  554.2 5.3 collective-permute-start.20
  556.3 4.6 collective-permute-start.19
Sparse Core Ops, SparseCore 0:
  11.4 79.9 all-gather.3
  94.3 75.6 all-gather.5
  172.9 75.6 all-gather.7
  254.4 134.7 reduce-scatter.4
  395.0 162.8 reduce-scatter.2

commit v3 on v2

--- a/solution.py
+++ b/solution.py
@@ -285,11 +285,10 @@
 
 
 def gelu_parts(pre):
-    square = pre * pre
-    tanh = jnp.tanh(pre * (GELU_IN + (GELU_IN * GELU_CUBE) * square))
-    half = 0.5 * tanh + 0.5
-    slope = half + (0.5 * pre * (1.0 - tanh * tanh)) * (GELU_IN + (3.0 * GELU_IN * GELU_CUBE) * square)
-    return pre * half, slope
+    cube = (GELU_IN * GELU_CUBE) * (pre * pre)
+    half = 0.5 * jnp.tanh(pre * (GELU_IN + cube)) + 0.5
+    act = pre * half
+    return act, half + (act - act * half) * (2.0 * GELU_IN + 6.0 * cube)
 
 
 CHUNK = 512
@@ -364,71 +363,106 @@
     return lax.dot_general(left, right, (((0,), (0,)), ((), ())), preferred_element_type=f32)
 
 
-def weight_grad_kernel(left_ref, right_ref, out_ref, *, chunk, used):
+def weight_grad_kernel(left_ref, right_ref, out_ref, *, chunk, fill):
     which = pl.program_id(1)
     start = pl.multiple_of(which * chunk, chunk)
     out_ref[0, :, pl.ds(start, chunk)] = dot_rows(left_ref[...], right_ref[0]).astype(bf16)
-    if out_ref.shape[2] > used:
+    if fill:
 
         @pl.when(which == 0)
         def _():
-            spare = out_ref.shape[2] - used
-            out_ref[0, :, used:] = jnp.zeros((out_ref.shape[1], spare), bf16)
-
-
-def weight_grad(left, right, spare=0):
+            spare = jnp.zeros((out_ref.shape[1], fill), bf16)
+            out_ref[0, :, out_ref.shape[2] - fill :] = spare
+
+
+def weight_grad(left, right, used, spare, fill):
+    rows, width = left.shape
+    shards = right.shape[0]
+    chunk = min(512, used)
+    block = (1, width, used + spare)
+    return call(
+        functools.partial(weight_grad_kernel, chunk=chunk, fill=spare if fill else 0),
+        "weight_grad",
+        (shards, used // chunk),
+        [
+            fixed((rows, width), 0, 0),
+            pl.BlockSpec((1, rows, chunk), lambda t, n: (t, 0, n)),
+        ],
+        [(block, lambda t, n: (t, 0, 0), (shards,) + block[1:], bf16)],
+        estimate=cost(2 * rows * width * used * shards, left, right),
+    )(left, right)[0]
+
+
+def weight_grad_into_kernel(left_ref, right_ref, _, out_ref):
+    out_ref[0] = dot_rows(left_ref[...], right_ref[0]).astype(bf16)
+
+
+def weight_grad_into(left, right, out):
     rows, width = left.shape
     shards, _, cols = right.shape
-    chunk = min(512, cols)
-    return call(
-        functools.partial(weight_grad_kernel, chunk=chunk, used=cols),
-        "weight_grad",
-        (shards, cols // chunk),
+    place = out.shape[2] // cols - 1
+    return call(
+        weight_grad_into_kernel,
+        "weight_grad_into",
+        (shards,),
         [
             fixed((rows, width), 0, 0),
-            pl.BlockSpec((1, rows, chunk), lambda t, n: (t, 0, n)),
-        ],
-        [
-            (
-                (1, width, cols + spare),
-                lambda t, n: (t, 0, 0),
-                (shards, width, cols + spare),
-                bf16,
-            )
-        ],
+            pl.BlockSpec((1, rows, cols), lambda t: (t, 0, 0)),
+            pl.BlockSpec(memory_space=pl.ANY),
+        ],
+        [((1, width, cols), lambda t: (t, 0, place), out.shape, bf16)],
+        aliases={2: 0},
         estimate=cost(2 * rows * width * cols * shards, left, right),
-    )(left, right)[0]
-
-
-def weight_grad_slots_kernel(slot_ref, left_ref, right_ref, out_ref, *, owners, per_chain):
+    )(left, right, out)[0]
+
+
+def weight_grad_split_kernel(slot_ref, left_ref, right_ref, *out_refs, per_chain):
     which, shard = pl.program_id(0), pl.program_id(1)
     grad = dot_rows(left_ref[...], right_ref[0]).astype(bf16)
-    part = out_ref.shape[1]
-    base = which // per_chain * out_ref.shape[0] + shard * owners
-    for owner in range(owners):
-        out_ref[slot_ref[base + owner]] = grad[owner * part : (owner + 1) * part]
-
-
-def weight_grad_slots(left, right, slots, chains):
+    pairs = grad.shape[0] // (2 * out_refs[0].shape[1])
+    second = slot_ref[slot_ref.shape[0] - 1] == 1
+    for chain in range(len(out_refs) // 2):
+
+        @pl.when(which // per_chain == chain)
+        def _():
+            near_ref, far_ref = out_refs[2 * chain : 2 * chain + 2]
+            part = near_ref.shape[1]
+            base = chain * near_ref.shape[0] + shard * pairs
+            for pair in range(pairs):
+                slot = slot_ref[base + pair]
+                low = grad[2 * pair * part : (2 * pair + 1) * part]
+                high = grad[(2 * pair + 1) * part : (2 * pair + 2) * part]
+                near_ref[slot] = jnp.where(second, high, low)
+                far_ref[slot] = jnp.where(second, low, high)
+
+
+def weight_grad_split(left, right, first, share, tables, second):
     rows, width = left.shape
-    shards, _, cols = right.shape
-    count = slots.shape[0] // chains
-    owners = count // shards
-    part = width // owners
-    share = cols // chains
+    shards, _, _ = right.shape
+    chains = len(tables)
+    half = tables[0].shape[0]
+    part = width // (2 * half // shards)
     chunk = share if share <= 1024 else 512
-    return call(
-        functools.partial(weight_grad_slots_kernel, owners=owners, per_chain=share // chunk),
-        "weight_grad_slots",
-        (cols // chunk, shards),
+    per_chain = share // chunk
+    out = lambda chain: (
+        (half, part, chunk),
+        lambda n, t, s: (0, 0, jnp.clip(n - chain * per_chain, 0, per_chain - 1)),
+        (half, part, share),
+        bf16,
+    )
+    parts = call(
+        functools.partial(weight_grad_split_kernel, per_chain=per_chain),
+        "weight_grad_split",
+        (chains * per_chain, shards),
         [
             fixed((rows, width), 0, 0),
-            pl.BlockSpec((1, rows, chunk), lambda n, t, s: (t, 0, n)),
-        ],
-        [((count, part, chunk), lambda n, t, s: (0, 0, n), (count, part, cols), bf16)],
+            pl.BlockSpec((1, rows, chunk), lambda n, t, s: (t, 0, first // chunk + n)),
+        ],
+        [out(chain) for chain in range(chains) for _ in range(2)],
         prefetch=1,
-        estimate=cost(2 * rows * width * cols * shards, left, right),
-    )(slots, left, right)[0]
+        estimate=cost(2 * rows * width * share * chains * shards, left, right),
+    )(jnp.concatenate(list(tables) + [second[None]]), left, right)
+    return [(parts[2 * chain], parts[2 * chain + 1]) for chain in range(chains)]
 
 
 def middle_back_kernel(
@@ -447,7 +481,7 @@
     gmixed_ref[...] = grad_mixed
     rounded = grad_mixed.astype(bf16)
     go_ref[...] = rounded
-    for index, value in enumerate((grad_h * normed, grad_h, grad_mixed, grad)):
+    for index, value in ((1, grad_h * normed), (3, grad_h), (4, grad_mixed), (5, grad)):
         sums_ref[index : index + 1, :] += jnp.sum(value, axis=0, keepdims=True)
     for shard in range(gattn_ref.shape[0]):
         gattn_ref[shard] = dot(rounded, out_w_ref[shard]).astype(bf16)
@@ -493,7 +527,7 @@
         grad_h += dot_flip(g_ref[shard], w_ref[shard])
     normed, inverse = norm_parts(x_ref[...].astype(f32))
     out_ref[...] = gmixed_ref[...] + norm_back(grad_h * row(vec_ref, GAIN1), normed, inverse)
-    for index, value in enumerate((grad_h * normed, grad_h)):
+    for index, value in ((0, grad_h * normed), (2, grad_h)):
         sums_ref[index : index + 1, :] += jnp.sum(value, axis=0, keepdims=True)
 
 
@@ -517,7 +551,7 @@
         + [pl.BlockSpec(memory_space=pl.ANY)] * len(out),
         [
             ((SEQ, width), step, (rows, width), f32),
-            ((8, width), lambda i: (0, 0), (8, width), f32),
+            (sums.shape, lambda i: (0, 0), sums.shape, f32),
         ],
         aliases={6: 0} if out else None,
         estimate=cost(2 * count * SEQ * width * cols * shards, weights),
@@ -577,29 +611,28 @@
     return values.reshape((lax.axis_size("dp"), lax.axis_size("tensor")) + part.shape)
 
 
-def owner_tables(order):
+def slot_table(order):
     dp, shards = lax.axis_size("dp"), lax.axis_size("tensor")
-    here = {axis: lax.axis_index(axis).astype(jnp.int32) for axis in ("dp", "tensor")}
-    index = jnp.arange(dp * shards, dtype=jnp.int32)
-    apart = {"tensor": (index // dp) ^ here["tensor"], "dp": (index % dp) ^ here["dp"]}
+    index = jnp.arange(shards * dp // 2, dtype=jnp.int32)
+    apart = {
+        "tensor": (index // (dp // 2)) ^ lax.axis_index("tensor").astype(jnp.int32),
+        "dp": (2 * (index % (dp // 2))) ^ lax.axis_index("dp").astype(jnp.int32),
+    }
     slot = jnp.zeros_like(index)
-    place = dict(here)
-    for depth, (axis, bit) in enumerate(order):
-        weight = 1 << (len(order) - 1 - depth)
-        slot += jnp.where((apart[axis] & bit) != 0, weight, 0)
-        place[axis] = place[axis] ^ jnp.where((index & weight) != 0, bit, 0)
-    return slot, place["tensor"] * dp + place["dp"]
+    for depth, (axis, bit) in enumerate(order[1:]):
+        slot += jnp.where((apart[axis] & bit) != 0, 1 << (len(order) - 2 - depth), 0)
+    return slot
 
 
 class Chain:
-    def __init__(self, values, order):
-        self.values, self.order = values, list(order)
+    def __init__(self, near, far, order):
+        self.near, self.order = near, list(order)
+        self.far = swap(far, *self.order.pop(0))
 
     def send(self):
-        axis, bit = self.order.pop(0)
         half = self.values.shape[0] // 2
         self.near = self.values[:half]
-        self.far = swap(self.values[half:], axis, bit)
+        self.far = swap(self.values[half:], *self.order.pop(0))
 
     def settle(self):
         self.values = self.near + self.far
@@ -610,6 +643,20 @@
             self.send()
             self.settle()
         return self.values[0]
+
+
+class Sum(Chain):
+    def __init__(self, values, order):
+        self.values, self.order = values, list(order)
+        self.send()
+
+    def send(self):
+        self.near = self.values
+        self.far = swap(self.values, *self.order.pop(0))
+
+    def finish(self):
+        super().finish()
+        return self.values
 
 
 def meet(values, *chains):
@@ -664,8 +711,8 @@
     core, along_x = [("dp", 1)], [("tensor", bit) for bit in bits_of("tensor")[::-1]]
     low, high = [("dp", 2)], [("dp", bit) for bit in bits_of("dp")[::-1] if bit > 2]
     order_x, order_low = core + along_x + low + high, core + low + along_x + high
-    slots_x, owners_x = owner_tables(order_x)
-    slots_both = jnp.concatenate([slots_x, owner_tables(order_low)[0]])
+    tables = [slot_table(order_x), slot_table(order_low)]
+    second = lax.axis_index("dp").astype(jnp.int32) & 1
 
     h1 = norm_in(tokens, vectors)
     qkv = project(h1, full_heads, bias_heads)
@@ -673,79 +720,79 @@
     mixed, h2 = mix(attn, full_heads, tokens, vectors)
     act, slope = expand(h2, full_up, bias_up)
 
-    spare = act.shape[2] // 8
-    grad_down = weight_grad(grad_m, act, spare)
+    hidden = act.shape[2]
+    grad_down = weight_grad(grad_m, act, hidden, hidden // 8, True)
     grad_m, grad_down = barrier((grad_m, grad_down))
-    sent_down = scatter(grad_down)[:, : act.shape[2]]
+    sent_down = scatter(grad_down)[:, :hidden]
     grad_pre, grad_bias_up = expand_back(grad_m, full_down, slope)
-    grad_up = weight_grad(h2, grad_pre, spare)
-    grad_pre, grad_up = barrier((grad_pre, grad_up))
-    sent_up = scatter(grad_up)[:, : act.shape[2]]
+
+    share = hidden // 2
+    ((near, far),) = weight_grad_split(h2, grad_pre, share, share, tables[:1], second)
+    grad_pre, near, far = barrier((grad_pre, near, far))
+    chain_up = Chain(near, far, order_x)
+    grad_first = weight_grad(h2, grad_pre, share, cols, False)
+    grad_pre, grad_first = barrier((grad_pre, grad_first))
+    grad_pre = meet(grad_pre, chain_up)
     grad_mixed, grad_o, grad_attn, sums2 = middle_back(
         grad_pre, full_up, mixed, grad_m, vectors, full_heads
     )
-
-    grad_out = weight_grad_slots(grad_o, attn, slots_x, 1)
-    grad_attn, grad_out = barrier((grad_attn, grad_out))
-    chain_out = Chain(grad_out, order_x)
-    chain_out.send()
+    grad_o = meet(grad_o, chain_up)
+    grad_first = weight_grad_into(grad_o, attn, grad_first)
+    grad_attn, grad_first = barrier((grad_attn, grad_first))
     grad_heads, grad_bias_qv = attend_back(qkv, grad_attn, attn, expo, inverse_sum)
-    grad_heads = meet(grad_heads, chain_out)
+    grad_heads = meet(grad_heads, chain_up)
+    grad_heads, sent_down, grad_first = barrier((grad_heads, sent_down, grad_first))
+    sent_first = scatter(grad_first)
+
     chains = 2 if (3 * cols // 2) % LANES == 0 else 1
-    grad_qkv = weight_grad_slots(h1, grad_heads, slots_both if chains == 2 else slots_x, chains)
-    grad_qkv = meet(grad_qkv, chain_out)
-    grad_heads, grad_qkv = barrier((grad_heads, grad_qkv))
-    share = 3 * cols // chains
-    chains_qkv = [
-        Chain(grad_qkv[..., share * at : share * (at + 1)], order)
-        for at, order in enumerate((order_x, order_low)[:chains])
-    ]
-    for chain in chains_qkv:
-        chain.send()
-
+    halves = weight_grad_split(h1, grad_heads, 0, 3 * cols // chains, tables[:chains], second)
+    grad_heads, halves = barrier((grad_heads, halves))
+    chains_qkv = [Chain(*half, order) for half, order in zip(halves, (order_x, order_low))]
+    sums = jnp.concatenate(
+        [
+            sums2[:6],
+            grad_bias_qv.transpose(1, 0, 2).reshape(2, width),
+            grad_bias_up.reshape(-1, width),
+        ],
+        0,
+    )
+    grad_heads = meet(grad_heads, chain_up)
     first = images // 2
-    blank = jnp.zeros((8, width), f32)
-    grad_tokens, sums1 = input_back(
-        0, first, grad_heads, full_heads, tokens, grad_mixed, vectors, blank
-    )
-    sums1 = meet(sums1, chain_out, *chains_qkv)
-    grad_tokens, sums1 = input_back(
-        first, images - first, grad_heads, full_heads, tokens, grad_mixed, vectors, sums1, grad_tokens
-    )
-    sums1, act = meet((sums1, act), chain_out, *chains_qkv)
-
-    sums = jnp.stack([sums1[0], sums2[0], sums1[1], sums2[1], sums2[2], sums2[3]])
-    packed = jnp.concatenate(
-        [
-            sums.reshape(6, dp, shards, own).transpose(2, 1, 0, 3),
-            grad_bias_qv.reshape(shards, 2, dp, own).transpose(0, 2, 1, 3),
-            grad_bias_up.reshape(shards, dp, -1, own),
-        ],
-        2,
-    )
-    packed = jnp.take(packed.reshape((dp * shards,) + packed.shape[2:]), owners_x, axis=0)
-    packed, act = barrier((packed, act))
-    chain_small = Chain(packed, order_x)
-    chain_small.send()
+    grad_tokens, sums = input_back(
+        0, first, grad_heads, full_heads, tokens, grad_mixed, vectors, sums
+    )
+    sums = meet(sums, *chains_qkv)
+    grad_tokens, sums = input_back(
+        first, images - first, grad_heads, full_heads, tokens, grad_mixed, vectors, sums, grad_tokens
+    )
+    chain_small = Sum(sums, order_x)
+    act = meet(barrier((act, sums))[0], *chains_qkv)
     layer_out = shrink(0, first, kept_own, act, full_down, mixed, vectors)
     layer_out = meet(layer_out, chain_small, *chains_qkv)
     layer_out = shrink(first, images - first, kept_own, act, full_down, mixed, vectors, layer_out)
     layer_out = meet(layer_out, chain_small, *chains_qkv)
+    sent_up = jnp.concatenate([sent_first[:, :share], chain_up.finish()], 1)
     sent_qkv = jnp.concatenate([chain.finish() for chain in chains_qkv], 1)
-    sent_out = chain_out.finish()
-    sent_small = chain_small.finish()
+    small = chain_small.finish()
+    at_dp, at_tensor = lax.axis_index("dp"), lax.axis_index("tensor")
+    row_place, shard_place = at_dp * shards + at_tensor, at_tensor * dp + at_dp
+    rows_own = lax.dynamic_slice(small, (0, row_place * own), (6, own))
+    heads_own = lax.dynamic_slice(small, (6, shard_place * own), (2, own))
+    count = up_bias.shape[0]
+    start = shard_place * count
+    up_own = lax.dynamic_slice(small, (8 + start // width, start % width), (1, count))
 
     return (
         layer_out,
         grad_tokens,
         sent_qkv.astype(f32).reshape(part, 3, cols).transpose(1, 0, 2),
-        sent_out.astype(f32).T,
+        sent_first[:, share:].astype(f32).T,
         sent_up.astype(f32),
         sent_down.astype(f32).T,
-        sent_small[6:8],
-        sent_small[8:].reshape(-1),
-        sent_small[:2],
-        sent_small[2:6],
+        heads_own,
+        up_own.reshape(-1),
+        rows_own[:2],
+        rows_own[2:],
     )
 
 

time: 582 us -> 574 us (0.986)
  local copies, waits for them, and re-layouts: 20.1 us -> 9.26 us
  waiting for transfers between devices: 80.7 us -> 87.9 us
  other arithmetic: 26.8 us -> 19.7 us
    pallas_call x4 -> x5, Pallas kernels: 95.3 us -> 101 us  [the longest x2 46.6 us: weight_grad(): call(functools.partial(weight_grad_kernel, chunk=chunk, fill=spare if fil...]
  transfers between devices with their start and end apart: 30 -> 30, of which waited for: 13 -> 14; matrix products, arithmetic and copies ran while one was open for 7% -> 4% of each run, Pallas kernels for 70% -> 72%
where the time goes in v3:
time: 574 us; the launch traced here: 565 us
  Pallas kernels  407 us (71%)
  waiting for transfers between devices  87.9 us (15%)
  starting transfers between devices  26.2 us (5%)
  other arithmetic  19.7 us (3%)
  between operations  14.4 us (3%)
  local copies, waits for them, and re-layouts  9.26 us (2%)
    all_gather x3, waiting for transfers between devices, gather(): full = lax.all_gather(part, ('tensor', 'dp'), axis=0, tiled=True)  50 us
    pallas_call x2, Pallas kernels, weight_grad(): call(functools.partial(weight_grad_kernel, chunk=chunk, fill=spare if fil...  46.6 us
    pallas_call x1, Pallas kernels, expand(): call(expand_kernel, 'expand', (shards, rows // size), [pl.BlockSpec((size...  45.9 us
    pallas_call x2, Pallas kernels, weight_grad_split(): call(functools.partial(weight_grad_split_kernel, per_chain=per_chain), 'w...  43.7 us
    pallas_call x1, Pallas kernels, attend_back(): pl.pallas_call(functools.partial(attend_back_kernel, pairs=pairs), grid=(...  41.7 us
    pallas_call x1, Pallas kernels, middle_back(): call(middle_back_kernel, 'middle_back', (rows // SEQ,), [pl.BlockSpec((sh...  40.2 us
    ppermute x25, waiting for transfers between devices, swap(): lax.ppermute(values, axis, [(place, place ^ bit) for place in places])  36.5 us
    pallas_call x2, Pallas kernels, shrink(): call(functools.partial(shrink_kernel, first=first), 'shrink', (count,), [...  35.9 us
  transfers between devices with their start and end apart: 30, of which 14 were waited for; matrix products, arithmetic and copies ran while one was open for 4% of the time, Pallas kernels for 72%

profile of v3, /device:TPU:0, one launch (start us, length us, event | category | flops | bytes accessed | tf_op | source)
XLA Modules:
  0.0 564.8 jit_solution(13275798048476218967)
XLA Ops:
  7.2 0.9 copy.39
  8.2 1.6 pad_maximum_fusion
  9.8 0.7 all-gather.6.cloned.1.call-update
  10.6 0.7 all-gather.8.cloned.1.call-update
  11.9 0.7 reshape.123
  12.7 0.7 maximum_bitcast_fusion
  13.4 3.0 collective-permute-start
  16.4 1.2 broadcast_add_fusion
  17.8 0.7 constant_dynamic-update-slice_fusion.4
  18.5 6.4 %broadcast_select_fusion.left_ref.g_ref.gm_ref = bf16[2560,1024]{1,0:T(8,128)(2,1)} fusion(bf16[2560,1024]{1,0:T(8,128)(2,1)} %param.13, pred[2560]{0:T(1024)(128)(4,1)S(1)} %lt.79), kind=kLoop, calls=%fused_computation.1 | loop fusion | flops 2621440 | bytes 10488320 | tf_op jit(solution)/shard_map/jit(_where)/select_n | solution.py:709
  25.0 1.2 collective-permute-done.1
  26.2 1.5 collective-permute-start.2
  27.7 2.4 collective-permute-done.2
  30.1 1.6 collective-permute-start.3
  31.8 3.5 collective-permute-done.3
  35.3 2.0 collective-permute-start.4
  37.5 5.2 collective-permute-done.4
  44.4 0.7 reshape.115.bias_ref
  45.1 8.6 %norm_in.1.h_ref.left_ref = bf16[2560,1024]{1,0:T(8,128)(2,1)} custom-call(bf16[2560,1024]{1,0:T(8,128)(2,1)} %x_ref.7, f32[8,1024]{1,0:T(8,128)} %concatenate.52.vec_ref), custom_call_target="tpu_custom_call" | custom-call | flops 41943040 | bytes 10485760 | tf_op jit(solution)/shard_map/norm_in/pallas_call | solution.py:217
  54.3 37.1 %all-gather.4.cloned.1.call-done = bf16[2048,2048]{1,0:T(8,128)(2,1)} async-done(((bf16[64,2048]{1,0:T(8,128)(2,1)}), bf16[2048,2048]{1,0:T(8,128)(2,1)}) %all-gather.4.cloned.1.call-update) | async-done | bytes 8388624 | tf_op jit(solution)/shard_map/all_gather | solution.py:673
  91.4 22.0 %project.1.q_ref.k_ref.v_ref = bf16[2,2560,1536]{2,1,0:T(8,128)(2,1)} custom-call(bf16[2560,1024]{1,0:T(8,128)(2,1)} %norm_in.1.h_ref.left_ref, bf16[2,1024,2048]{2,1,0:T(8,128)(2,1)} %bitcast.48, f32[2,1,1536]{2,1,0:T(1,128)} %pad_maximum_fusion.5.bias_ref), custom_call_target="tpu_custom_call" | custom-call | flops 16106127360 | bytes 13631488 | tf_op jit(solution)/shard_map/project/pallas_call | solution.py:236
  113.4 32.6 %attend.1 = (bf16[2,2560,512]{2,1,0:T(8,128)(2,1)}, bf16[2,8,4,2,320,384]{5,4,3,2,1,0:T(8,128)(2,1)}, f32[2,2560,512]{2,1,0:T(8,128)}) custom-call(s32[8]{0:T(128)} %get-tuple-element.161.kept_ref, bf16[2,2560,1536]{2,1,0:T(8,128)(2,1)} %project.1.q_ref.k_ref.v_ref, bf16[2,2560,1536]{2,1,0:T(8,128)(2,1)} %project.1.q_ref.k_ref.v_ref, ...), custom_call_target="tpu_custom_call" | custom-call | flops 13421772800 | bytes 31457280 | tf_op jit(solution)/shard_map/attend/pallas_call | solution.py:74
  146.0 13.5 %mix.1 = (f32[2560,1024]{1,0:T(8,128)}, bf16[2560,1024]{1,0:T(8,128)(2,1)}) custom-call(bf16[2,2560,512]{2,1,0:T(8,128)(2,1)} %get-tuple-element.75.attn_ref.right_ref.o_ref, bf16[2,1024,2048]{2,1,0:T(8,128)(2,1)} %bitcast.49, bf16[2560,1024]{1,0:T(8,128)(2,1)} %x_ref.7, f32[8,1024]{1,0:T(8,128)} %concatenate.52.vec_ref), custom_call_target="tpu_custom_call" | custom-call | flops 5368709120 | bytes 10485760 | tf_op jit(solution)/shard_map/mix/pallas_call | solution.py:265
  159.5 10.6 %all-gather.6.cloned.1.call-done = bf16[2048,2048]{1,0:T(8,128)(2,1)} async-done(((bf16[64,2048]{1,0:T(8,128)(2,1)}), bf16[2048,2048]{1,0:T(8,128)(2,1)}) %all-gather.6.cloned.1.call-update) | async-done | bytes 8388624 | tf_op jit(solution)/shard_map/all_gather | solution.py:673
  170.0 45.9 %expand.1 = (bf16[2,2560,2048]{2,1,0:T(8,128)(2,1)}, bf16[2,2560,2048]{2,1,0:T(8,128)(2,1)}) custom-call(bf16[2560,1024]{1,0:T(8,128)(2,1)} %get-tuple-element.76.h_ref.left_ref, bf16[2,1024,2048]{2,1,0:T(8,128)(2,1)} %bitcast.63, f32[2,1,2048]{2,1,0:T(1,128)} %reshape.115.bias_ref), custom_call_target="tpu_custom_call" | custom-call | flops 32212254720 | bytes 13631488 | tf_op jit(solution)/shard_map/expand/pallas_call | solution.py:312
  215.9 29.8 %weight_grad.2 = bf16[2,1024,2304]{2,1,0:T(8,128)(2,1)} custom-call(bf16[2560,1024]{1,0:T(8,128)(2,1)} %broadcast_select_fusion.left_ref.g_ref.gm_ref, bf16[2,2560,2048]{2,1,0:T(8,128)(2,1)} %get-tuple-element.125.right_ref.act_ref), custom_call_target="tpu_custom_call" | custom-call | flops 21474836480 | bytes 26214400 | tf_op jit(solution)/shard_map/weight_grad/pallas_call | solution.py:383
  246.4 2.3 all-gather.8.cloned.1.call-done
  248.6 33.3 %expand_back.1 = (bf16[2,2560,2048]{2,1,0:T(8,128)(2,1)}, f32[2,1,2048]{2,1,0:T(1,128)}) custom-call(bf16[2560,1024]{1,0:T(8,128)(2,1)} %broadcast_select_fusion.left_ref.g_ref.gm_ref, bf16[2,1024,2048]{2,1,0:T(8,128)(2,1)} %bitcast.45, bf16[2,2560,2048]{2,1,0:T(8,128)(2,1)} %get-tuple-element.79.slope_ref), custom_call_target="tpu_custom_call" | custom-call | flops 21474836480 | bytes 41943040 | tf_op jit(solution)/shard_map/expand_back/pallas_call | solution.py:345
  281.9 18.6 %weight_grad_split.2 = (bf16[16,64,1024]{2,1,0:T(8,128)(2,1)}, bf16[16,64,1024]{2,1,0:T(8,128)(2,1)}) custom-call(s32[17]{0:T(128)} %pad_add_fusion.slot_ref, bf16[2560,1024]{1,0:T(8,128)(2,1)} %get-tuple-element.76.h_ref.left_ref, bf16[2,2560,2048]{2,1,0:T(8,128)(2,1)} %get-tuple-element.86.right_ref.g_ref), custom_call_target="tpu_custom_call" | custom-call | flops 10737418240 | bytes 26214400 | tf_op jit(solution)/shard_map/weight_grad_split/pallas_call | solution.py:453
  301.4 16.8 %weight_grad.3._ = bf16[2,1024,1536]{2,1,0:T(8,128)(2,1)} custom-call(bf16[2560,1024]{1,0:T(8,128)(2,1)} %get-tuple-element.76.h_ref.left_ref, bf16[2,2560,2048]{2,1,0:T(8,128)(2,1)} %get-tuple-element.86.right_ref.g_ref), custom_call_target="tpu_custom_call" | custom-call | flops 10737418240 | bytes 26214400 | tf_op jit(solution)/shard_map/weight_grad/pallas_call | solution.py:383
  318.2 1.0 add.163
  319.3 1.6 collective-permute-start.6
  320.8 40.2 %middle_back.1 = (f32[2560,1024]{1,0:T(8,128)}, bf16[2560,1024]{1,0:T(8,128)(2,1)}, bf16[2,2560,512]{2,1,0:T(8,128)(2,1)}, f32[8,1024]{1,0:T(8,128)}) custom-call(bf16[2,2560,2048]{2,1,0:T(8,128)(2,1)} %get-tuple-element.86.right_ref.g_ref, bf16[2,1024,2048]{2,1,0:T(8,128)(2,1)} %bitcast.64, f32[2560,1024]{1,0:T(8,128)} %get-tuple-element.87.mixed_ref, ...), custom_call_target="tpu_custom_call" | custom-call | flops 26843545600 | bytes 39845888 | tf_op jit(solution)/shard_map/middle_back/pallas_call | solution.py:496
  361.0 10.2 %weight_grad_into.1 = bf16[2,1024,1536]{2,1,0:T(8,128)(2,1)} custom-call(bf16[2560,1024]{1,0:T(8,128)(2,1)} %get-tuple-element.92.left_ref, bf16[2,2560,512]{2,1,0:T(8,128)(2,1)} %get-tuple-element.75.attn_ref.right_ref.o_ref, bf16[2,1024,1536]{2,1,0:T(8,128)(2,1)} %weight_grad.3._), custom_call_target="tpu_custom_call", output_to_operand_aliasing={{}: (2, {})} | custom-call | flops 5368709120 | bytes 10485760 | tf_op jit(solution)/shard_map/weight_grad_into/pallas_call | solution.py:404
  372.0 41.7 %attend_back.1 = (bf16[2,2560,1536]{2,1,0:T(8,128)(2,1)}, f32[2,2,512]{2,1,0:T(2,128)}) custom-call(bf16[2,2560,1536]{2,1,0:T(8,128)(2,1)} %project.1.q_ref.k_ref.v_ref, bf16[2,2560,1536]{2,1,0:T(8,128)(2,1)} %project.1.q_ref.k_ref.v_ref, bf16[2,2560,1536]{2,1,0:T(8,128)(2,1)} %project.1.q_ref.k_ref.v_ref, bf16[2,2560,512]{2,1,0:T(8,128)(2,1)} %get-tuple-element.94.g_ref, ...), custom_call_target="tpu_custom_call" | custom-call | flops 20132659200 | bytes 62914560 | tf_op jit(solution)/shard_map/attend_back/pallas_call | solution.py:137
  413.8 1.8 collective-permute-start.8
  415.7 25.1 %weight_grad_split.3 = (bf16[16,64,768]{2,1,0:T(8,128)(2,1)}, bf16[16,64,768]{2,1,0:T(8,128)(2,1)}, bf16[16,64,768]{2,1,0:T(8,128)(2,1)}, bf16[16,64,768]{2,1,0:T(8,128)(2,1)}) custom-call(s32[33]{0:T(128)} %pad_add_fusion.1.slot_ref, bf16[2560,1024]{1,0:T(8,128)(2,1)} %norm_in.1.h_ref.left_ref, bf16[2,2560,1536]{2,1,0:T(8,128)(2,1)} %get-tuple-element.109.right_ref.g_ref), custom_call_target="tpu_custom_call" | custom-call | flops 16106127360 | bytes 20971520 | tf_op jit(solution)/shard_map/weight_grad_split/pallas_call | solution.py:453
  442.1 0.9 collective-permute-start.21
  442.9 16.9 %input_back.2 = (f32[2560,1024]{1,0:T(8,128)}, f32[12,1024]{1,0:T(8,128)}) custom-call(bf16[2,2560,1536]{2,1,0:T(8,128)(2,1)} %get-tuple-element.109.right_ref.g_ref, bf16[2,1024,2048]{2,1,0:T(8,128)(2,1)} %bitcast.51, bf16[2560,1024]{1,0:T(8,128)(2,1)} %x_ref.7, f32[2560,1024]{1,0:T(8,128)} %get-tuple-element.110.gmixed_ref, ...), custom_call_target="tpu_custom_call" | custom-call | flops 8053063680 | bytes 8388608 | tf_op jit(solution)/shard_map/input_back/pallas_call | solution.py:539
  459.8 0.8 convert_bitcast_fusion
  462.0 1.4 collective-permute-start.12
  463.3 0.7 collective-permute-start.11
  464.0 16.5 %input_back.3 = (f32[2560,1024]{1,0:T(8,128)}, f32[12,1024]{1,0:T(8,128)}) custom-call(bf16[2,2560,1536]{2,1,0:T(8,128)(2,1)} %get-tuple-element.109.right_ref.g_ref, bf16[2,1024,2048]{2,1,0:T(8,128)(2,1)} %bitcast.52, bf16[2560,1024]{1,0:T(8,128)(2,1)} %x_ref.7, f32[2560,1024]{1,0:T(8,128)} %get-tuple-element.110.gmixed_ref, ...), custom_call_target="tpu_custom_call", output_to_operand_aliasing={{0}: (6, {})} | custom-call | flops 8053063680 | bytes 8388608 | tf_op jit(solution)/shard_map/input_back/pallas_call | solution.py:539
  480.6 11.8 %collective-permute-done.12 = bf16[8,64,768]{2,1,0:T(8,128)(2,1)S(1)} collective-permute-done((bf16[8,64,768]{2,1,0:T(8,128)(2,1)S(1)}, bf16[8,64,768]{2,1,0:T(8,128)(2,1)S(1)}, u32[]{:S(2)}, u32[]{:S(2)}) %collective-permute-start.12) | collective-permute-done | bytes 786464 | tf_op jit(solution)/shard_map/ppermute | solution.py:596
  492.4 1.0 collective-permute-done.11
  493.7 0.7 collective-permute-start.15
  494.5 1.5 collective-permute-start.14
  496.0 17.9 %shrink.2.refs_0_ = bf16[2560,1024]{1,0:T(8,128)(2,1)} custom-call(s32[8]{0:T(128)} %get-tuple-element.161.kept_ref, bf16[2,2560,2048]{2,1,0:T(8,128)(2,1)} %get-tuple-element.125.right_ref.act_ref, bf16[2,1024,2048]{2,1,0:T(8,128)(2,1)} %bitcast.46, f32[2560,1024]{1,0:T(8,128)} %get-tuple-element.87.mixed_ref, f32[8,1024]{1,0:T(8,128)} %concatenate.52.vec_ref), custom_call_target="tpu_custom_call" | custom-call | flops 10737418240 | bytes 8388608 | tf_op jit(solution)/shard_map/shrink/pallas_call | solution.py:576
  513.9 0.7 collective-permute-start.16
  514.8 1.8 collective-permute-start.18
  516.6 1.2 collective-permute-start.17
  517.8 18.0 %shrink.3 = bf16[2560,1024]{1,0:T(8,128)(2,1)} custom-call(s32[8]{0:T(128)} %get-tuple-element.161.kept_ref, bf16[2,2560,2048]{2,1,0:T(8,128)(2,1)} %get-tuple-element.125.right_ref.act_ref, bf16[2,1024,2048]{2,1,0:T(8,128)(2,1)} %bitcast.47, f32[2560,1024]{1,0:T(8,128)} %get-tuple-element.87.mixed_ref, ...), custom_call_target="tpu_custom_call", output_to_operand_aliasing={{}: (5, {})} | custom-call | flops 10737418240 | bytes 8388608 | tf_op jit(solution)/shard_map/shrink/pallas_call | solution.py:576
  535.7 1.5 collective-permute-done.17
  537.3 0.8 collective-permute-start.22
  538.5 3.1 collective-permute-done.22
  541.6 0.9 collective-permute-start.23
  542.6 1.8 collective-permute-start.19
  544.4 3.7 collective-permute-done.23
  548.3 0.7 collective-permute-done.19
  549.4 0.9 copy.38
  550.2 2.2 collective-permute-done.24
  554.9 0.9 slice.170
  555.8 0.8 maximum_convert_fusion
  556.7 1.5 convert_bitcast_fusion.1
  (122 shorter events, 12.3 us)
Async XLA Ops:
  7.2 84.2 %all-gather.4.cloned.1.call-start = ((), (), s32[]{:S(2)}) async-start(), calls=%async_computation.2 | async-start | bytes 8650752 | tf_op jit(solution)/shard_map/all_gather | solution.py:673
  9.8 160.3 %all-gather.6.cloned.1.call-start = ((), (), s32[]{:S(2)}) async-start(), calls=%async_computation.3 | async-start | bytes 8650752 | tf_op jit(solution)/shard_map/all_gather | solution.py:673
  10.5 238.1 %all-gather.8.cloned.1.call-start = ((), (), s32[]{:S(2)}) async-start(), calls=%async_computation.4 | async-start | bytes 8650752 | tf_op jit(solution)/shard_map/all_gather | solution.py:673
  11.2 404.4 %reduce-scatter.3.cloned.1.call-start = ((), (), s32[]{:S(2)}) async-start(), calls=%async_computation.5 | async-start | bytes 9732096 | tf_op jit(solution)/shard_map/reduce_scatter | solution.py:679
  13.4 11.5 %collective-permute-start = (f32[1,12,32]{2,1,0:T(8,128)S(1)}, f32[1,12,32]{2,1,0:T(8,128)S(1)}, u32[]{:S(2)}, u32[]{:S(2)}) collective-permute-start(f32[1,12,32]{2,1,0:T(8,128)S(1)} %maximum_bitcast_fusion), channel_id=1, source_target_pairs={{0,1},{1,0},{2,3},{3,2},{4,5},{5,4},{6,7},{7,6},{8,9},{9,8},{10,11... | collective-permute-start | bytes 4616 | tf_op jit(solution)/shard_map/ppermute | solution.py:596
  24.9 1.2 collective-permute-start.1
  26.2 3.9 collective-permute-start.2
  30.1 5.2 collective-permute-start.3
  35.3 7.3 %collective-permute-start.4 = (f32[16,12,32]{2,1,0:T(8,128)S(1)}, f32[16,12,32]{2,1,0:T(8,128)S(1)}, u32[]{:S(2)}, u32[]{:S(2)}) collective-permute-start(f32[16,12,32]{2,1,0:T(8,128)S(1)} %get-tuple-element.162), channel_id=1, source_target_pairs={{0,16},{2,18},{4,20},{6,22},{8,24},{10,26},{12,28},{14,30},{16,0},... | collective-permute-start | bytes 73736 | tf_op jit(solution)/shard_map/ppermute | solution.py:596
  245.7 309.2 %reduce-scatter.5.cloned.1.call-start = ((), (), s32[]{:S(2)}) async-start(), calls=%async_computation.6 | async-start | bytes 6488064 | tf_op jit(solution)/shard_map/reduce_scatter | solution.py:679
  281.9 19.4 %copy-start.5 = (f32[2,1,2048]{2,1,0:T(1,128)S(1)}, f32[2,1,2048]{2,1,0:T(1,128)}, u32[]{:S(2)}) copy-start(f32[2,1,2048]{2,1,0:T(1,128)} %get-tuple-element.113) | copy-start | bytes 49156
  300.5 17.8 %collective-permute-start.5 = (bf16[16,64,1024]{2,1,0:T(8,128)(2,1)}, bf16[16,64,1024]{2,1,0:T(8,128)(2,1)S(1)}, u32[]{:S(2)}, u32[]{:S(2)}) collective-permute-start(bf16[16,64,1024]{2,1,0:T(8,128)(2,1)} %get-tuple-element.85), channel_id=1, source_target_pairs={{0,2},{2,0},{4,6},{6,4},{8,10},{10,8},{12,14},{14,12},{16,18},{18,... | collective-permute-start | bytes 6291464 | tf_op jit(solution)/shard_map/ppermute | solution.py:596
  301.4 16.8 %copy-start = (bf16[16,64,1024]{2,1,0:T(8,128)(2,1)S(1)}, bf16[16,64,1024]{2,1,0:T(8,128)(2,1)}, u32[]{:S(2)}) copy-start(bf16[16,64,1024]{2,1,0:T(8,128)(2,1)} %get-tuple-element.90) | copy-start | bytes 6291460
  319.3 41.8 %collective-permute-start.6 = (bf16[8,64,1024]{2,1,0:T(8,128)(2,1)S(1)}, bf16[8,64,1024]{2,1,0:T(8,128)(2,1)S(1)}, u32[]{:S(2)}, u32[]{:S(2)}) collective-permute-start(bf16[8,64,1024]{2,1,0:T(8,128)(2,1)S(1)} %slice.147), channel_id=1, source_target_pairs={{0,1},{1,0},{2,3},{3,2},{4,5},{5,4},{6,7},{7,6},{8,9},{9,8},{10,11... | collective-permute-start | bytes 3145736 | tf_op jit(solution)/shard_map/ppermute | solution.py:596
  371.4 42.3 %collective-permute-start.7 = (bf16[4,64,1024]{2,1,0:T(8,128)(2,1)S(1)}, bf16[4,64,1024]{2,1,0:T(8,128)(2,1)S(1)}, u32[]{:S(2)}, u32[]{:S(2)}) collective-permute-start(bf16[4,64,1024]{2,1,0:T(8,128)(2,1)S(1)} %slice.149), channel_id=1, source_target_pairs={{0,4},{2,6},{4,0},{6,2},{8,12},{10,14},{12,8},{14,10},{16,20},{18,... | collective-permute-start | bytes 1572872 | tf_op jit(solution)/shard_map/ppermute | solution.py:596
  413.8 28.2 %collective-permute-start.8 = (bf16[2,64,1024]{2,1,0:T(8,128)(2,1)S(1)}, bf16[2,64,1024]{2,1,0:T(8,128)(2,1)S(1)}, u32[]{:S(2)}, u32[]{:S(2)}) collective-permute-start(bf16[2,64,1024]{2,1,0:T(8,128)(2,1)S(1)} %slice.152), channel_id=1, source_target_pairs={{0,16},{2,18},{4,20},{6,22},{8,24},{10,26},{12,28},{14,30},{16,0},... | collective-permute-start | bytes 786440 | tf_op jit(solution)/shard_map/ppermute | solution.py:596
  415.7 25.7 %copy-start.4 = (f32[8,1024]{1,0:T(8,128)S(1)}, f32[8,1024]{1,0:T(8,128)}, u32[]{:S(2)}) copy-start(f32[8,1024]{1,0:T(8,128)} %get-tuple-element.111) | copy-start | bytes 98308
  415.7 25.7 %copy-start.6 = (f32[2,2,512]{2,1,0:T(2,128)S(1)}, f32[2,2,512]{2,1,0:T(2,128)}, u32[]{:S(2)}) copy-start(f32[2,2,512]{2,1,0:T(2,128)} %get-tuple-element.112) | copy-start | bytes 24580
  440.9 19.8 %collective-permute-start.9 = (bf16[16,64,768]{2,1,0:T(8,128)(2,1)}, bf16[16,64,768]{2,1,0:T(8,128)(2,1)S(1)}, u32[]{:S(2)}, u32[]{:S(2)}) collective-permute-start(bf16[16,64,768]{2,1,0:T(8,128)(2,1)} %get-tuple-element.115), channel_id=1, source_target_pairs={{0,2},{2,0},{4,6},{6,4},{8,10},{10,8},{12,14},{14,12},{16,18},{18,... | collective-permute-start | bytes 4718600 | tf_op jit(solution)/shard_map/ppermute | solution.py:596
  440.9 19.8 %collective-permute-start.10 = (bf16[16,64,768]{2,1,0:T(8,128)(2,1)}, bf16[16,64,768]{2,1,0:T(8,128)(2,1)S(1)}, u32[]{:S(2)}, u32[]{:S(2)}) collective-permute-start(bf16[16,64,768]{2,1,0:T(8,128)(2,1)} %get-tuple-element.116), channel_id=1, source_target_pairs={{0,2},{2,0},{4,6},{6,4},{8,10},{10,8},{12,14},{14,12},{16,18},{18,... | collective-permute-start | bytes 4718600 | tf_op jit(solution)/shard_map/ppermute | solution.py:596
  442.1 21.9 %collective-permute-start.21 = (bf16[1,64,1024]{2,1,0:T(8,128)(2,1)S(1)}, bf16[1,64,1024]{2,1,0:T(8,128)(2,1)S(1)}, u32[]{:S(2)}, u32[]{:S(2)}) collective-permute-start(bf16[1,64,1024]{2,1,0:T(8,128)(2,1)S(1)} %slice.173), channel_id=1, source_target_pairs={{0,8},{2,10},{4,12},{6,14},{8,0},{10,2},{12,4},{14,6},{16,24},{18,... | collective-permute-start | bytes 393224 | tf_op jit(solution)/shard_map/ppermute | solution.py:596
  442.9 16.9 %slice-start = ((bf16[64,2304]{1,0:T(8,128)(2,1)}), bf16[64,2048]{1,0:T(8,128)(2,1)S(1)}, s32[]{:S(2)}) async-start(bf16[64,2304]{1,0:T(8,128)(2,1)} %reduce-scatter.3.cloned.1.call-done), calls=%async_computation.7 | async-start | bytes 524288 | tf_op jit(solution)/shard_map/slice | solution.py:726
  442.9 17.7 %copy-start.2 = (bf16[16,64,768]{2,1,0:T(8,128)(2,1)S(1)}, bf16[16,64,768]{2,1,0:T(8,128)(2,1)}, u32[]{:S(2)}) copy-start(bf16[16,64,768]{2,1,0:T(8,128)(2,1)} %get-tuple-element.121) | copy-start | bytes 4718596
  459.8 1.6 copy-start.1
  462.0 30.5 %collective-permute-start.12 = (bf16[8,64,768]{2,1,0:T(8,128)(2,1)S(1)}, bf16[8,64,768]{2,1,0:T(8,128)(2,1)S(1)}, u32[]{:S(2)}, u32[]{:S(2)}) collective-permute-start(bf16[8,64,768]{2,1,0:T(8,128)(2,1)S(1)} %slice.154), channel_id=1, source_target_pairs={{0,4},{2,6},{4,0},{6,2},{8,12},{10,14},{12,8},{14,10},{16,20},{18,... | collective-permute-start | bytes 2359304 | tf_op jit(solution)/shard_map/ppermute | solution.py:596
  463.3 30.1 %collective-permute-start.11 = (bf16[8,64,768]{2,1,0:T(8,128)(2,1)S(1)}, bf16[8,64,768]{2,1,0:T(8,128)(2,1)S(1)}, u32[]{:S(2)}, u32[]{:S(2)}) collective-permute-start(bf16[8,64,768]{2,1,0:T(8,128)(2,1)S(1)} %slice.153), channel_id=1, source_target_pairs={{0,1},{1,0},{2,3},{3,2},{4,5},{5,4},{6,7},{7,6},{8,9},{9,8},{10,11... | collective-permute-start | bytes 2359304 | tf_op jit(solution)/shard_map/ppermute | solution.py:596
  480.6 33.3 %collective-permute-start.13 = (f32[12,1024]{1,0:T(8,128)}, f32[12,1024]{1,0:T(8,128)S(1)}, u32[]{:S(2)}, u32[]{:S(2)}) collective-permute-start(f32[12,1024]{1,0:T(8,128)} %get-tuple-element.119), channel_id=1, source_target_pairs={{0,2},{2,0},{4,6},{6,4},{8,10},{10,8},{12,14},{14,12},{16,18},{18,... | collective-permute-start | bytes 147464 | tf_op jit(solution)/shard_map/ppermute | solution.py:596
  493.7 20.2 %copy-start.3 = (f32[12,1024]{1,0:T(8,128)S(1)}, f32[12,1024]{1,0:T(8,128)}, u32[]{:S(2)}) copy-start(f32[12,1024]{1,0:T(8,128)} %get-tuple-element.119) | copy-start | bytes 147460
  493.7 20.2 %collective-permute-start.15 = (bf16[4,64,768]{2,1,0:T(8,128)(2,1)S(1)}, bf16[4,64,768]{2,1,0:T(8,128)(2,1)S(1)}, u32[]{:S(2)}, u32[]{:S(2)}) collective-permute-start(bf16[4,64,768]{2,1,0:T(8,128)(2,1)S(1)} %slice.158), channel_id=1, source_target_pairs={{0,1},{1,0},{2,3},{3,2},{4,5},{5,4},{6,7},{7,6},{8,9},{9,8},{10,11... | collective-permute-start | bytes 1179656 | tf_op jit(solution)/shard_map/ppermute | solution.py:596
  494.5 19.4 %collective-permute-start.14 = (bf16[4,64,768]{2,1,0:T(8,128)(2,1)S(1)}, bf16[4,64,768]{2,1,0:T(8,128)(2,1)S(1)}, u32[]{:S(2)}, u32[]{:S(2)}) collective-permute-start(bf16[4,64,768]{2,1,0:T(8,128)(2,1)S(1)} %slice.156), channel_id=1, source_target_pairs={{0,4},{2,6},{4,0},{6,2},{8,12},{10,14},{12,8},{14,10},{16,20},{18,... | collective-permute-start | bytes 1179656 | tf_op jit(solution)/shard_map/ppermute | solution.py:596
  513.9 21.8 %collective-permute-start.16 = (f32[12,1024]{1,0:T(8,128)S(1)}, f32[12,1024]{1,0:T(8,128)S(1)}, u32[]{:S(2)}, u32[]{:S(2)}) collective-permute-start(f32[12,1024]{1,0:T(8,128)S(1)} %add.173), channel_id=1, source_target_pairs={{0,1},{1,0},{2,3},{3,2},{4,5},{5,4},{6,7},{7,6},{8,9},{9,8},{10,11... | collective-permute-start | bytes 147464 | tf_op jit(solution)/shard_map/ppermute | solution.py:596
  514.8 21.0 %collective-permute-start.18 = (bf16[2,64,768]{2,1,0:T(8,128)(2,1)S(1)}, bf16[2,64,768]{2,1,0:T(8,128)(2,1)S(1)}, u32[]{:S(2)}, u32[]{:S(2)}) collective-permute-start(bf16[2,64,768]{2,1,0:T(8,128)(2,1)S(1)} %slice.162), channel_id=1, source_target_pairs={{0,16},{2,18},{4,20},{6,22},{8,24},{10,26},{12,28},{14,30},{16,0},... | collective-permute-start | bytes 589832 | tf_op jit(solution)/shard_map/ppermute | solution.py:596
  516.6 20.7 %collective-permute-start.17 = (bf16[2,64,768]{2,1,0:T(8,128)(2,1)S(1)}, bf16[2,64,768]{2,1,0:T(8,128)(2,1)S(1)}, u32[]{:S(2)}, u32[]{:S(2)}) collective-permute-start(bf16[2,64,768]{2,1,0:T(8,128)(2,1)S(1)} %slice.160), channel_id=1, source_target_pairs={{0,16},{2,18},{4,20},{6,22},{8,24},{10,26},{12,28},{14,30},{16,0},... | collective-permute-start | bytes 589832 | tf_op jit(solution)/shard_map/ppermute | solution.py:596
  537.3 4.3 collective-permute-start.22
  538.2 10.1 %collective-permute-start.20 = (bf16[1,64,768]{2,1,0:T(8,128)(2,1)S(1)}, bf16[1,64,768]{2,1,0:T(8,128)(2,1)S(1)}, u32[]{:S(2)}, u32[]{:S(2)}) collective-permute-start(bf16[1,64,768]{2,1,0:T(8,128)(2,1)S(1)} %slice.168), channel_id=1, source_target_pairs={{0,8},{2,10},{4,12},{6,14},{8,0},{10,2},{12,4},{14,6},{16,24},{18,... | collective-permute-start | bytes 294920 | tf_op jit(solution)/shard_map/ppermute | solution.py:596
  541.6 6.5 %collective-permute-start.23 = (f32[12,1024]{1,0:T(8,128)S(1)}, f32[12,1024]{1,0:T(8,128)S(1)}, u32[]{:S(2)}, u32[]{:S(2)}) collective-permute-start(f32[12,1024]{1,0:T(8,128)S(1)} %add.183), channel_id=1, source_target_pairs={{0,16},{2,18},{4,20},{6,22},{8,24},{10,26},{12,28},{14,30},{16,0},... | collective-permute-start | bytes 147464 | tf_op jit(solution)/shard_map/ppermute | solution.py:596
  542.6 6.5 %collective-permute-start.19 = (bf16[1,64,768]{2,1,0:T(8,128)(2,1)S(1)}, bf16[1,64,768]{2,1,0:T(8,128)(2,1)S(1)}, u32[]{:S(2)}, u32[]{:S(2)}) collective-permute-start(bf16[1,64,768]{2,1,0:T(8,128)(2,1)S(1)} %slice.165), channel_id=1, source_target_pairs={{0,8},{2,10},{4,12},{6,14},{8,0},{10,2},{12,4},{14,6},{16,24},{18,... | collective-permute-start | bytes 294920 | tf_op jit(solution)/shard_map/ppermute | solution.py:596
  548.1 4.3 collective-permute-start.24
Sparse Core Ops, SparseCore 0:
  11.4 79.9 all-gather.3
  94.3 75.6 all-gather.5
  172.9 75.6 all-gather.7
  254.4 143.3 reduce-scatter.2
  415.8 134.3 reduce-scatter.4

commit v4 on v3

--- a/solution.py
+++ b/solution.py
@@ -124,7 +124,8 @@
             start = which * width + LANES * pair
             out_ref[0, :, start : start + LANES] = value
         bias_ref[0, 0:1, cols] += jnp.sum(grad_query.astype(f32), axis=0, keepdims=True)
-        bias_ref[0, 1:2, cols] += jnp.sum(grad_value.astype(f32), axis=0, keepdims=True)
+        bias_ref[0, 1:2, cols] += jnp.sum(grad_key.astype(f32), axis=0, keepdims=True)
+        bias_ref[0, 2:3, cols] += jnp.sum(grad_value.astype(f32), axis=0, keepdims=True)
 
 
 def attend_back(qkv, grad, attn, expo, inverse):
@@ -140,11 +141,11 @@
         in_specs=[part(0), part(1), part(2), part(0), part(0), probs, part(0)],
         out_specs=[
             pl.BlockSpec((1, SEQ, width), lambda t, i: (t, i, 0)),
-            pl.BlockSpec((1, 2, cols), lambda t, i: (t, 0, 0)),
+            pl.BlockSpec((1, 3, cols), lambda t, i: (t, 0, 0)),
         ],
         out_shape=[
             jax.ShapeDtypeStruct((shards, rows, width), bf16),
-            jax.ShapeDtypeStruct((shards, 2, cols), f32),
+            jax.ShapeDtypeStruct((shards, 3, cols), f32),
         ],
         name="attend_back",
         cost_estimate=cost(rows * cols * shards * SEQ * 24, qkv, qkv, expo),
@@ -268,7 +269,7 @@
         (rows // size,),
         [
             pl.BlockSpec((shards, size, cols), lambda i: (0, i, 0)),
-            fixed((shards, width, cols), 0, 0, 3),
+            fixed(weights.shape, 0, 0, 0),
             pl.BlockSpec((size, width), step),
             fixed(vectors.shape, 0, 0),
         ],
@@ -375,13 +376,13 @@
             out_ref[0, :, out_ref.shape[2] - fill :] = spare
 
 
-def weight_grad(left, right, used, spare, fill):
+def weight_grad(left, right, spare):
     rows, width = left.shape
-    shards = right.shape[0]
+    shards, _, used = right.shape
     chunk = min(512, used)
     block = (1, width, used + spare)
     return call(
-        functools.partial(weight_grad_kernel, chunk=chunk, fill=spare if fill else 0),
+        functools.partial(weight_grad_kernel, chunk=chunk, fill=spare),
         "weight_grad",
         (shards, used // chunk),
         [
@@ -393,39 +394,31 @@
     )(left, right)[0]
 
 
-def weight_grad_into_kernel(left_ref, right_ref, _, out_ref):
-    out_ref[0] = dot_rows(left_ref[...], right_ref[0]).astype(bf16)
-
-
-def weight_grad_into(left, right, out):
-    rows, width = left.shape
-    shards, _, cols = right.shape
-    place = out.shape[2] // cols - 1
-    return call(
-        weight_grad_into_kernel,
-        "weight_grad_into",
-        (shards,),
-        [
-            fixed((rows, width), 0, 0),
-            pl.BlockSpec((1, rows, cols), lambda t: (t, 0, 0)),
-            pl.BlockSpec(memory_space=pl.ANY),
-        ],
-        [((1, width, cols), lambda t: (t, 0, place), out.shape, bf16)],
-        aliases={2: 0},
-        estimate=cost(2 * rows * width * cols * shards, left, right),
-    )(left, right, out)[0]
-
-
-def weight_grad_split_kernel(slot_ref, left_ref, right_ref, *out_refs, per_chain):
+def weight_grad_split_kernel(slot_ref, left_ref, right_ref, *refs, per_chain, chains):
     which, shard = pl.program_id(0), pl.program_id(1)
-    grad = dot_rows(left_ref[...], right_ref[0]).astype(bf16)
-    pairs = grad.shape[0] // (2 * out_refs[0].shape[1])
+    grad = dot_rows(left_ref[...], right_ref[0])
+    if len(refs) > 2 * chains:
+        w_ref, total_ref, product_ref, sum_ref = refs[0], refs[1], refs[-2], refs[-1]
+
+        @pl.when((which == 0) & (shard == 0))
+        def _():
+            product_ref[...] = jnp.zeros_like(product_ref)
+            sum_ref[...] = jnp.zeros_like(sum_ref)
+
+        for start in range(0, grad.shape[1], LANES):
+            part = slice(start, start + LANES)
+            weights = w_ref[0, :, part].astype(f32)
+            product_ref[...] += weights * grad[:, part]
+            sum_ref[...] += weights * total_ref[0, :, part]
+        refs = refs[2:-2]
+    grad = grad.astype(bf16)
+    pairs = grad.shape[0] // (2 * refs[0].shape[1])
     second = slot_ref[slot_ref.shape[0] - 1] == 1
-    for chain in range(len(out_refs) // 2):
+    for chain in range(chains):
 
         @pl.when(which // per_chain == chain)
         def _():
-            near_ref, far_ref = out_refs[2 * chain : 2 * chain + 2]
+            near_ref, far_ref = refs[2 * chain : 2 * chain + 2]
             part = near_ref.shape[1]
             base = chain * near_ref.shape[0] + shard * pairs
             for pair in range(pairs):
@@ -436,10 +429,11 @@
                 far_ref[slot] = jnp.where(second, low, high)
 
 
-def weight_grad_split(left, right, first, share, tables, second):
+def weight_grad_split(left, right, tables, second, weights=None, total=None):
     rows, width = left.shape
-    shards, _, _ = right.shape
+    shards, _, cols = right.shape
     chains = len(tables)
+    share = cols // chains
     half = tables[0].shape[0]
     part = width // (2 * half // shards)
     chunk = share if share <= 1024 else 512
@@ -450,19 +444,29 @@
         (half, part, share),
         bf16,
     )
+    outs = [out(chain) for chain in range(chains) for _ in range(2)]
+    more_specs, more = [], []
+    if weights is not None:
+        more = [weights, total]
+        more_specs = [
+            pl.BlockSpec((1, width, chunk), lambda n, t, s: (t, 0, n)),
+            pl.BlockSpec((1, 1, chunk), lambda n, t, s: (t, 0, n)),
+        ]
+        outs = outs + [((width, LANES), lambda n, t, s: (0, 0), (width, LANES), f32)] * 2
     parts = call(
-        functools.partial(weight_grad_split_kernel, per_chain=per_chain),
+        functools.partial(weight_grad_split_kernel, per_chain=per_chain, chains=chains),
         "weight_grad_split",
         (chains * per_chain, shards),
         [
             fixed((rows, width), 0, 0),
-            pl.BlockSpec((1, rows, chunk), lambda n, t, s: (t, 0, first // chunk + n)),
-        ],
-        [out(chain) for chain in range(chains) for _ in range(2)],
+            pl.BlockSpec((1, rows, chunk), lambda n, t, s: (t, 0, n)),
+        ]
+        + more_specs,
+        outs,
         prefetch=1,
-        estimate=cost(2 * rows * width * share * chains * shards, left, right),
-    )(jnp.concatenate(list(tables) + [second[None]]), left, right)
-    return [(parts[2 * chain], parts[2 * chain + 1]) for chain in range(chains)]
+        estimate=cost(2 * rows * width * cols * shards, left, right),
+    )(jnp.concatenate(list(tables) + [second[None]]), left, right, *more)
+    return [(parts[2 * chain], parts[2 * chain + 1]) for chain in range(chains)], parts[2 * chains :]
 
 
 def middle_back_kernel(
@@ -490,7 +494,7 @@
 def middle_back(grad_pre, up, mixed, grad_m, vectors, weights):
     shards, rows, cols = grad_pre.shape
     width = mixed.shape[1]
-    heads = weights.shape[2] // 4
+    heads = weights.shape[2]
     step = lambda i: (i, 0)
     wide = pl.BlockSpec((SEQ, width), step)
     return call(
@@ -503,7 +507,7 @@
             wide,
             wide,
             fixed(vectors.shape, 0, 0),
-            fixed((shards, width, heads), 0, 0, 3),
+            fixed(weights.shape, 0, 0, 0),
         ],
         [
             ((SEQ, width), step, (rows, width), f32),
@@ -515,23 +519,16 @@
     )(grad_pre, up, mixed, grad_m, vectors, weights)
 
 
-def input_back_kernel(g_ref, w_ref, x_ref, gmixed_ref, vec_ref, before_ref, *refs):
-    out_ref, sums_ref = refs[-2:]
-
-    @pl.when(pl.program_id(0) == 0)
-    def _():
-        sums_ref[...] = before_ref[...]
-
+def input_back_kernel(g_ref, w_ref, x_ref, gmixed_ref, vec_ref, *refs):
+    out_ref = refs[-1]
     grad_h = dot_flip(g_ref[0], w_ref[0])
     for shard in range(1, g_ref.shape[0]):
         grad_h += dot_flip(g_ref[shard], w_ref[shard])
     normed, inverse = norm_parts(x_ref[...].astype(f32))
     out_ref[...] = gmixed_ref[...] + norm_back(grad_h * row(vec_ref, GAIN1), normed, inverse)
-    for index, value in ((0, grad_h * normed), (2, grad_h)):
-        sums_ref[index : index + 1, :] += jnp.sum(value, axis=0, keepdims=True)
-
-
-def input_back(first, count, grad_heads, weights, tokens, grad_mixed, vectors, sums, *out):
+
+
+def input_back(first, count, grad_heads, weights, tokens, grad_mixed, vectors, *out):
     shards, rows, cols = grad_heads.shape
     width = tokens.shape[1]
     step = lambda i: (first + i, 0)
@@ -542,20 +539,16 @@
         (count,),
         [
             pl.BlockSpec((shards, SEQ, cols), lambda i: (0, first + i, 0)),
-            fixed((shards, width, cols), 0, 0, 0),
+            fixed(weights.shape, 0, 0, 0),
             wide,
             wide,
             fixed(vectors.shape, 0, 0),
-            fixed(sums.shape, 0, 0),
         ]
         + [pl.BlockSpec(memory_space=pl.ANY)] * len(out),
-        [
-            ((SEQ, width), step, (rows, width), f32),
-            (sums.shape, lambda i: (0, 0), sums.shape, f32),
-        ],
-        aliases={6: 0} if out else None,
+        [((SEQ, width), step, (rows, width), f32)],
+        aliases={5: 0} if out else None,
         estimate=cost(2 * count * SEQ * width * cols * shards, weights),
-    )(grad_heads, weights, tokens, grad_mixed, vectors, sums, *out)
+    )(grad_heads, weights, tokens, grad_mixed, vectors, *out)[0]
 
 
 def shrink_kernel(kept_ref, act_ref, w_ref, mixed_ref, vec_ref, *refs, first):
@@ -600,15 +593,19 @@
     return [1 << power for power in range(lax.axis_size(axis).bit_length() - 1)]
 
 
-def flip_gather(part):
+def flip_gather(part, order):
+    dp, shards = lax.axis_size("dp"), lax.axis_size("tensor")
     values = part[None]
-    for axis in ("tensor", "dp"):
-        for bit in bits_of(axis):
-            values = jnp.concatenate([values, swap(values, axis, bit)], 0)
-    here = lax.axis_index("dp") * lax.axis_size("tensor") + lax.axis_index("tensor")
-    places = jnp.arange(values.shape[0], dtype=jnp.int32) ^ here.astype(jnp.int32)
-    values = jnp.take(values, places, axis=0)
-    return values.reshape((lax.axis_size("dp"), lax.axis_size("tensor")) + part.shape)
+    index = jnp.arange(shards * dp, dtype=jnp.int32)
+    apart = {
+        "tensor": (index // dp) ^ lax.axis_index("tensor").astype(jnp.int32),
+        "dp": (index % dp) ^ lax.axis_index("dp").astype(jnp.int32),
+    }
+    place = jnp.zeros_like(index)
+    for axis, bit in order:
+        place += jnp.where((apart[axis] & bit) != 0, values.shape[0], 0)
+        values = jnp.concatenate([values, swap(values, axis, bit)], 0)
+    return jnp.take(values, place, axis=0)
 
 
 def slot_table(order):
@@ -688,19 +685,25 @@
     own = ln_gain.shape[1]
     barrier = lax.optimization_barrier
 
-    full_heads = gather(jnp.concatenate([w_qkv.transpose(1, 0, 2).reshape(part, 3 * cols), w_out.T], 1))
+    core, along_x = [("dp", 1)], [("tensor", bit) for bit in bits_of("tensor")[::-1]]
+    low, high = [("dp", 2)], [("dp", bit) for bit in bits_of("dp")[::-1] if bit > 2]
+    order_x, order_low = core + along_x + low + high, core + low + along_x + high
+
+    full_qkv = gather(w_qkv.transpose(1, 0, 2).reshape(part, 3 * cols))
     full_up = gather(w_up)
     full_down = gather(w_down.T)
 
     small = jnp.concatenate(
         [ln_gain, shift, qv_bias.astype(f32), up_bias.astype(f32).reshape(-1, own)], 0
     )
-    small = flip_gather(small)
-    vectors = small[:, :, :6].transpose(2, 0, 1, 3).reshape(6, width)
+    small = flip_gather(small, high + low + along_x + core)
+    small = small.reshape((shards, dp) + small.shape[1:])
+    vectors = small[:, :, :6].transpose(2, 1, 0, 3).reshape(6, width)
     vectors = jnp.concatenate([vectors, jnp.zeros((2, width), f32)], 0)
-    bias_qv = small[:, :, 6:8].transpose(1, 2, 0, 3).reshape(shards, 2, cols)
-    bias_up = small[:, :, 8:].transpose(1, 0, 2, 3).reshape(shards, 1, -1)
+    bias_qv = small[:, :, 6:8].transpose(0, 2, 1, 3).reshape(shards, 2, cols)
+    bias_up = small[:, :, 8:].reshape(shards, 1, -1)
     bias_heads = jnp.concatenate([bias_qv[:, :1], jnp.zeros_like(bias_qv[:, :1]), bias_qv[:, 1:]], 2)
+    full_out = flip_gather(w_out.T, high + low + along_x + core).reshape(shards, width, cols)
 
     first_image = lax.axis_index("tensor") * images
     kept_own = lax.dynamic_slice_in_dim(kept, first_image, images, 0)
@@ -708,70 +711,65 @@
     alive = (positions[None, :] < BUFFER + kept_own[:, None]).reshape(rows, 1)
     grad_m = jnp.where(alive, cotangent, jnp.zeros_like(cotangent))
 
-    core, along_x = [("dp", 1)], [("tensor", bit) for bit in bits_of("tensor")[::-1]]
-    low, high = [("dp", 2)], [("dp", bit) for bit in bits_of("dp")[::-1] if bit > 2]
-    order_x, order_low = core + along_x + low + high, core + low + along_x + high
     tables = [slot_table(order_x), slot_table(order_low)]
     second = lax.axis_index("dp").astype(jnp.int32) & 1
 
     h1 = norm_in(tokens, vectors)
-    qkv = project(h1, full_heads, bias_heads)
+    qkv = project(h1, full_qkv, bias_heads)
     attn, expo, inverse_sum = attend(qkv, kept_own)
-    mixed, h2 = mix(attn, full_heads, tokens, vectors)
+    mixed, h2 = mix(attn, full_out, tokens, vectors)
     act, slope = expand(h2, full_up, bias_up)
 
     hidden = act.shape[2]
-    grad_down = weight_grad(grad_m, act, hidden, hidden // 8, True)
+    grad_down = weight_grad(grad_m, act, hidden // 8)
     grad_m, grad_down = barrier((grad_m, grad_down))
     sent_down = scatter(grad_down)[:, :hidden]
     grad_pre, grad_bias_up = expand_back(grad_m, full_down, slope)
-
-    share = hidden // 2
-    ((near, far),) = weight_grad_split(h2, grad_pre, share, share, tables[:1], second)
+    ((near, far),), _ = weight_grad_split(h2, grad_pre, tables[:1], second)
     grad_pre, near, far = barrier((grad_pre, near, far))
     chain_up = Chain(near, far, order_x)
-    grad_first = weight_grad(h2, grad_pre, share, cols, False)
-    grad_pre, grad_first = barrier((grad_pre, grad_first))
-    grad_pre = meet(grad_pre, chain_up)
     grad_mixed, grad_o, grad_attn, sums2 = middle_back(
-        grad_pre, full_up, mixed, grad_m, vectors, full_heads
+        grad_pre, full_up, mixed, grad_m, vectors, full_out
     )
     grad_o = meet(grad_o, chain_up)
-    grad_first = weight_grad_into(grad_o, attn, grad_first)
-    grad_attn, grad_first = barrier((grad_attn, grad_first))
-    grad_heads, grad_bias_qv = attend_back(qkv, grad_attn, attn, expo, inverse_sum)
+    grad_out = weight_grad(grad_o, attn, cols // 2)
+    grad_attn, grad_out = barrier((grad_attn, grad_out))
+    grad_heads, totals = attend_back(qkv, grad_attn, attn, expo, inverse_sum)
     grad_heads = meet(grad_heads, chain_up)
-    grad_heads, sent_down, grad_first = barrier((grad_heads, sent_down, grad_first))
-    sent_first = scatter(grad_first)
+    grad_heads, sent_down, grad_out = barrier((grad_heads, sent_down, grad_out))
+    sent_out = scatter(grad_out)[:, :cols]
 
     chains = 2 if (3 * cols // 2) % LANES == 0 else 1
-    halves = weight_grad_split(h1, grad_heads, 0, 3 * cols // chains, tables[:chains], second)
-    grad_heads, halves = barrier((grad_heads, halves))
+    halves, (product, total) = weight_grad_split(
+        h1, grad_heads, tables[:chains], second, full_qkv, totals.reshape(shards, 1, 3 * cols)
+    )
+    grad_heads, halves, product, total = barrier((grad_heads, halves, product, total))
     chains_qkv = [Chain(*half, order) for half, order in zip(halves, (order_x, order_low))]
+    grad_heads = meet(grad_heads, chain_up)
+    total = jnp.sum(total, axis=-1)
+    product = (jnp.sum(product, axis=-1) - vectors[SHIFT1] * total) / vectors[GAIN1]
     sums = jnp.concatenate(
         [
-            sums2[:6],
-            grad_bias_qv.transpose(1, 0, 2).reshape(2, width),
+            jnp.stack([product, sums2[1], total, sums2[3], sums2[4], sums2[5]]),
+            totals[:, 0].reshape(1, width),
+            totals[:, 2].reshape(1, width),
             grad_bias_up.reshape(-1, width),
         ],
         0,
     )
-    grad_heads = meet(grad_heads, chain_up)
+    chain_small = Sum(sums, order_x)
     first = images // 2
-    grad_tokens, sums = input_back(
-        0, first, grad_heads, full_heads, tokens, grad_mixed, vectors, sums
-    )
-    sums = meet(sums, *chains_qkv)
-    grad_tokens, sums = input_back(
-        first, images - first, grad_heads, full_heads, tokens, grad_mixed, vectors, sums, grad_tokens
-    )
-    chain_small = Sum(sums, order_x)
-    act = meet(barrier((act, sums))[0], *chains_qkv)
+    grad_tokens = input_back(0, first, grad_heads, full_qkv, tokens, grad_mixed, vectors)
+    grad_tokens = meet(grad_tokens, chain_small, *chains_qkv)
+    grad_tokens = input_back(
+        first, images - first, grad_heads, full_qkv, tokens, grad_mixed, vectors, grad_tokens
+    )
+    act, grad_tokens = meet((act, grad_tokens), chain_up, chain_small, *chains_qkv)
     layer_out = shrink(0, first, kept_own, act, full_down, mixed, vectors)
-    layer_out = meet(layer_out, chain_small, *chains_qkv)
+    layer_out = meet(layer_out, chain_up, chain_small, *chains_qkv)
     layer_out = shrink(first, images - first, kept_own, act, full_down, mixed, vectors, layer_out)
     layer_out = meet(layer_out, chain_small, *chains_qkv)
-    sent_up = jnp.concatenate([sent_first[:, :share], chain_up.finish()], 1)
+    sent_up = chain_up.finish()
     sent_qkv = jnp.concatenate([chain.finish() for chain in chains_qkv], 1)
     small = chain_small.finish()
     at_dp, at_tensor = lax.axis_index("dp"), lax.axis_index("tensor")
@@ -786,7 +784,7 @@
         layer_out,
         grad_tokens,
         sent_qkv.astype(f32).reshape(part, 3, cols).transpose(1, 0, 2),
-        sent_first[:, share:].astype(f32).T,
+        sent_out.astype(f32).T,
         sent_up.astype(f32),
         sent_down.astype(f32).T,
         heads_own,

time: 574 us -> 583 us (1.016)
  waiting for transfers between devices: 87.9 us -> 56.2 us
  local copies, waits for them, and re-layouts: 9.26 us -> 28.6 us
  other arithmetic: 19.7 us -> 31.7 us
  starting transfers between devices: 26.2 us -> 35.3 us
    all_gather x3, waiting for transfers between devices: 50 us -> 21.8 us  [gather(): full = lax.all_gather(part, ('tensor', 'dp'), axis=0, tiled=True)]
    add x17, other arithmetic: 2.44 us -> 12.2 us  [settle(): self.values = self.near + self.far]
    ppermute x25 -> x30, starting transfers between devices: 26 us -> 35.1 us  [swap(): lax.ppermute(values, axis, [(place, place ^ bit) for place in places])]
    unnamed x18 -> x26, local copies, waits for them, and re-layouts: 1.13 us -> 9.71 us
    ppermute x25 -> x30, waiting for transfers between devices: 36.5 us -> 32.9 us  [swap(): lax.ppermute(values, axis, [(place, place ^ bit) for place in places])]
    pallas_call x5 -> x4, Pallas kernels: 101 us -> 102 us  [the longest x2 61.7 us: weight_grad_split(): call(functools.partial(weight_grad_split_kernel, per_chain=per_chain, cha...]
  transfers between devices with their start and end apart: 30 -> 35, of which waited for: 14 -> 13; matrix products, arithmetic and copies ran while one was open for 4% -> 9% of each run, Pallas kernels for 72% -> 71%
where the time goes in v4:
time: 583 us; the launch traced here: 573 us
  Pallas kernels  406 us (70%)
  waiting for transfers between devices  56.2 us (10%)
  starting transfers between devices  35.3 us (6%)
  other arithmetic  31.7 us (5%)
  local copies, waits for them, and re-layouts  28.6 us (5%)
  between operations  14.5 us (2%)
    pallas_call x2, Pallas kernels, weight_grad_split(): call(functools.partial(weight_grad_split_kernel, per_chain=per_chain, cha...  61.7 us
    pallas_call x1, Pallas kernels, expand(): call(expand_kernel, 'expand', (shards, rows // size), [pl.BlockSpec((size...  45.9 us
    pallas_call x1, Pallas kernels, attend_back(): pl.pallas_call(functools.partial(attend_back_kernel, pairs=pairs), grid=(...  41.3 us
    pallas_call x2, Pallas kernels, weight_grad(): call(functools.partial(weight_grad_kernel, chunk=chunk, fill=spare), 'wei...  40.5 us
    pallas_call x1, Pallas kernels, middle_back(): call(middle_back_kernel, 'middle_back', (rows // SEQ,), [pl.BlockSpec((sh...  39.8 us
    pallas_call x2, Pallas kernels, shrink(): call(functools.partial(shrink_kernel, first=first), 'shrink', (count,), [...  35.8 us
    ppermute x30, starting transfers between devices, swap(): lax.ppermute(values, axis, [(place, place ^ bit) for place in places])  35.1 us
    pallas_call x1, Pallas kernels, expand_back(): call(expand_back_kernel, 'expand_back', (shards, rows // size), [pl.Block...  33.3 us
  transfers between devices with their start and end apart: 35, of which 13 were waited for; matrix products, arithmetic and copies ran while one was open for 9% of the time, Pallas kernels for 71%

profile of v4, /device:TPU:0, one launch (start us, length us, event | category | flops | bytes accessed | tf_op | source)
XLA Modules:
  0.0 572.6 jit_solution(2711208931633752566)
XLA Ops:
  7.2 1.6 copy.42
  12.5 4.1 collective-permute-start
  16.7 1.2 broadcast_add_fusion
  18.8 1.5 constant_dynamic-update-slice_fusion.15
  20.3 6.5 %broadcast_select_fusion.left_ref.g_ref.gm_ref = bf16[2560,1024]{1,0:T(8,128)(2,1)} fusion(bf16[2560,1024]{1,0:T(8,128)(2,1)} %param.13, pred[2560]{0:T(1024)(128)(4,1)S(1)} %lt.89), kind=kLoop, calls=%fused_computation.2 | loop fusion | flops 2621440 | bytes 10488320 | tf_op jit(solution)/shard_map/jit(_where)/select_n | solution.py:712
  26.9 1.9 collective-permute-start.1
  28.8 2.3 collective-permute-done.1
  31.0 1.7 collective-permute-start.2
  32.8 1.4 collective-permute-start.6
  35.0 1.8 collective-permute-start.3
  36.7 1.1 collective-permute-done.6
  39.7 1.0 collective-permute-done.4
  41.3 5.8 %collective-permute-done.7 = bf16[4,64,512]{2,1,0:T(8,128)(2,1)S(1)} collective-permute-done((bf16[4,64,512]{2,1,0:T(8,128)(2,1)S(1)}, bf16[4,64,512]{2,1,0:T(8,128)(2,1)S(1)}, u32[]{:S(2)}, u32[]{:S(2)}) %collective-permute-start.7) | collective-permute-done | bytes 262176 | tf_op jit(solution)/shard_map/ppermute | solution.py:589
  47.2 1.9 collective-permute-start.8
  51.4 7.7 %collective-permute-done.8 = bf16[8,64,512]{2,1,0:T(8,128)(2,1)S(1)} collective-permute-done((bf16[8,64,512]{2,1,0:T(8,128)(2,1)S(1)}, bf16[8,64,512]{2,1,0:T(8,128)(2,1)S(1)}, u32[]{:S(2)}, u32[]{:S(2)}) %collective-permute-start.8) | collective-permute-done | bytes 524320 | tf_op jit(solution)/shard_map/ppermute | solution.py:589
  59.1 0.9 constant_dynamic-update-slice_fusion.11
  61.6 8.5 %norm_in.1.h_ref.left_ref = bf16[2560,1024]{1,0:T(8,128)(2,1)} custom-call(bf16[2560,1024]{1,0:T(8,128)(2,1)} %x_ref.7, f32[8,1024]{1,0:T(8,128)} %concatenate.66.vec_ref), custom_call_target="tpu_custom_call" | custom-call | flops 41943040 | bytes 10485760 | tf_op jit(solution)/shard_map/norm_in/pallas_call | solution.py:218
  70.8 1.1 constant_dynamic-update-slice_fusion.16
  71.9 2.3 gather_fusion.1
  74.2 1.5 bitcast_select_fusion.w_ref.out_w_ref
  75.7 9.1 %all-gather.4.cloned.1.call-done = bf16[2048,1536]{1,0:T(8,128)(2,1)} async-done(((bf16[64,1536]{1,0:T(8,128)(2,1)}), bf16[2048,1536]{1,0:T(8,128)(2,1)}) %all-gather.4.cloned.1.call-update) | async-done | bytes 6291472 | tf_op jit(solution)/shard_map/all_gather | solution.py:670
  84.8 22.0 %project.1.q_ref.k_ref.v_ref = bf16[2,2560,1536]{2,1,0:T(8,128)(2,1)} custom-call(bf16[2560,1024]{1,0:T(8,128)(2,1)} %norm_in.1.h_ref.left_ref, bf16[2,1024,1536]{2,1,0:T(8,128)(2,1)} %bitcast.56, f32[2,1,1536]{2,1,0:T(1,128)} %pad_maximum_fusion.6.bias_ref), custom_call_target="tpu_custom_call" | custom-call | flops 16106127360 | bytes 11534336 | tf_op jit(solution)/shard_map/project/pallas_call | solution.py:237
  106.8 32.5 %attend.1 = (bf16[2,2560,512]{2,1,0:T(8,128)(2,1)}, bf16[2,8,4,2,320,384]{5,4,3,2,1,0:T(8,128)(2,1)}, f32[2,2560,512]{2,1,0:T(8,128)}) custom-call(s32[8]{0:T(128)} %get-tuple-element.161.kept_ref, bf16[2,2560,1536]{2,1,0:T(8,128)(2,1)} %project.1.q_ref.k_ref.v_ref, bf16[2,2560,1536]{2,1,0:T(8,128)(2,1)} %project.1.q_ref.k_ref.v_ref, ...), custom_call_target="tpu_custom_call" | custom-call | flops 13421772800 | bytes 31457280 | tf_op jit(solution)/shard_map/attend/pallas_call | solution.py:74
  139.4 13.5 %mix.1 = (f32[2560,1024]{1,0:T(8,128)}, bf16[2560,1024]{1,0:T(8,128)(2,1)}) custom-call(bf16[2,2560,512]{2,1,0:T(8,128)(2,1)} %get-tuple-element.75.attn_ref.right_ref.o_ref, bf16[2,1024,512]{2,1,0:T(8,128)(2,1)} %bitcast_select_fusion.w_ref.out_w_ref, bf16[2560,1024]{1,0:T(8,128)(2,1)} %x_ref.7, f32[8,1024]{1,0:T(8,128)} %concatenate.66.vec_ref), custom_call_target="tpu_custom_call" | custom-call | flops 5368709120 | bytes 10485760 | tf_op jit(solution)/shard_map/mix/pallas_call | solution.py:266
  152.9 10.5 %all-gather.6.cloned.1.call-done = bf16[2048,2048]{1,0:T(8,128)(2,1)} async-done(((bf16[64,2048]{1,0:T(8,128)(2,1)}), bf16[2048,2048]{1,0:T(8,128)(2,1)}) %all-gather.6.cloned.1.call-update) | async-done | bytes 8388624 | tf_op jit(solution)/shard_map/all_gather | solution.py:670
  163.4 45.9 %expand.1 = (bf16[2,2560,2048]{2,1,0:T(8,128)(2,1)}, bf16[2,2560,2048]{2,1,0:T(8,128)(2,1)}) custom-call(bf16[2560,1024]{1,0:T(8,128)(2,1)} %get-tuple-element.76.h_ref.left_ref, bf16[2,1024,2048]{2,1,0:T(8,128)(2,1)} %bitcast.77, f32[2,1,2048]{2,1,0:T(1,128)} %reshape.265.bias_ref), custom_call_target="tpu_custom_call" | custom-call | flops 32212254720 | bytes 13631488 | tf_op jit(solution)/shard_map/expand/pallas_call | solution.py:313
  209.2 29.8 %weight_grad.2 = bf16[2,1024,2304]{2,1,0:T(8,128)(2,1)} custom-call(bf16[2560,1024]{1,0:T(8,128)(2,1)} %broadcast_select_fusion.left_ref.g_ref.gm_ref, bf16[2,2560,2048]{2,1,0:T(8,128)(2,1)} %get-tuple-element.123.right_ref.act_ref), custom_call_target="tpu_custom_call" | custom-call | flops 21474836480 | bytes 26214400 | tf_op jit(solution)/shard_map/weight_grad/pallas_call | solution.py:384
  239.8 2.2 all-gather.8.cloned.1.call-done
  242.0 33.3 %expand_back.1 = (bf16[2,2560,2048]{2,1,0:T(8,128)(2,1)}, f32[2,1,2048]{2,1,0:T(1,128)}) custom-call(bf16[2560,1024]{1,0:T(8,128)(2,1)} %broadcast_select_fusion.left_ref.g_ref.gm_ref, bf16[2,1024,2048]{2,1,0:T(8,128)(2,1)} %bitcast.53, bf16[2,2560,2048]{2,1,0:T(8,128)(2,1)} %get-tuple-element.79.slope_ref), custom_call_target="tpu_custom_call" | custom-call | flops 21474836480 | bytes 41943040 | tf_op jit(solution)/shard_map/expand_back/pallas_call | solution.py:346
  275.3 29.9 %weight_grad_split.2 = (bf16[16,64,2048]{2,1,0:T(8,128)(2,1)}, bf16[16,64,2048]{2,1,0:T(8,128)(2,1)}) custom-call(s32[17]{0:T(128)} %pad_add_fusion.slot_ref, bf16[2560,1024]{1,0:T(8,128)(2,1)} %get-tuple-element.76.h_ref.left_ref, bf16[2,2560,2048]{2,1,0:T(8,128)(2,1)} %get-tuple-element.83.right_ref.g_ref), custom_call_target="tpu_custom_call" | custom-call | flops 21474836480 | bytes 26214400 | tf_op jit(solution)/shard_map/weight_grad_split/pallas_call | solution.py:456
  306.2 39.8 %middle_back.1 = (f32[2560,1024]{1,0:T(8,128)}, bf16[2560,1024]{1,0:T(8,128)(2,1)}, bf16[2,2560,512]{2,1,0:T(8,128)(2,1)}, f32[8,1024]{1,0:T(8,128)}) custom-call(bf16[2,2560,2048]{2,1,0:T(8,128)(2,1)} %get-tuple-element.83.right_ref.g_ref, bf16[2,1024,2048]{2,1,0:T(8,128)(2,1)} %bitcast.78, f32[2560,1024]{1,0:T(8,128)} %get-tuple-element.84.mixed_ref, ...), custom_call_target="tpu_custom_call" | custom-call | flops 26843545600 | bytes 39845888 | tf_op jit(solution)/shard_map/middle_back/pallas_call | solution.py:500
  347.6 5.4 add.273
  353.1 1.7 slice.170
  354.8 1.0 copy-done
  355.8 1.5 collective-permute-start.11
  357.3 10.7 %weight_grad.3 = bf16[2,1024,768]{2,1,0:T(8,128)(2,1)} custom-call(bf16[2560,1024]{1,0:T(8,128)(2,1)} %get-tuple-element.88.left_ref, bf16[2,2560,512]{2,1,0:T(8,128)(2,1)} %get-tuple-element.75.attn_ref.right_ref.o_ref), custom_call_target="tpu_custom_call" | custom-call | flops 5368709120 | bytes 10485760 | tf_op jit(solution)/shard_map/weight_grad/pallas_call | solution.py:384
  368.0 41.3 %attend_back.1 = (bf16[2,2560,1536]{2,1,0:T(8,128)(2,1)}, f32[2,3,512]{2,1,0:T(4,128)}) custom-call(bf16[2,2560,1536]{2,1,0:T(8,128)(2,1)} %project.1.q_ref.k_ref.v_ref, bf16[2,2560,1536]{2,1,0:T(8,128)(2,1)} %project.1.q_ref.k_ref.v_ref, bf16[2,2560,1536]{2,1,0:T(8,128)(2,1)} %project.1.q_ref.k_ref.v_ref, bf16[2,2560,512]{2,1,0:T(8,128)(2,1)} %get-tuple-element.89.g_ref, ...), custom_call_target="tpu_custom_call" | custom-call | flops 20132659200 | bytes 62914560 | tf_op jit(solution)/shard_map/attend_back/pallas_call | solution.py:138
  409.3 1.3 reshape.292.refs_1_
  410.6 1.3 copy-done.1
  411.9 2.4 slice_add_fusion
  414.4 1.0 slice.173
  416.1 31.8 %weight_grad_split.3 = (bf16[16,64,768]{2,1,0:T(8,128)(2,1)}, bf16[16,64,768]{2,1,0:T(8,128)(2,1)}, bf16[16,64,768]{2,1,0:T(8,128)(2,1)}, bf16[16,64,768]{2,1,0:...) custom-call(s32[33]{0:T(128)} %pad_add_fusion.1.slot_ref, bf16[2560,1024]{1,0:T(8,128)(2,1)} %norm_in.1.h_ref.left_ref, ...), custom_call_target="tpu_custom_call" | custom-call | flops 16106127360 | bytes 20971520 | tf_op jit(solution)/shard_map/weight_grad_split/pallas_call | solution.py:456
  448.6 1.2 reduce_sum.22
  449.8 1.2 reduce_sum.24
  451.3 15.8 %input_back.2.refs_0_ = f32[2560,1024]{1,0:T(8,128)} custom-call(bf16[2,2560,1536]{2,1,0:T(8,128)(2,1)} %get-tuple-element.108.right_ref.g_ref, bf16[2,1024,1536]{2,1,0:T(8,128)(2,1)} %bitcast.58, bf16[2560,1024]{1,0:T(8,128)(2,1)} %x_ref.7, f32[2560,1024]{1,0:T(8,128)} %get-tuple-element.109.gmixed_ref, f32[8,1024]{1,0:T(8,128)} %concatenate.66.vec_ref), custom_call_target="tpu_custom_call" | custom-call | flops 8053063680 | bytes 6291456 | tf_op jit(solution)/shard_map/input_back/pallas_call | solution.py:536
  467.3 1.3 copy-done.3
  468.6 1.9 add.280
  470.6 2.0 add.281
  472.6 1.4 collective-permute-start.19
  476.3 2.0 collective-permute-start.16
  478.4 1.5 collective-permute-start.17
  479.9 15.6 %input_back.3 = f32[2560,1024]{1,0:T(8,128)} custom-call(bf16[2,2560,1536]{2,1,0:T(8,128)(2,1)} %get-tuple-element.108.right_ref.g_ref, bf16[2,1024,1536]{2,1,0:T(8,128)(2,1)} %bitcast.59, bf16[2560,1024]{1,0:T(8,128)(2,1)} %x_ref.7, f32[2560,1024]{1,0:T(8,128)} %get-tuple-element.109.gmixed_ref, ...), custom_call_target="tpu_custom_call", output_to_operand_aliasing={{}: (5, {})} | custom-call | flops 8053063680 | bytes 6291456 | tf_op jit(solution)/shard_map/input_back/pallas_call | solution.py:536
  495.5 11.6 %collective-permute-done.16 = bf16[2,64,2048]{2,1,0:T(8,128)(2,1)S(1)} collective-permute-done((bf16[2,64,2048]{2,1,0:T(8,128)(2,1)}, bf16[2,64,2048]{2,1,0:T(8,128)(2,1)S(1)}, u32[]{:S(2)}, u32[]{:S(2)}) %collective-permute-start.16) | collective-permute-done | bytes 524320 | tf_op jit(solution)/shard_map/ppermute | solution.py:589
  508.1 0.9 copy-done.6
  509.0 2.0 collective-permute-start.21
  511.5 1.1 collective-permute-start.22
  512.6 18.0 %shrink.2.refs_0_ = bf16[2560,1024]{1,0:T(8,128)(2,1)} custom-call(s32[8]{0:T(128)} %get-tuple-element.161.kept_ref, bf16[2,2560,2048]{2,1,0:T(8,128)(2,1)} %get-tuple-element.123.right_ref.act_ref, bf16[2,1024,2048]{2,1,0:T(8,128)(2,1)} %bitcast.54, f32[2560,1024]{1,0:T(8,128)} %get-tuple-element.84.mixed_ref, f32[8,1024]{1,0:T(8,128)} %concatenate.66.vec_ref), custom_call_target="tpu_custom_call" | custom-call | flops 10737418240 | bytes 8388608 | tf_op jit(solution)/shard_map/shrink/pallas_call | solution.py:569
  530.6 3.8 collective-permute-start.24
  534.7 2.9 collective-permute-start.25
  537.6 17.9 %shrink.3 = bf16[2560,1024]{1,0:T(8,128)(2,1)} custom-call(s32[8]{0:T(128)} %get-tuple-element.161.kept_ref, bf16[2,2560,2048]{2,1,0:T(8,128)(2,1)} %get-tuple-element.123.right_ref.act_ref, bf16[2,1024,2048]{2,1,0:T(8,128)(2,1)} %bitcast.55, f32[2560,1024]{1,0:T(8,128)} %get-tuple-element.84.mixed_ref, ...), custom_call_target="tpu_custom_call", output_to_operand_aliasing={{}: (5, {})} | custom-call | flops 10737418240 | bytes 8388608 | tf_op jit(solution)/shard_map/shrink/pallas_call | solution.py:569
  556.5 2.1 collective-permute-start.28
  558.7 2.0 collective-permute-done.29
  563.5 0.9 copy.41
  564.4 1.5 convert_bitcast_fusion.1
  (155 shorter events, 25.5 us)
Async XLA Ops:
  7.2 77.7 %all-gather.4.cloned.1.call-start = ((), (), s32[]{:S(2)}) async-start(), calls=%async_computation.2 | async-start | bytes 6488064 | tf_op jit(solution)/shard_map/all_gather | solution.py:670
  8.9 154.5 %all-gather.6.cloned.1.call-start = ((), (), s32[]{:S(2)}) async-start(), calls=%async_computation.3 | async-start | bytes 8650752 | tf_op jit(solution)/shard_map/all_gather | solution.py:670
  9.6 232.4 %all-gather.8.cloned.1.call-start = ((), (), s32[]{:S(2)}) async-start(), calls=%async_computation.4 | async-start | bytes 8650752 | tf_op jit(solution)/shard_map/all_gather | solution.py:670
  10.4 405.8 %reduce-scatter.3.cloned.1.call-start = ((), (), s32[]{:S(2)}) async-start(), calls=%async_computation.5 | async-start | bytes 9732096 | tf_op jit(solution)/shard_map/reduce_scatter | solution.py:676
  12.5 14.3 %collective-permute-start = (f32[1,12,32]{2,1,0:T(8,128)S(1)}, f32[1,12,32]{2,1,0:T(8,128)S(1)}, u32[]{:S(2)}, u32[]{:S(2)}) collective-permute-start(f32[1,12,32]{2,1,0:T(8,128)S(1)} %maximum_bitcast_fusion), channel_id=1, source_target_pairs={{0,16},{2,18},{4,20},{6,22},{8,24},{10,26},{12,28},{14,30},{16,0},... | collective-permute-start | bytes 4616 | tf_op jit(solution)/shard_map/ppermute | solution.py:589
  16.6 16.1 %collective-permute-start.5 = (bf16[1,64,512]{2,1,0:T(8,128)(2,1)}, bf16[1,64,512]{2,1,0:T(8,128)(2,1)S(1)}, u32[]{:S(2)}, u32[]{:S(2)}) collective-permute-start(bf16[1,64,512]{2,1,0:T(8,128)(2,1)} %bitcast.65), channel_id=1, source_target_pairs={{0,16},{2,18},{4,20},{6,22},{8,24},{10,26},{12,28},{14,30},{16,0},... | collective-permute-start | bytes 196616 | tf_op jit(solution)/shard_map/ppermute | solution.py:589
  20.3 12.5 %copy-start.4 = (bf16[512,64]{0,1:T(8,128)(2,1)S(1)}, bf16[512,64]{0,1:T(8,128)(2,1)}, u32[]{:S(2)}) copy-start(bf16[512,64]{0,1:T(8,128)(2,1)} %param.15) | copy-start | bytes 196612
  26.9 4.2 collective-permute-start.1
  31.0 3.9 collective-permute-start.2
  32.8 5.0 collective-permute-start.6
  35.0 4.3 collective-permute-start.3
  37.8 9.2 %collective-permute-start.7 = (bf16[4,64,512]{2,1,0:T(8,128)(2,1)S(1)}, bf16[4,64,512]{2,1,0:T(8,128)(2,1)S(1)}, u32[]{:S(2)}, u32[]{:S(2)}) collective-permute-start(bf16[4,64,512]{2,1,0:T(8,128)(2,1)S(1)} %pad_maximum_fusion.1), channel_id=1, source_target_pairs={{0,4},{2,6},{4,0},{6,2},{8,12},{10,14},{12,8},{14,10},{16,20},{18,... | collective-permute-start | bytes 786440 | tf_op jit(solution)/shard_map/ppermute | solution.py:589
  39.3 1.4 collective-permute-start.4
  47.2 12.0 %collective-permute-start.8 = (bf16[8,64,512]{2,1,0:T(8,128)(2,1)S(1)}, bf16[8,64,512]{2,1,0:T(8,128)(2,1)S(1)}, u32[]{:S(2)}, u32[]{:S(2)}) collective-permute-start(bf16[8,64,512]{2,1,0:T(8,128)(2,1)S(1)} %pad_maximum_fusion), channel_id=1, source_target_pairs={{0,1},{1,0},{2,3},{3,2},{4,5},{5,4},{6,7},{7,6},{8,9},{9,8},{10,11... | collective-permute-start | bytes 1572872 | tf_op jit(solution)/shard_map/ppermute | solution.py:589
  60.0 10.8 %collective-permute-start.9 = (bf16[16,64,512]{2,1,0:T(8,128)(2,1)S(1)}, bf16[16,64,512]{2,1,0:T(8,128)(2,1)S(1)}, u32[]{:S(2)}, u32[]{:S(2)}) collective-permute-start(bf16[16,64,512]{2,1,0:T(8,128)(2,1)S(1)} %get-tuple-element.162), channel_id=1, source_target_pairs={{0,2},{2,0},{4,6},{6,4},{8,10},{10,8},{12,14},{14,12},{16,18},{18,... | collective-permute-start | bytes 3145736 | tf_op jit(solution)/shard_map/ppermute | solution.py:589
  239.1 325.3 %reduce-scatter.5.cloned.1.call-start = ((), (), s32[]{:S(2)}) async-start(), calls=%async_computation.6 | async-start | bytes 3244032 | tf_op jit(solution)/shard_map/reduce_scatter | solution.py:676
  305.1 42.5 %collective-permute-start.10 = (bf16[16,64,2048]{2,1,0:T(8,128)(2,1)}, bf16[16,64,2048]{2,1,0:T(8,128)(2,1)}, u32[]{:S(2)}, u32[]{:S(2)}) collective-permute-start(bf16[16,64,2048]{2,1,0:T(8,128)(2,1)} %get-tuple-element.87), channel_id=1, source_target_pairs={{0,2},{2,0},{4,6},{6,4},{8,10},{10,8},{12,14},{14,12},{16,18},{18,... | collective-permute-start | bytes 12582920 | tf_op jit(solution)/shard_map/ppermute | solution.py:589
  306.2 41.4 %copy-start.8 = (f32[2,1,2048]{2,1,0:T(1,128)S(1)}, f32[2,1,2048]{2,1,0:T(1,128)}, u32[]{:S(2)}) copy-start(f32[2,1,2048]{2,1,0:T(1,128)} %get-tuple-element.113) | copy-start | bytes 49156
  353.1 2.7 copy-start
  355.8 54.8 %collective-permute-start.11 = (bf16[8,64,2048]{2,1,0:T(8,128)(2,1)}, bf16[8,64,2048]{2,1,0:T(8,128)(2,1)S(1)}, u32[]{:S(2)}, u32[]{:S(2)}) collective-permute-start(bf16[8,64,2048]{2,1,0:T(8,128)(2,1)} %slice.170), channel_id=1, source_target_pairs={{0,1},{1,0},{2,3},{3,2},{4,5},{5,4},{6,7},{7,6},{8,9},{9,8},{10,11... | collective-permute-start | bytes 6291464 | tf_op jit(solution)/shard_map/ppermute | solution.py:589
  410.6 1.3 copy-start.1
  415.4 33.1 %collective-permute-start.12 = (bf16[4,64,2048]{2,1,0:T(8,128)(2,1)}, bf16[4,64,2048]{2,1,0:T(8,128)(2,1)S(1)}, u32[]{:S(2)}, u32[]{:S(2)}) collective-permute-start(bf16[4,64,2048]{2,1,0:T(8,128)(2,1)} %slice.173), channel_id=1, source_target_pairs={{0,4},{2,6},{4,0},{6,2},{8,12},{10,14},{12,8},{14,10},{16,20},{18,... | collective-permute-start | bytes 3145736 | tf_op jit(solution)/shard_map/ppermute | solution.py:589
  416.1 32.4 %copy-start.7 = (f32[2,3,512]{2,1,0:T(4,128)S(1)}, f32[2,3,512]{2,1,0:T(4,128)}, u32[]{:S(2)}) copy-start(f32[2,3,512]{2,1,0:T(4,128)} %get-tuple-element.99) | copy-start | bytes 36868
  447.9 19.3 %collective-permute-start.14 = (bf16[16,64,768]{2,1,0:T(8,128)(2,1)}, bf16[16,64,768]{2,1,0:T(8,128)(2,1)}, u32[]{:S(2)}, u32[]{:S(2)}) collective-permute-start(bf16[16,64,768]{2,1,0:T(8,128)(2,1)} %get-tuple-element.114), channel_id=1, source_target_pairs={{0,2},{2,0},{4,6},{6,4},{8,10},{10,8},{12,14},{14,12},{16,18},{18,... | collective-permute-start | bytes 4718600 | tf_op jit(solution)/shard_map/ppermute | solution.py:589
  448.0 19.3 %collective-permute-start.15 = (bf16[16,64,768]{2,1,0:T(8,128)(2,1)}, bf16[16,64,768]{2,1,0:T(8,128)(2,1)}, u32[]{:S(2)}, u32[]{:S(2)}) collective-permute-start(bf16[16,64,768]{2,1,0:T(8,128)(2,1)} %get-tuple-element.115), channel_id=1, source_target_pairs={{0,2},{2,0},{4,6},{6,4},{8,10},{10,8},{12,14},{14,12},{16,18},{18,... | collective-permute-start | bytes 4718600 | tf_op jit(solution)/shard_map/ppermute | solution.py:589
  451.2 16.1 %collective-permute-start.13 = (f32[12,1024]{1,0:T(8,128)S(1)}, f32[12,1024]{1,0:T(8,128)S(1)}, u32[]{:S(2)}, u32[]{:S(2)}) collective-permute-start(f32[12,1024]{1,0:T(8,128)S(1)} %concatenate.75), channel_id=1, source_target_pairs={{0,2},{2,0},{4,6},{6,4},{8,10},{10,8},{12,14},{14,12},{16,18},{18,... | collective-permute-start | bytes 147464 | tf_op jit(solution)/shard_map/ppermute | solution.py:589
  467.2 1.4 copy-start.3
  467.3 3.3 copy-start.2
  470.6 4.1 slice-start
  472.6 34.5 %collective-permute-start.19 = (bf16[8,64,768]{2,1,0:T(8,128)(2,1)S(1)}, bf16[8,64,768]{2,1,0:T(8,128)(2,1)S(1)}, u32[]{:S(2)}, u32[]{:S(2)}) collective-permute-start(bf16[8,64,768]{2,1,0:T(8,128)(2,1)S(1)} %slice.179), channel_id=1, source_target_pairs={{0,4},{2,6},{4,0},{6,2},{8,12},{10,14},{12,8},{14,10},{16,20},{18,... | collective-permute-start | bytes 2359304 | tf_op jit(solution)/shard_map/ppermute | solution.py:589
  474.0 33.9 %collective-permute-start.18 = (bf16[8,64,768]{2,1,0:T(8,128)(2,1)S(1)}, bf16[8,64,768]{2,1,0:T(8,128)(2,1)S(1)}, u32[]{:S(2)}, u32[]{:S(2)}) collective-permute-start(bf16[8,64,768]{2,1,0:T(8,128)(2,1)S(1)} %slice.178), channel_id=1, source_target_pairs={{0,1},{1,0},{2,3},{3,2},{4,5},{5,4},{6,7},{7,6},{8,9},{9,8},{10,11... | collective-permute-start | bytes 2359304 | tf_op jit(solution)/shard_map/ppermute | solution.py:589
  476.3 30.8 %collective-permute-start.16 = (bf16[2,64,2048]{2,1,0:T(8,128)(2,1)}, bf16[2,64,2048]{2,1,0:T(8,128)(2,1)S(1)}, u32[]{:S(2)}, u32[]{:S(2)}) collective-permute-start(bf16[2,64,2048]{2,1,0:T(8,128)(2,1)} %slice.177), channel_id=1, source_target_pairs={{0,16},{2,18},{4,20},{6,22},{8,24},{10,26},{12,28},{14,30},{16,0},... | collective-permute-start | bytes 1572872 | tf_op jit(solution)/shard_map/ppermute | solution.py:589
  478.4 28.7 %collective-permute-start.17 = (f32[12,1024]{1,0:T(8,128)S(1)}, f32[12,1024]{1,0:T(8,128)S(1)}, u32[]{:S(2)}, u32[]{:S(2)}) collective-permute-start(f32[12,1024]{1,0:T(8,128)S(1)} %add.279), channel_id=1, source_target_pairs={{0,1},{1,0},{2,3},{3,2},{4,5},{5,4},{6,7},{7,6},{8,9},{9,8},{10,11... | collective-permute-start | bytes 147464 | tf_op jit(solution)/shard_map/ppermute | solution.py:589
  507.1 0.8 copy-start.5
  507.9 1.1 copy-start.6
  509.0 21.6 %collective-permute-start.21 = (f32[12,1024]{1,0:T(8,128)S(1)}, f32[12,1024]{1,0:T(8,128)S(1)}, u32[]{:S(2)}, u32[]{:S(2)}) collective-permute-start(f32[12,1024]{1,0:T(8,128)S(1)} %add.283), channel_id=1, source_target_pairs={{0,4},{2,6},{4,0},{6,2},{8,12},{10,14},{12,8},{14,10},{16,20},{18,... | collective-permute-start | bytes 147464 | tf_op jit(solution)/shard_map/ppermute | solution.py:589
  511.0 19.6 %collective-permute-start.20 = (bf16[1,64,2048]{2,1,0:T(8,128)(2,1)S(1)}, bf16[1,64,2048]{2,1,0:T(8,128)(2,1)S(1)}, u32[]{:S(2)}, u32[]{:S(2)}) collective-permute-start(bf16[1,64,2048]{2,1,0:T(8,128)(2,1)S(1)} %slice.181), channel_id=1, source_target_pairs={{0,8},{2,10},{4,12},{6,14},{8,0},{10,2},{12,4},{14,6},{16,24},{18,... | collective-permute-start | bytes 786440 | tf_op jit(solution)/shard_map/ppermute | solution.py:589
  511.2 19.4 %collective-permute-start.23 = (bf16[4,64,768]{2,1,0:T(8,128)(2,1)S(1)}, bf16[4,64,768]{2,1,0:T(8,128)(2,1)S(1)}, u32[]{:S(2)}, u32[]{:S(2)}) collective-permute-start(bf16[4,64,768]{2,1,0:T(8,128)(2,1)S(1)} %slice.185), channel_id=1, source_target_pairs={{0,1},{1,0},{2,3},{3,2},{4,5},{5,4},{6,7},{7,6},{8,9},{9,8},{10,11... | collective-permute-start | bytes 1179656 | tf_op jit(solution)/shard_map/ppermute | solution.py:589
  511.5 19.1 %collective-permute-start.22 = (bf16[4,64,768]{2,1,0:T(8,128)(2,1)S(1)}, bf16[4,64,768]{2,1,0:T(8,128)(2,1)S(1)}, u32[]{:S(2)}, u32[]{:S(2)}) collective-permute-start(bf16[4,64,768]{2,1,0:T(8,128)(2,1)S(1)} %slice.183), channel_id=1, source_target_pairs={{0,4},{2,6},{4,0},{6,2},{8,12},{10,14},{12,8},{14,10},{16,20},{18,... | collective-permute-start | bytes 1179656 | tf_op jit(solution)/shard_map/ppermute | solution.py:589
  530.6 25.7 %collective-permute-start.24 = (f32[12,1024]{1,0:T(8,128)S(1)}, f32[12,1024]{1,0:T(8,128)S(1)}, u32[]{:S(2)}, u32[]{:S(2)}) collective-permute-start(f32[12,1024]{1,0:T(8,128)S(1)} %add.286), channel_id=1, source_target_pairs={{0,16},{2,18},{4,20},{6,22},{8,24},{10,26},{12,28},{14,30},{16,0},... | collective-permute-start | bytes 147464 | tf_op jit(solution)/shard_map/ppermute | solution.py:589
  534.6 21.7 %collective-permute-start.26 = (bf16[2,64,768]{2,1,0:T(8,128)(2,1)S(1)}, bf16[2,64,768]{2,1,0:T(8,128)(2,1)S(1)}, u32[]{:S(2)}, u32[]{:S(2)}) collective-permute-start(bf16[2,64,768]{2,1,0:T(8,128)(2,1)S(1)} %slice.189), channel_id=1, source_target_pairs={{0,16},{2,18},{4,20},{6,22},{8,24},{10,26},{12,28},{14,30},{16,0},... | collective-permute-start | bytes 589832 | tf_op jit(solution)/shard_map/ppermute | solution.py:589
  534.7 21.6 %collective-permute-start.25 = (bf16[2,64,768]{2,1,0:T(8,128)(2,1)S(1)}, bf16[2,64,768]{2,1,0:T(8,128)(2,1)S(1)}, u32[]{:S(2)}, u32[]{:S(2)}) collective-permute-start(bf16[2,64,768]{2,1,0:T(8,128)(2,1)S(1)} %slice.187), channel_id=1, source_target_pairs={{0,16},{2,18},{4,20},{6,22},{8,24},{10,26},{12,28},{14,30},{16,0},... | collective-permute-start | bytes 589832 | tf_op jit(solution)/shard_map/ppermute | solution.py:589
  556.3 4.3 collective-permute-start.29
  556.5 6.6 %collective-permute-start.28 = (bf16[1,64,768]{2,1,0:T(8,128)(2,1)S(1)}, bf16[1,64,768]{2,1,0:T(8,128)(2,1)S(1)}, u32[]{:S(2)}, u32[]{:S(2)}) collective-permute-start(bf16[1,64,768]{2,1,0:T(8,128)(2,1)S(1)} %slice.195), channel_id=1, source_target_pairs={{0,8},{2,10},{4,12},{6,14},{8,0},{10,2},{12,4},{14,6},{16,24},{18,... | collective-permute-start | bytes 294920 | tf_op jit(solution)/shard_map/ppermute | solution.py:589
  558.6 4.6 collective-permute-start.27
Sparse Core Ops, SparseCore 0:
  11.4 73.3 all-gather.3
  87.7 75.5 all-gather.5
  166.2 75.6 all-gather.7
  247.7 135.9 reduce-scatter.2
  448.7 103.6 reduce-scatter.4
